TPU v7x, 32 devices: a whole 2x2x4 slice. The times are simulated.
32 devices in a mesh: col: 8 (over z, y), row: 4 (over x, core).
Axes of the slice: x: 2, y: 2, z: 4, core: 2. Of those that a mesh axis runs over, the one named last changes fastest.
Arguments:
- right_side: float32 [32, 256], P(('row', 'col')), may hold values from -6 to 6
- precond: float32 [32, 256], P(('row', 'col')), may hold values from 0.3 to 3
- scaling: float32 [64, 256], P('col'), may hold values from 0.1 to 10
- blocks: float32 [8, 4, 16, 256, 256], P('col', 'row'), may hold values from -0.09375 to 0.09375
- block_count: int32 [8, 4], P('col', 'row'), may hold values from 5 to 16, as said below
- block_rows: int32 [8, 4, 16], P('col', 'row'), may hold values from 0 to 7
- block_cols: int32 [8, 4, 16], P('col', 'row'), may hold values from 0 to 7
Outputs:
- solution_field: float32 [32, 256], P(('row', 'col'))
- residual: float32 [32, 256], P(('row', 'col'))
Inputs may be any that keep to these rules, and one draw needn't show every extreme that they name: `block_count`: each device has between 5 and 16 live slots; device (0, 0) has 16.
All inputs are finite; a program needn't handle non-finite values.
Results may differ from a plain program's by a relative error of at most 0.0003.
Values sent between devices are 32-bit elements; how exact they have to be, the bound alone decides.
No kernel may reach another device: no remote copies, remote signals or barrier semaphores. Data moves between devices by JAX's collectives and lax.ppermute only.
A program may use at most 64 MiB of HBM per device.

v0:
```python
import jax
import jax.numpy as jnp
from jax import lax
from jax.sharding import PartitionSpec as P

ITERS = 2


ridge_weight = 0.5


def run_solver(residual, weights, operate, inner):
    solution_field = jnp.zeros_like(residual)
    precon_res = weights * residual
    direction = precon_res
    gamma = inner((jnp.sum(residual * precon_res),))[0]
    for step in range(ITERS):
        image = operate(direction)
        alpha = gamma / inner((jnp.sum(direction * image),))[0]
        solution_field = solution_field + alpha * direction
        residual = residual - alpha * image
        if step + 1 < ITERS:
            precon_res = weights * residual
            gamma_next = inner((jnp.sum(residual * precon_res),))[0]
            direction = precon_res + gamma_next / gamma * direction
            gamma = gamma_next
    return (solution_field, residual)


def local(right_side, precond, scaling, blocks, block_count, block_rows, block_cols):
    highest = lax.Precision.HIGHEST
    tiles = blocks[0, 0]
    row_index = block_rows[0, 0]
    col_index = block_cols[0, 0]
    live = (jnp.arange(tiles.shape[0], dtype=jnp.int32) < block_count[0, 0]).astype(jnp.float32)
    own_rows = right_side.shape[0]
    group_rows = own_rows * lax.axis_size("col")
    row_table = jnp.where(
        row_index[None, :] == jnp.arange(group_rows, dtype=jnp.int32)[:, None], live[None, :], 0.0
    )
    col_table = jnp.where(
        col_index[None, :] == jnp.arange(scaling.shape[0], dtype=jnp.int32)[:, None],
        live[None, :],
        0.0,
    )

    def apply_blocks(whole):
        picked = whole[row_index]
        lifted = jnp.einsum("kab,ka->kb", tiles, picked, precision=highest)
        partial_cols = jnp.dot(col_table, lifted, precision=highest)
        column_total = lax.psum(partial_cols, "row")
        weighted = scaling * column_total
        spread = jnp.dot(col_table.T, weighted, precision=highest)
        return jnp.einsum("kab,kb->ka", tiles, spread, precision=highest)

    residual, weights = (
        lax.all_gather(right_side, "col", axis=0, tiled=True),
        lax.all_gather(precond, "col", axis=0, tiled=True),
    )

    def operate(vector):
        contrib = apply_blocks(vector)
        summed = lax.psum(jnp.dot(row_table, contrib, precision=highest), "col")
        return summed + ridge_weight * vector

    def inner(values):
        return lax.psum(values, "row")

    solution_field, residual = run_solver(residual, weights, operate, inner)
    offset = lax.axis_index("col") * own_rows
    solution_field = lax.dynamic_slice_in_dim(solution_field, offset, own_rows, 0)
    residual = lax.dynamic_slice_in_dim(residual, offset, own_rows, 0)
    return (solution_field, residual)


def solution(mesh):
    placed = (
        P(("row", "col"), None),
        P(("row", "col"), None),
        P("col", None),
        P("col", "row", None, None, None),
        P("col", "row"),
        P("col", "row", None),
        P("col", "row", None),
    )
    return jax.shard_map(
        local,
        mesh=mesh,
        in_specs=placed,
        out_specs=(P(("row", "col"), None), P(("row", "col"), None)),
        check_vma=False,
    )
```

profile of v0, /device:TPU:0, one launch (start us, length us, event | category | flops | bytes accessed | tf_op | source)
XLA Modules:
  0.0 138.4 jit_solution(4918166018955609358)
XLA Ops:
  0.6 0.0 copy-start.1
  0.6 0.0 copy-start
  0.6 22.6 %all-gather = f32[8,1,256]{2,1,0:T(1,128)S(1)} all-gather(f32[1,1,256]{2,1,0:T(1,128)} %bitcast.59), channel_id=1, replica_groups=mesh['col'=8,'row'=4] {'col'}, dimensions={0}, use_global_device_ids=true | all-gather | bytes 9216 | tf_op jit(solution)/shard_map/all_gather | solution.py:57
  23.2 16.6 %all-gather.1 = f32[8,1,256]{2,1,0:T(1,128)S(1)} all-gather(f32[1,1,256]{2,1,0:T(1,128)} %bitcast.60), channel_id=1, replica_groups=mesh['col'=8,'row'=4] {'col'}, dimensions={0}, use_global_device_ids=true | all-gather | bytes 9216 | tf_op jit(solution)/shard_map/all_gather | solution.py:58
  39.8 0.7 fusion.52
  40.5 0.6 gather_fusion
  41.1 0.0 copy-start.2
  41.1 4.3 %fusion.6 = f32[16,1,256]{2,1,0:T(1,128)S(1)} fusion(f32[1,1,16,256,256]{4,3,2,1,0:T(8,128)} %param.10, f32[16,256,1]{1,0,2:T(8,128)S(1)} %bitcast.52), kind=kOutput, calls=%fused_computation.8 | convolution fusion | flops 12582912 | bytes 4227072 | tf_op jit(solution)/shard_map/kab,ka->kb/dot_general | solution.py:49
  46.0 0.0 copy-done.1
  46.0 0.1 fusion.14
  46.2 5.8 %psum.57 = f32[8,256]{1,0:T(8,128)S(1)} all-reduce(f32[8,256]{1,0:T(8,128)S(1)} %fusion.14), channel_id=1, replica_groups=mesh['col'=8,'row'=4] {'row'}, use_global_device_ids=true, to_apply=%region_2.3 | all-reduce | flops 2048 | bytes 16384 | tf_op jit(solution)/shard_map/psum | solution.py:51
  51.9 0.0 copy-done
  51.9 0.2 convolution_bitcast_fusion.1
  52.1 5.7 %fusion.4 = f32[16,1,256]{2,1,0:T(1,128)S(1)} fusion(f32[1,1,16,256,256]{4,3,2,1,0:T(8,128)} %param.10, f32[16,256,1]{1,0,2:T(8,128)S(1)} %convolution_bitcast_fusion.1), kind=kOutput, calls=%fused_computation.6 | convolution fusion | flops 12582912 | bytes 4227072 | tf_op jit(solution)/shard_map/kab,kb->ka/dot_general | solution.py:54
  57.8 0.0 copy-done.2
  57.8 0.1 fusion.12
  57.9 19.3 %psum.58 = f32[8,256]{1,0:T(8,128)S(1)} all-reduce(f32[8,256]{1,0:T(8,128)S(1)} %fusion.12), channel_id=1, replica_groups=mesh['col'=8,'row'=4] {'col'}, use_global_device_ids=true, to_apply=%region_3.4 | all-reduce | flops 2048 | bytes 16384 | tf_op jit(solution)/shard_map/psum | solution.py:63
  77.2 0.6 multiply_reduce_fusion.2
  77.8 6.3 %all-reduce = (f32[]{:T(128)}, f32[]{:T(128)}) all-reduce(f32[]{:T(128)} %get-tuple-element.3, f32[]{:T(128)} %get-tuple-element.2), channel_id=1, replica_groups=mesh['col'=8,'row'=4] {'row'}, use_global_device_ids=true, to_apply=%region_1.2 | all-reduce | flops 2 | bytes 16 | tf_op jit(solution)/shard_map/psum | solution.py:67
  85.5 0.6 multiply_reduce_fusion.1
  86.1 7.5 %psum.60 = f32[]{:T(128)} all-reduce(f32[]{:T(128)} %get-tuple-element.6), channel_id=1, replica_groups=mesh['col'=8,'row'=4] {'row'}, use_global_device_ids=true, to_apply=%region_7.8 | all-reduce | flops 1 | bytes 8 | tf_op jit(solution)/shard_map/psum | solution.py:67
  94.9 0.6 gather_fusion.1
  95.5 4.3 %fusion.2 = f32[16,1,256]{2,1,0:T(1,128)S(1)} fusion(f32[1,1,16,256,256]{4,3,2,1,0:T(8,128)} %param.10, f32[16,256,1]{1,0,2:T(8,128)S(1)} %bitcast.51), kind=kOutput, calls=%fused_computation.4 | convolution fusion | flops 12582912 | bytes 4227072 | tf_op jit(solution)/shard_map/kab,ka->kb/dot_general | solution.py:49
  99.7 0.1 fusion.10
  99.9 6.2 %psum.61 = f32[8,256]{1,0:T(8,128)S(1)} all-reduce(f32[8,256]{1,0:T(8,128)S(1)} %fusion.10), channel_id=1, replica_groups=mesh['col'=8,'row'=4] {'row'}, use_global_device_ids=true, to_apply=%region_8.9 | all-reduce | flops 2048 | bytes 16384 | tf_op jit(solution)/shard_map/psum | solution.py:51
  106.1 0.2 convolution_bitcast_fusion
  106.3 5.7 %fusion = f32[16,1,256]{2,1,0:T(1,128)S(1)} fusion(f32[1,1,16,256,256]{4,3,2,1,0:T(8,128)} %param.10, f32[16,256,1]{1,0,2:T(8,128)S(1)} %convolution_bitcast_fusion), kind=kOutput, calls=%fused_computation.2 | convolution fusion | flops 12582912 | bytes 4227072 | tf_op jit(solution)/shard_map/kab,kb->ka/dot_general | solution.py:54
  111.9 0.1 fusion.8
  112.1 17.5 %psum.62 = f32[8,256]{1,0:T(8,128)S(1)} all-reduce(f32[8,256]{1,0:T(8,128)S(1)} %fusion.8), channel_id=1, replica_groups=mesh['col'=8,'row'=4] {'col'}, use_global_device_ids=true, to_apply=%region_9.10 | all-reduce | flops 2048 | bytes 16384 | tf_op jit(solution)/shard_map/psum | solution.py:63
  129.6 0.6 multiply_add_fusion
  130.2 6.4 %psum.63 = f32[]{:T(128)} all-reduce(f32[]{:T(128)} %get-tuple-element.9), channel_id=1, replica_groups=mesh['col'=8,'row'=4] {'row'}, use_global_device_ids=true, to_apply=%region_11.12 | all-reduce | flops 1 | bytes 8 | tf_op jit(solution)/shard_map/psum | solution.py:67
  137.9 0.6 dynamic-slice_subtract_fusion
  (4 shorter events, 0.0 us)
Async XLA Ops:
  0.6 45.4 %copy-start.1 = (s32[1,1,16]{2,1,0:T(1,128)S(1)}, s32[1,1,16]{2,1,0:T(1,128)}, u32[]{:S(2)}) copy-start(s32[1,1,16]{2,1,0:T(1,128)} %param.13) | copy-start | bytes 196
  0.6 51.3 %copy-start = (f32[8,256]{1,0:T(8,128)S(1)}, f32[8,256]{1,0:T(8,128)}, u32[]{:S(2)}) copy-start(f32[8,256]{1,0:T(8,128)} %param.9) | copy-start | bytes 24580
  41.1 16.7 %copy-start.2 = (s32[1,1,16]{2,1,0:T(1,128)S(1)}, s32[1,1,16]{2,1,0:T(1,128)}, u32[]{:S(2)}) copy-start(s32[1,1,16]{2,1,0:T(1,128)} %param.12) | copy-start | bytes 196
where the time goes:
time: 139 us; the launch traced here: 138 us
  blocking collectives  108 us (78%)
  matrix products  20.8 us (15%)
  between operations  5.42 us (4%)
  other arithmetic  3.08 us (2%)
    psum x2, blocking collectives, operate(): summed = lax.psum(jnp.dot(row_table, contrib, precision=highest), 'col')  36.8 us
    all_gather x1, blocking collectives, local(): lax.all_gather(right_side, 'col', axis=0, tiled=True)  22.6 us
    psum x3, blocking collectives, inner(): return lax.psum(values, 'row')  20.1 us
    all_gather x1, blocking collectives, local(): lax.all_gather(precond, 'col', axis=0, tiled=True)  16.6 us
    psum x2, blocking collectives, apply_blocks(): column_total = lax.psum(partial_cols, 'row')  11.9 us
    dot_general x2, matrix products, apply_blocks(): return jnp.einsum('kab,kb->ka', tiles, spread, precision=highest)  11.3 us
    dot_general x2, matrix products, apply_blocks(): lifted = jnp.einsum('kab,ka->kb', tiles, picked, precision=highest)  8.56 us

commit v1 on v0

v1 whole, which is shorter than its diff:
```python
import jax
import jax.numpy as jnp
from jax import lax
from jax.experimental import pallas as pl
from jax.experimental.pallas import tpu as pltpu
from jax.sharding import PartitionSpec as P

ridge_weight = 0.5
LANES = 128
EXTRA = 8
VMEM_LIMIT = 16 << 20
F32 = jnp.float32
BF16 = jnp.bfloat16


def vmem():
    return pl.BlockSpec(memory_space=pltpu.VMEM)


def smem():
    return pl.BlockSpec(memory_space=pltpu.SMEM)


def call(body, name, out_shapes, args, in_specs=None, scratch=(), flops=0, moved=0):
    return pl.pallas_call(
        body,
        name=name,
        out_shape=[pltpu.VMEM(s, d) for s, d in out_shapes],
        in_specs=in_specs or [vmem()] * len(args),
        out_specs=[vmem()] * len(out_shapes),
        scratch_shapes=list(scratch),
        compiler_params=pltpu.CompilerParams(vmem_limit_bytes=VMEM_LIMIT),
        cost_estimate=pl.CostEstimate(flops=flops, bytes_accessed=moved, transcendentals=0),
    )(*args)


def split(x):
    high = x.astype(BF16).astype(F32)
    return jnp.concatenate([high, x - high], axis=0).astype(BF16)


def lane_sum(row):
    return jnp.sum(row, axis=1, keepdims=True)


def row_sum(x):
    return jnp.sum(x, axis=0, keepdims=True)


def block_product(table, vector, high, low, slots):
    placed = jnp.dot(table, split(vector), preferred_element_type=F32).astype(BF16)
    step = placed.shape[0] // slots
    size = vector.shape[1]
    total = jnp.zeros((step, size), F32)
    rest = jnp.zeros((step, size), F32)
    for k in range(slots):
        left = placed[k * step : (k + 1) * step]
        total += jnp.dot(left, high[k * size : (k + 1) * size, :], preferred_element_type=F32)
        rest += jnp.dot(left, low[k * size : (k + 1) * size, :], preferred_element_type=F32)
    total += rest
    half = step // 2
    return total[:half] + total[half:]


def prepare_body(group, cols, tiles, count, rows_of, cols_of, high, low, high_t, low_t, to_cols, to_rows, own, buf, sem):
    slots = buf.shape[0]
    size = buf.shape[1]

    def copy(k):
        return pltpu.make_async_copy(tiles.at[0, 0, k], buf.at[k], sem.at[k])

    @pl.loop(0, slots)
    def _(k):
        copy(k).start()

    def table(targets, sources, target, source, live):
        r = lax.broadcasted_iota(jnp.int32, (2 * targets, 2 * sources), 0)
        q = lax.broadcasted_iota(jnp.int32, (2 * targets, 2 * sources), 1)
        first = (r == target) & (q == source)
        second = (r == targets + target) & (q == sources + source)
        return jnp.where((first | second) & live, 1.0, 0.0).astype(BF16)

    @pl.loop(0, slots)
    def _(k):
        live = k < count[0, 0]
        row, col = rows_of[0, 0, k], cols_of[0, 0, k]
        to_cols[pl.ds(pl.multiple_of(k * 2 * cols, 2 * cols), 2 * cols), :] = table(cols, group, col, row, live)
        to_rows[pl.ds(pl.multiple_of(k * 2 * group, 2 * group), 2 * group), :] = table(group, cols, row, col, live)

    mine = lax.broadcasted_iota(jnp.int32, own.shape, 0) == lax.axis_index("col")
    own[...] = jnp.where(mine, 1.0, 0.0)

    @pl.loop(0, slots)
    def _(k):
        copy(k).wait()
        here = pl.ds(pl.multiple_of(k * size, size), size)
        tile = buf[k]
        part = tile.astype(BF16)
        high[here, :] = part
        low[here, :] = (tile - part.astype(F32)).astype(BF16)
        flip = tile.T
        part = flip.astype(BF16)
        high_t[here, :] = part
        low_t[here, :] = (flip - part.astype(F32)).astype(BF16)


def first_body(slots, gathered, high, low, to_cols, out):
    residual, weights = gathered[:, 0, :], gathered[:, 1, :]
    z = weights * residual
    cols = out.shape[0] - EXTRA
    out[pl.ds(cols, EXTRA), :] = jnp.zeros((EXTRA, out.shape[1]), F32)
    out[pl.ds(cols, 1), :] = row_sum(residual * z)
    out[pl.ds(cols + 1, 1), :] = row_sum(z * z)
    out[pl.ds(0, cols), :] = block_product(to_cols[...], z, high, low, slots)


def second_body(slots, peers, p0, p1, p2, p3, scaling, high_t, low_t, to_rows, total, out):
    summed = (p0[...] + p1[...]) + (p2[...] + p3[...])
    total[...] = summed
    cols = scaling.shape[0]
    lifted = summed[:cols]
    weighted = scaling[...] * lifted
    inner = row_sum(weighted * lifted)
    rows = block_product(to_rows[...], weighted, high_t, low_t, slots)
    group = rows.shape[0]
    for j in range(peers):
        out[j, pl.ds(0, group), :] = rows
        out[j, pl.ds(group, EXTRA), :] = jnp.broadcast_to(inner, (EXTRA, inner.shape[1]))


def third_body(slots, arrived, gathered, total, high, low, to_cols, out, residual_out, alpha_out):
    residual, weights = gathered[:, 0, :], gathered[:, 1, :]
    z = weights * residual
    group = residual.shape[0]
    cols = out.shape[0] - EXTRA
    summed = jnp.sum(arrived[...], axis=0)
    image = summed[:group] + ridge_weight * z
    gamma = lane_sum(total[pl.ds(cols, 1), :])
    curve = lane_sum(summed[group : group + 1]) + ridge_weight * lane_sum(total[pl.ds(cols + 1, 1), :])
    alpha = gamma / curve
    alpha_out[...] = jnp.broadcast_to(alpha, alpha_out.shape)
    later = residual - alpha * image
    residual_out[...] = later
    z1 = weights * later
    out[pl.ds(cols, EXTRA), :] = jnp.zeros((EXTRA, out.shape[1]), F32)
    out[pl.ds(cols, 1), :] = row_sum(later * z1)
    out[pl.ds(cols + 1, 1), :] = row_sum(z1 * z1)
    out[pl.ds(cols + 2, 1), :] = row_sum(z1 * z)
    out[pl.ds(0, cols), :] = block_product(to_cols[...], z1, high, low, slots)


def fourth_body(slots, p0, p1, p2, p3, total, gathered, residual, scaling, high_t, low_t, to_rows, out, direction_out, scalars):
    summed = (p0[...] + p1[...]) + (p2[...] + p3[...])
    cols = scaling.shape[0]
    gamma = lane_sum(total[pl.ds(cols, 1), :])
    norm = lane_sum(total[pl.ds(cols + 1, 1), :])
    later = lane_sum(summed[cols : cols + 1])
    beta = later / gamma
    square = lane_sum(summed[cols + 1 : cols + 2]) + beta * (2.0 * lane_sum(summed[cols + 2 : cols + 3]) + beta * norm)
    lifted = summed[:cols] + beta * total[pl.ds(0, cols), :]
    weighted = scaling[...] * lifted
    inner = row_sum(weighted * lifted)
    rows = block_product(to_rows[...], weighted, high_t, low_t, slots)
    peers, pieces = out.shape[0], rows.shape[1] // LANES
    own = rows.shape[0] // peers
    for h in range(pieces):
        here = slice(h * LANES, (h + 1) * LANES)
        for m in range(own):
            out[:, m * pieces + h, :] = rows.reshape(peers, own, -1)[:, m, here] if own > 1 else rows[:, here]
        out[:, own * pieces + h, :] = jnp.broadcast_to(inner[:, here], (peers, LANES))
    weights = gathered[:, 1, :]
    direction_out[...] = weights * residual[...] + beta * (weights * gathered[:, 0, :])
    scalars[pl.ds(0, 1), :] = jnp.broadcast_to(later, (1, LANES))
    scalars[pl.ds(1, 1), :] = jnp.broadcast_to(square, (1, LANES))


def last_body(arrived, gathered, residual, direction, alpha, scalars, own, solution, residual_out):
    pieces = solution.shape[1] // LANES
    mask = own[:, :1]
    summed = jnp.sum(arrived[...], axis=0)
    image = jnp.concatenate([summed[h : h + 1] for h in range(pieces)], axis=1)
    inner = summed[pieces : pieces + 1]
    for h in range(1, pieces):
        inner += summed[pieces + h : pieces + h + 1]
    curve = lane_sum(inner) + ridge_weight * scalars[1:2, :1]
    step = scalars[0:1, :1] / curve
    first = row_sum(mask * (gathered[:, 0, :] * gathered[:, 1, :]))
    second = row_sum(mask * direction[...])
    before = row_sum(mask * residual[...])
    solution[...] = alpha[:1, :1] * first + step * second
    residual_out[...] = before - step * (image + ridge_weight * second)


def share(value, axis, size):
    moved = [value]
    for s in range(1, size):
        moved.append(lax.ppermute(value, axis, [(i, i ^ s) for i in range(size)]))
    return moved


def local(right_side, precond, scaling, blocks, block_count, block_rows, block_cols):
    peers = lax.axis_size("col")
    groups = lax.axis_size("row")
    slots, size = blocks.shape[2], blocks.shape[3]
    group = right_side.shape[0] * peers
    cols = scaling.shape[0]
    long = slots * size

    both = jnp.stack([right_side, precond], axis=1)
    gathered = lax.all_to_all(
        jnp.broadcast_to(both, (peers, 2, size)), "col", 0, 0, tiled=True
    )
    high, low, high_t, low_t, to_cols, to_rows, own = call(
        lambda *refs: prepare_body(group, cols, *refs),
        "prepare",
        [((long, size), BF16)] * 4
        + [((slots * 2 * cols, 2 * group), BF16), ((slots * 2 * group, 2 * cols), BF16), ((group, LANES), F32)],
        (blocks, block_count, block_rows, block_cols),
        in_specs=[pl.BlockSpec(memory_space=pl.ANY), smem(), smem(), smem()],
        scratch=[pltpu.VMEM((slots, size, size), F32), pltpu.SemaphoreType.DMA((slots,))],
        flops=8 * long * size,
        moved=4 * long * size,
    )
    work = dict(flops=8 * long * size, moved=0)
    (mine,) = call(
        lambda *refs: first_body(slots, *refs),
        "first",
        [((cols + EXTRA, size), F32)],
        (gathered, high, low, to_cols),
        **work,
    )
    total, sent = call(
        lambda *refs: second_body(slots, peers, *refs),
        "second",
        [((cols + EXTRA, size), F32), ((peers, group + EXTRA, size), F32)],
        (*share(mine, "row", groups), scaling, high_t, low_t, to_rows),
        **work,
    )
    arrived = lax.all_to_all(sent, "col", 0, 0, tiled=True)
    mine, residual, alpha = call(
        lambda *refs: third_body(slots, *refs),
        "third",
        [((cols + EXTRA, size), F32), ((group, size), F32), ((1, LANES), F32)],
        (arrived, gathered, total, high, low, to_cols),
        **work,
    )
    pieces = size // LANES
    sent, direction, scalars = call(
        lambda *refs: fourth_body(slots, *refs),
        "fourth",
        [((peers, (right_side.shape[0] + 1) * pieces, LANES), F32), ((group, size), F32), ((2, LANES), F32)],
        (*share(mine, "row", groups), total, gathered, residual, scaling, high_t, low_t, to_rows),
        **work,
    )
    arrived = lax.all_to_all(sent, "col", 0, 0, tiled=True)
    return pl.pallas_call(
        last_body,
        name="last",
        out_shape=[jax.ShapeDtypeStruct(right_side.shape, F32)] * 2,
        in_specs=[vmem()] * 7,
        out_specs=[vmem()] * 2,
        compiler_params=pltpu.CompilerParams(vmem_limit_bytes=VMEM_LIMIT),
    )(arrived, gathered, residual, direction, alpha, scalars, own)


def solution(mesh):
    placed = (
        P(("row", "col"), None),
        P(("row", "col"), None),
        P("col", None),
        P("col", "row", None, None, None),
        P("col", "row"),
        P("col", "row", None),
        P("col", "row", None),
    )
    return jax.shard_map(
        local,
        mesh=mesh,
        in_specs=placed,
        out_specs=(P(("row", "col"), None), P(("row", "col"), None)),
        check_vma=False,
    )
```

time: 139 us -> 59 us (0.42)
  blocking collectives: 108 us -> 21.9 us
  matrix products: 20.8 us -> 0 us
  starting transfers between devices: 0 us -> 11.1 us
  local copies, waits for them, and re-layouts: 1.16 us -> 11.3 us
  Pallas kernels: 0 us -> 7.71 us
  waiting for transfers between devices: 0 us -> 4.61 us
  between operations: 5.42 us -> 1.34 us
  other arithmetic: 3.08 us -> 0.7 us
    psum x7 -> x0, blocking collectives: 68.8 us -> none  [the longest x2 36.8 us: operate(): summed = lax.psum(jnp.dot(row_table, contrib, precision=highest), 'col')]
    all_gather x2 -> x0, blocking collectives: 39.2 us -> none  [the longest x1 22.6 us: local(): lax.all_gather(right_side, 'col', axis=0, tiled=True)]
    all_to_all x0 -> x2, blocking collectives: none -> 21.9 us  [local(): arrived = lax.all_to_all(sent, 'col', 0, 0, tiled=True)]
    dot_general x10 -> x0, matrix products: 20.8 us -> none  [the longest x2 11.3 us: apply_blocks(): return jnp.einsum('kab,kb->ka', tiles, spread, precision=highest)]
    unnamed x6 -> x20, local copies, waits for them, and re-layouts: 0.01 us -> 10.7 us
    pallas_call x0 -> x6, Pallas kernels: none -> 7.71 us  [the longest x5 6.97 us: call(): pl.pallas_call(body, name=name, out_shape=[pltpu.VMEM(s, d) for s, d in o...]
    all_to_all x0 -> x1, starting transfers between devices: none -> 7.31 us  [local(): lax.all_to_all(jnp.broadcast_to(both, (peers, 2, size)), 'col', 0, 0, til...]
    ppermute x0 -> x6, waiting for transfers between devices: none -> 4.61 us  [share(): moved.append(lax.ppermute(value, axis, [(i, i ^ s) for i in range(size)]))]
  transfers between devices with their start and end apart: 0 -> 7, of which waited for: 0 -> 4; matrix products, arithmetic and copies ran while one was open for 0% -> 0% of each run, Pallas kernels for 0% -> 6%
where the time goes in v1:
time: 59 us; the launch traced here: 58.6 us
  blocking collectives  21.9 us (37%)
  local copies, waits for them, and re-layouts  11.3 us (19%)
  starting transfers between devices  11.1 us (19%)
  Pallas kernels  7.71 us (13%)
  waiting for transfers between devices  4.61 us (8%)
  between operations  1.34 us (2%)
  other arithmetic  0.7 us (1%)
    all_to_all x2, blocking collectives, local(): arrived = lax.all_to_all(sent, 'col', 0, 0, tiled=True)  21.9 us
    unnamed x20, local copies, waits for them, and re-layouts  10.7 us
    all_to_all x1, starting transfers between devices, local(): lax.all_to_all(jnp.broadcast_to(both, (peers, 2, size)), 'col', 0, 0, til...  7.31 us
    pallas_call x5, Pallas kernels, call(): pl.pallas_call(body, name=name, out_shape=[pltpu.VMEM(s, d) for s, d in o...  6.97 us
    ppermute x6, waiting for transfers between devices, share(): moved.append(lax.ppermute(value, axis, [(i, i ^ s) for i in range(size)]))  4.61 us
    ppermute x6, starting transfers between devices, share(): moved.append(lax.ppermute(value, axis, [(i, i ^ s) for i in range(size)]))  3.78 us
  transfers between devices with their start and end apart: 7, of which 4 were waited for; matrix products, arithmetic and copies ran while one was open for 0% of the time, Pallas kernels for 6%

profile of v1, /device:TPU:0, one launch (start us, length us, event | category | flops | bytes accessed | tf_op | source)
XLA Modules:
  0.0 58.6 jit_solution(3219178362580097009)
XLA Ops:
  0.6 0.7 %maximum_bitcast_fusion = f32[2,256]{1,0:T(2,128)S(1)} fusion(f32[1,1,256]{2,1,0:T(1,128)} %bitcast.4, f32[1,1,256]{2,1,0:T(1,128)} %bitcast.5), kind=kLoop, calls=%fused_computation | loop fusion | flops 512 | bytes 4096 | tf_op jit(solution)/shard_map/broadcast_in_dim | solution.py:211
  1.3 0.6 %broadcast_in_dim.8 = f32[8,2,256]{2,1,0:T(2,128)} broadcast(f32[2,256]{1,0:T(2,128)S(1)} %maximum_bitcast_fusion), dimensions={1,2} | broadcast | bytes 18432 | tf_op jit(solution)/shard_map/broadcast_in_dim | solution.py:211
  1.9 7.3 %all-to-all-start = ((f32[8,2,256]{2,1,0:T(2,128)}), f32[8,2,256]{2,1,0:T(2,128)S(1)}, u32[]{:S(2)}, u32[]{:S(2)}) async-start(f32[8,2,256]{2,1,0:T(2,128)} %broadcast_in_dim.8), calls=%async_computation | async-start | bytes 32768 | tf_op jit(solution)/shard_map/all_to_all | solution.py:210
  9.9 0.0 copy-start.6
  9.9 2.2 %copy-done.6 = f32[1,1,16,256,256]{4,3,2,1,0:T(8,128)S(1)} copy-done((f32[1,1,16,256,256]{4,3,2,1,0:T(8,128)S(1)}, f32[1,1,16,256,256]{4,3,2,1,0:T(8,128)}, u32[]{:S(2)}) %copy-start.6) | copy-done | bytes 4194328
  12.1 0.7 %copy-done.8 = s32[1,1,16]{2,1,0:T(1,128)S(1)} copy-done((s32[1,1,16]{2,1,0:T(1,128)S(1)}, s32[1,1,16]{2,1,0:T(1,128)}, u32[]{:S(2)}) %copy-start.8) | copy-done | bytes 88
  12.8 0.7 %copy-done.9 = s32[1,1,16]{2,1,0:T(1,128)S(1)} copy-done((s32[1,1,16]{2,1,0:T(1,128)S(1)}, s32[1,1,16]{2,1,0:T(1,128)}, u32[]{:S(2)}) %copy-start.9) | copy-done | bytes 88
  13.4 3.6 %prepare.1 = (bf16[4096,256]{1,0:T(8,128)(2,1)S(1)}, bf16[4096,256]{1,0:T(8,128)(2,1)S(1)}, bf16[4096,256]{1,0:T(8,128)(2,1)S(1)}, bf16[4096,256]{1,0:T(8,128)(2...) custom-call(f32[1,1,16,256,256]{4,3,2,1,0:T(8,128)S(1)} %copy-done.6, ...), custom_call_target="tpu_custom_call" | custom-call | flops 8388608 | bytes 4194304 | tf_op jit(solution)/shard_map/prepare/pallas_call | solution.py:25
  17.0 1.3 %copy-done = bf16[4096,256]{1,0:T(8,128)(2,1)} copy-done((bf16[4096,256]{1,0:T(8,128)(2,1)}, bf16[4096,256]{1,0:T(8,128)(2,1)S(1)}, u32[]{:S(2)}) %copy-start) | copy-done | bytes 2097176
  18.3 1.3 %copy-done.2 = bf16[4096,256]{1,0:T(8,128)(2,1)} copy-done((bf16[4096,256]{1,0:T(8,128)(2,1)}, bf16[4096,256]{1,0:T(8,128)(2,1)S(1)}, u32[]{:S(2)}) %copy-start.2) | copy-done | bytes 2097176
  19.6 1.3 %copy-done.4 = bf16[4096,256]{1,0:T(8,128)(2,1)} copy-done((bf16[4096,256]{1,0:T(8,128)(2,1)}, bf16[4096,256]{1,0:T(8,128)(2,1)S(1)}, u32[]{:S(2)}) %copy-start.4) | copy-done | bytes 2097176
  21.0 0.0 all-to-all-done.refs_0_.refs_1_.refs_5_.gathered
  21.0 1.6 %copy-done.3 = bf16[4096,256]{1,0:T(8,128)(2,1)S(1)} copy-done((bf16[4096,256]{1,0:T(8,128)(2,1)S(1)}, bf16[4096,256]{1,0:T(8,128)(2,1)}, u32[]{:S(2)}) %copy-start.3) | copy-done | bytes 2097176
  22.6 1.6 %copy-done.5 = bf16[4096,256]{1,0:T(8,128)(2,1)S(1)} copy-done((bf16[4096,256]{1,0:T(8,128)(2,1)S(1)}, bf16[4096,256]{1,0:T(8,128)(2,1)}, u32[]{:S(2)}) %copy-start.5) | copy-done | bytes 2097176
  24.1 0.8 %first.1.refs_0_ = f32[16,256]{1,0:T(8,128)S(1)} custom-call(f32[8,2,256]{2,1,0:T(2,128)S(1)} %all-to-all-done.refs_0_.refs_1_.refs_5_.gathered, bf16[4096,256]{1,0:T(8,128)(2,1)S(1)} %copy-done.3, bf16[4096,256]{1,0:T(8,128)(2,1)S(1)} %copy-done.5, bf16[256,16]{1,0:T(8,128)(2,1)S(1)} %get-tuple-element.19.refs_3_.refs_5_), custom_call_target="tpu_custom_call" | custom-call | flops 8388608 | tf_op jit(solution)/shard_map/first/pallas_call | solution.py:25
  25.0 0.7 %collective-permute-start.2 = (f32[16,256]{1,0:T(8,128)S(1)}, f32[16,256]{1,0:T(8,128)S(1)}, u32[]{:S(2)}, u32[]{:S(2)}) collective-permute-start(f32[16,256]{1,0:T(8,128)S(1)} %first.1.refs_0_), channel_id=1, source_target_pairs={{0,3},{1,2},{2,1},{3,0},{4,7},{5,6},{6,5},{7,4},{8,11},{9,10},{10,... | collective-permute-start | bytes 49160 | tf_op jit(solution)/shard_map/ppermute | solution.py:197
  25.6 0.9 %collective-permute-start.1 = (f32[16,256]{1,0:T(8,128)S(1)}, f32[16,256]{1,0:T(8,128)S(1)}, u32[]{:S(2)}, u32[]{:S(2)}) collective-permute-start(f32[16,256]{1,0:T(8,128)S(1)} %first.1.refs_0_), channel_id=1, source_target_pairs={{0,2},{1,3},{2,0},{3,1},{4,6},{5,7},{6,4},{7,5},{8,10},{9,11},{10,... | collective-permute-start | bytes 49160 | tf_op jit(solution)/shard_map/ppermute | solution.py:197
  26.5 0.3 collective-permute-start
  26.9 1.4 %collective-permute-done.2.refs_3_ = f32[16,256]{1,0:T(8,128)S(1)} collective-permute-done((f32[16,256]{1,0:T(8,128)S(1)}, f32[16,256]{1,0:T(8,128)S(1)}, u32[]{:S(2)}, u32[]{:S(2)}) %collective-permute-start.2) | collective-permute-done | bytes 16416 | tf_op jit(solution)/shard_map/ppermute | solution.py:197
  28.3 1.3 %collective-permute-done.1.refs_2_ = f32[16,256]{1,0:T(8,128)S(1)} collective-permute-done((f32[16,256]{1,0:T(8,128)S(1)}, f32[16,256]{1,0:T(8,128)S(1)}, u32[]{:S(2)}, u32[]{:S(2)}) %collective-permute-start.1) | collective-permute-done | bytes 16416 | tf_op jit(solution)/shard_map/ppermute | solution.py:197
  29.5 0.0 collective-permute-done.refs_1_
  29.6 0.8 %second.1 = (f32[16,256]{1,0:T(8,128)S(1)}, f32[8,16,256]{2,1,0:T(8,128)S(1)}) custom-call(f32[16,256]{1,0:T(8,128)S(1)} %first.1.refs_0_, f32[16,256]{1,0:T(8,128)S(1)} %collective-permute-done.refs_1_, f32[16,256]{1,0:T(8,128)S(1)} %collective-permute-done.1.refs_2_, f32[16,256]{1,0:T(8,128)S(1)} %collective-permute-done.2.refs_3_, ...), custom_call_target="tpu_custom_call" | custom-call | flops 8388608 | tf_op jit(solution)/shard_map/second/pallas_call | solution.py:25
  30.4 12.7 %all_to_all.15.refs_0_ = f32[8,16,256]{2,1,0:T(8,128)S(1)} all-to-all(f32[8,16,256]{2,1,0:T(8,128)S(1)} %get-tuple-element.23), channel_id=1, replica_groups=mesh['col'=8,'row'=4] {'col'}, dimensions={0} | all-to-all | bytes 262144 | tf_op jit(solution)/shard_map/all_to_all | solution.py:239
  43.1 0.9 %third.1 = (f32[16,256]{1,0:T(8,128)S(1)}, f32[8,256]{1,0:T(8,128)S(1)}, f32[1,128]{1,0:T(1,128)S(1)}) custom-call(f32[8,16,256]{2,1,0:T(8,128)S(1)} %all_to_all.15.refs_0_, f32[8,2,256]{2,1,0:T(2,128)S(1)} %all-to-all-done.refs_0_.refs_1_.refs_5_.gathered, f32[16,256]{1,0:T(8,128)S(1)} %get-tuple-element.24.refs_2_.refs_4_, ...), custom_call_target="tpu_custom_call" | custom-call | flops 8388608 | tf_op jit(solution)/shard_map/third/pallas_call | solution.py:25
  43.9 0.0 collective-permute-start.5
  44.0 1.2 %collective-permute-start.4 = (f32[16,256]{1,0:T(8,128)S(1)}, f32[16,256]{1,0:T(8,128)S(1)}, u32[]{:S(2)}, u32[]{:S(2)}) collective-permute-start(f32[16,256]{1,0:T(8,128)S(1)} %get-tuple-element.25.refs_0_), channel_id=1, source_target_pairs={{0,2},{1,3},{2,0},{3,1},{4,6},{5,7},{6,4},{7,5},{8,10},{9,11},{10,... | collective-permute-start | bytes 49160 | tf_op jit(solution)/shard_map/ppermute | solution.py:197
  45.2 0.7 %collective-permute-start.3 = (f32[16,256]{1,0:T(8,128)S(1)}, f32[16,256]{1,0:T(8,128)S(1)}, u32[]{:S(2)}, u32[]{:S(2)}) collective-permute-start(f32[16,256]{1,0:T(8,128)S(1)} %get-tuple-element.25.refs_0_), channel_id=1, source_target_pairs={{0,1},{1,0},{2,3},{3,2},{4,5},{5,4},{6,7},{7,6},{8,9},{9,8},{10,11... | collective-permute-start | bytes 49160 | tf_op jit(solution)/shard_map/ppermute | solution.py:197
  45.8 1.3 %collective-permute-done.5.refs_3_ = f32[16,256]{1,0:T(8,128)S(1)} collective-permute-done((f32[16,256]{1,0:T(8,128)S(1)}, f32[16,256]{1,0:T(8,128)S(1)}, u32[]{:S(2)}, u32[]{:S(2)}) %collective-permute-start.5) | collective-permute-done | bytes 16416 | tf_op jit(solution)/shard_map/ppermute | solution.py:197
  47.1 0.6 %collective-permute-done.4.refs_2_ = f32[16,256]{1,0:T(8,128)S(1)} collective-permute-done((f32[16,256]{1,0:T(8,128)S(1)}, f32[16,256]{1,0:T(8,128)S(1)}, u32[]{:S(2)}, u32[]{:S(2)}) %collective-permute-start.4) | collective-permute-done | bytes 16416 | tf_op jit(solution)/shard_map/ppermute | solution.py:197
  47.8 0.9 %fourth.1 = (f32[8,4,128]{2,1,0:T(4,128)S(1)}, f32[8,256]{1,0:T(8,128)S(1)}, f32[2,128]{1,0:T(2,128)S(1)}) custom-call(f32[16,256]{1,0:T(8,128)S(1)} %get-tuple-element.25.refs_0_, f32[16,256]{1,0:T(8,128)S(1)} %collective-permute-done.3.refs_1_, f32[16,256]{1,0:T(8,128)S(1)} %collective-permute-done.4.refs_2_, ...), custom_call_target="tpu_custom_call" | custom-call | flops 8388608 | tf_op jit(solution)/shard_map/fourth/pallas_call | solution.py:25
  48.7 9.2 %all_to_all.16.arrived = f32[8,4,128]{2,1,0:T(4,128)S(1)} all-to-all(f32[8,4,128]{2,1,0:T(4,128)S(1)} %get-tuple-element.27), channel_id=1, replica_groups=mesh['col'=8,'row'=4] {'col'}, dimensions={0} | all-to-all | bytes 32768 | tf_op jit(solution)/shard_map/all_to_all | solution.py:255
  57.9 0.7 %last.1 = (f32[1,256]{1,0:T(1,128)}, f32[1,256]{1,0:T(1,128)}) custom-call(f32[8,4,128]{2,1,0:T(4,128)S(1)} %all_to_all.16.arrived, f32[8,2,256]{2,1,0:T(2,128)S(1)} %all-to-all-done.refs_0_.refs_1_.refs_5_.gathered, f32[8,256]{1,0:T(8,128)S(1)} %get-tuple-element.26.refs_6_.residual, f32[8,256]{1,0:T(8,128)S(1)} %get-tuple-element.28.direction, ...), custom_call_target="tpu_custom_call" | custom-call | tf_op jit(solution)/shard_map/last/pallas_call | solution.py:256
  (12 shorter events, 0.0 us)
Async XLA Ops:
  1.9 19.0 %all-to-all-start = ((f32[8,2,256]{2,1,0:T(2,128)}), f32[8,2,256]{2,1,0:T(2,128)S(1)}, u32[]{:S(2)}, u32[]{:S(2)}) async-start(f32[8,2,256]{2,1,0:T(2,128)} %broadcast_in_dim.8), calls=%async_computation | async-start | bytes 32768 | tf_op jit(solution)/shard_map/all_to_all | solution.py:210
  9.9 2.2 %copy-start.6 = (f32[1,1,16,256,256]{4,3,2,1,0:T(8,128)S(1)}, f32[1,1,16,256,256]{4,3,2,1,0:T(8,128)}, u32[]{:S(2)}) copy-start(f32[1,1,16,256,256]{4,3,2,1,0:T(8,128)} %refs_0_.1) | copy-start | bytes 12582916
  12.1 0.7 %copy-start.8 = (s32[1,1,16]{2,1,0:T(1,128)S(1)}, s32[1,1,16]{2,1,0:T(1,128)}, u32[]{:S(2)}) copy-start(s32[1,1,16]{2,1,0:T(1,128)} %refs_2_.1) | copy-start | bytes 196
  12.8 0.7 %copy-start.9 = (s32[1,1,16]{2,1,0:T(1,128)S(1)}, s32[1,1,16]{2,1,0:T(1,128)}, u32[]{:S(2)}) copy-start(s32[1,1,16]{2,1,0:T(1,128)} %refs_3_.1) | copy-start | bytes 196
  17.0 1.3 %copy-start = (bf16[4096,256]{1,0:T(8,128)(2,1)}, bf16[4096,256]{1,0:T(8,128)(2,1)S(1)}, u32[]{:S(2)}) copy-start(bf16[4096,256]{1,0:T(8,128)(2,1)S(1)} %get-tuple-element.21.refs_6_.refs_9_) | copy-start | bytes 6291460
  18.3 1.3 %copy-start.2 = (bf16[4096,256]{1,0:T(8,128)(2,1)}, bf16[4096,256]{1,0:T(8,128)(2,1)S(1)}, u32[]{:S(2)}) copy-start(bf16[4096,256]{1,0:T(8,128)(2,1)S(1)} %get-tuple-element.17.refs_1_.refs_3_) | copy-start | bytes 6291460
  19.6 1.3 %copy-start.4 = (bf16[4096,256]{1,0:T(8,128)(2,1)}, bf16[4096,256]{1,0:T(8,128)(2,1)S(1)}, u32[]{:S(2)}) copy-start(bf16[4096,256]{1,0:T(8,128)(2,1)S(1)} %get-tuple-element.18.refs_2_.refs_4_) | copy-start | bytes 6291460
  21.0 1.6 %copy-start.3 = (bf16[4096,256]{1,0:T(8,128)(2,1)S(1)}, bf16[4096,256]{1,0:T(8,128)(2,1)}, u32[]{:S(2)}) copy-start(bf16[4096,256]{1,0:T(8,128)(2,1)} %copy-done.2) | copy-start | bytes 6291460
  22.6 1.6 %copy-start.5 = (bf16[4096,256]{1,0:T(8,128)(2,1)S(1)}, bf16[4096,256]{1,0:T(8,128)(2,1)}, u32[]{:S(2)}) copy-start(bf16[4096,256]{1,0:T(8,128)(2,1)} %copy-done.4) | copy-start | bytes 6291460
  24.1 5.4 %copy-start.1 = (bf16[4096,256]{1,0:T(8,128)(2,1)S(1)}, bf16[4096,256]{1,0:T(8,128)(2,1)}, u32[]{:S(2)}) copy-start(bf16[4096,256]{1,0:T(8,128)(2,1)} %copy-done) | copy-start | bytes 6291460
  24.1 5.4 %copy-start.7 = (f32[8,256]{1,0:T(8,128)S(1)}, f32[8,256]{1,0:T(8,128)}, u32[]{:S(2)}) copy-start(f32[8,256]{1,0:T(8,128)} %refs_7_.1) | copy-start | bytes 24580
  25.0 3.3 %collective-permute-start.2 = (f32[16,256]{1,0:T(8,128)S(1)}, f32[16,256]{1,0:T(8,128)S(1)}, u32[]{:S(2)}, u32[]{:S(2)}) collective-permute-start(f32[16,256]{1,0:T(8,128)S(1)} %first.1.refs_0_), channel_id=1, source_target_pairs={{0,3},{1,2},{2,1},{3,0},{4,7},{5,6},{6,5},{7,4},{8,11},{9,10},{10,... | collective-permute-start | bytes 49160 | tf_op jit(solution)/shard_map/ppermute | solution.py:197
  25.6 3.9 %collective-permute-start.1 = (f32[16,256]{1,0:T(8,128)S(1)}, f32[16,256]{1,0:T(8,128)S(1)}, u32[]{:S(2)}, u32[]{:S(2)}) collective-permute-start(f32[16,256]{1,0:T(8,128)S(1)} %first.1.refs_0_), channel_id=1, source_target_pairs={{0,2},{1,3},{2,0},{3,1},{4,6},{5,7},{6,4},{7,5},{8,10},{9,11},{10,... | collective-permute-start | bytes 49160 | tf_op jit(solution)/shard_map/ppermute | solution.py:197
  26.5 3.0 %collective-permute-start = (f32[16,256]{1,0:T(8,128)S(1)}, f32[16,256]{1,0:T(8,128)S(1)}, u32[]{:S(2)}, u32[]{:S(2)}) collective-permute-start(f32[16,256]{1,0:T(8,128)S(1)} %first.1.refs_0_), channel_id=1, source_target_pairs={{0,1},{1,0},{2,3},{3,2},{4,5},{5,4},{6,7},{7,6},{8,9},{9,8},{10,11... | collective-permute-start | bytes 49160 | tf_op jit(solution)/shard_map/ppermute | solution.py:197
  43.9 3.2 %collective-permute-start.5 = (f32[16,256]{1,0:T(8,128)S(1)}, f32[16,256]{1,0:T(8,128)S(1)}, u32[]{:S(2)}, u32[]{:S(2)}) collective-permute-start(f32[16,256]{1,0:T(8,128)S(1)} %get-tuple-element.25.refs_0_), channel_id=1, source_target_pairs={{0,3},{1,2},{2,1},{3,0},{4,7},{5,6},{6,5},{7,4},{8,11},{9,10},{10,... | collective-permute-start | bytes 49160 | tf_op jit(solution)/shard_map/ppermute | solution.py:197
  44.0 3.8 %collective-permute-start.4 = (f32[16,256]{1,0:T(8,128)S(1)}, f32[16,256]{1,0:T(8,128)S(1)}, u32[]{:S(2)}, u32[]{:S(2)}) collective-permute-start(f32[16,256]{1,0:T(8,128)S(1)} %get-tuple-element.25.refs_0_), channel_id=1, source_target_pairs={{0,2},{1,3},{2,0},{3,1},{4,6},{5,7},{6,4},{7,5},{8,10},{9,11},{10,... | collective-permute-start | bytes 49160 | tf_op jit(solution)/shard_map/ppermute | solution.py:197
  45.2 2.6 %collective-permute-start.3 = (f32[16,256]{1,0:T(8,128)S(1)}, f32[16,256]{1,0:T(8,128)S(1)}, u32[]{:S(2)}, u32[]{:S(2)}) collective-permute-start(f32[16,256]{1,0:T(8,128)S(1)} %get-tuple-element.25.refs_0_), channel_id=1, source_target_pairs={{0,1},{1,0},{2,3},{3,2},{4,5},{5,4},{6,7},{7,6},{8,9},{9,8},{10,11... | collective-permute-start | bytes 49160 | tf_op jit(solution)/shard_map/ppermute | solution.py:197

commit v2 on v1

v2 whole, which is shorter than its diff:
```python
import jax
import jax.numpy as jnp
from jax import lax
from jax.experimental import pallas as pl
from jax.experimental.pallas import tpu as pltpu
from jax.sharding import PartitionSpec as P

ridge_weight = 0.5
LANES = 128
EXTRA = 8
VMEM_LIMIT = 16 << 20
F32 = jnp.float32
BF16 = jnp.bfloat16


def vmem():
    return pl.BlockSpec(memory_space=pltpu.VMEM)


def stay(x):
    return pltpu.with_memory_space_constraint(x, pltpu.HBM)


def call(body, name, out_shapes, args, in_specs=None, scratch=(), flops=0, moved=0):
    return pl.pallas_call(
        body,
        name=name,
        out_shape=[pltpu.VMEM(s, d) for s, d in out_shapes],
        in_specs=in_specs or [vmem()] * len(args),
        out_specs=[vmem()] * len(out_shapes),
        scratch_shapes=list(scratch),
        compiler_params=pltpu.CompilerParams(vmem_limit_bytes=VMEM_LIMIT),
        cost_estimate=pl.CostEstimate(flops=flops, bytes_accessed=moved, transcendentals=0),
    )(*args)


def split(x):
    high = x.astype(BF16).astype(F32)
    return jnp.concatenate([high, x - high], axis=0).astype(BF16)


def lane_sum(row):
    return jnp.sum(row, axis=1, keepdims=True)


def row_sum(x):
    return jnp.sum(x, axis=0, keepdims=True)


def pieces_of(x):
    return [x[:, h : h + LANES] for h in range(0, x.shape[1], LANES)]


def fold(row):
    return sum(pieces_of(row)[1:], pieces_of(row)[0])


def put(ref, first, x):
    for piece in pieces_of(x):
        ref[pl.ds(first, piece.shape[0]), 0, :] = piece
        first += piece.shape[0]


def take(x, rows, size):
    return jnp.concatenate([x[h * rows : (h + 1) * rows] for h in range(size // LANES)], axis=1)


def place(table, vector):
    return jnp.dot(table, split(vector), preferred_element_type=F32).astype(BF16)


def join(total):
    half = total.shape[0] // 2
    return total[:half] + total[half:]


def block_product(table, vector, high, low, slots, flip):
    placed = place(table, vector)
    step = placed.shape[0] // slots
    size = vector.shape[1]
    contract = (((1,), (1 if flip else 0,)), ((), ()))
    total = jnp.zeros((step, size), F32)
    rest = jnp.zeros((step, size), F32)
    for k in range(slots):
        left = placed[k * step : (k + 1) * step]
        here = slice(k * size, (k + 1) * size)
        total += lax.dot_general(left, high[here, :], contract, preferred_element_type=F32)
        rest += lax.dot_general(left, low[here, :], contract, preferred_element_type=F32)
    return join(total + rest)


def start_body(group, cols, slots, *refs):
    sources, (sent, to_cols, to_rows, own), held, sem = refs[:5], refs[5:9], refs[9:14], refs[14]
    copies = [pltpu.make_async_copy(a, b, sem.at[i]) for i, (a, b) in enumerate(zip(sources, held))]
    for copy in copies:
        copy.start()
    mine = lax.broadcasted_iota(jnp.int32, own.shape, 0) == lax.axis_index("col")
    own[...] = jnp.where(mine, 1.0, 0.0)
    for copy in copies:
        copy.wait()
    side, weights, count, rows_of, cols_of = held
    both = jnp.concatenate([side[...], weights[...]], axis=0)
    sent[...] = jnp.broadcast_to(both[None], sent.shape)

    def table(targets, sources, target, source, live):
        r = lax.broadcasted_iota(jnp.int32, (2 * targets, 2 * sources), 0)
        q = lax.broadcasted_iota(jnp.int32, (2 * targets, 2 * sources), 1)
        first = (r == target) & (q == source)
        second = (r == targets + target) & (q == sources + source)
        return jnp.where((first | second) & live, 1.0, 0.0).astype(BF16)

    for k in range(slots):
        live = k < count[0, 0]
        row, col = rows_of[0, 0, k], cols_of[0, 0, k]
        to_cols[pl.ds(k * 2 * cols, 2 * cols), :] = table(cols, group, col, row, live)
        to_rows[pl.ds(k * 2 * group, 2 * group), :] = table(group, cols, row, col, live)


def first_body(slots, cols, gathered, tiles, to_cols, out, high, low):
    residual, weights = gathered[:, 0, :], gathered[:, 1, :]
    z = weights * residual
    size = z.shape[1]
    placed = place(to_cols[...], z)
    step = 2 * cols
    total = jnp.zeros((step, size), F32)
    rest = jnp.zeros((step, size), F32)
    for k in range(slots):
        left = placed[k * step : (k + 1) * step]
        tile = tiles[0, 0, k]
        upper = tile.astype(BF16)
        lower = (tile - upper.astype(F32)).astype(BF16)
        high[pl.ds(k * size, size), :] = upper
        low[pl.ds(k * size, size), :] = lower
        total += jnp.dot(left, upper, preferred_element_type=F32)
        rest += jnp.dot(left, lower, preferred_element_type=F32)
    put(out, 0, join(total + rest))
    count = cols * (size // LANES)
    put(out, count, fold(row_sum(residual * z)))
    put(out, count + 1, fold(row_sum(z * z)))


def gather4(refs):
    a, b, c, d = [r[:, 0, :] for r in refs]
    return (a + b) + (c + d)


def second_body(slots, peers, p0, p1, p2, p3, scaling, high, low, to_rows, total, out):
    summed = gather4((p0, p1, p2, p3))
    total[...] = summed
    cols, size = scaling.shape
    lifted = take(summed, cols, size)
    weighted = scaling[...] * lifted
    inner = fold(row_sum(weighted * lifted))
    rows = block_product(to_rows[...], weighted, high, low, slots, True)
    length = out.shape[0] // peers
    for j in range(peers):
        put(out, j * length, rows)
        put(out, (j + 1) * length - 1, inner)


def third_body(slots, cols, arrived, gathered, total, high, low, to_cols, out, residual_out, alpha_out):
    residual, weights = gathered[:, 0, :], gathered[:, 1, :]
    z = weights * residual
    group, size = residual.shape
    length = group * (size // LANES) + 1
    peers = arrived.shape[0] // length
    summed = arrived[pl.ds(0, length), 0, :]
    for j in range(1, peers):
        summed += arrived[pl.ds(j * length, length), 0, :]
    image = take(summed, group, size) + ridge_weight * z
    count = cols * (size // LANES)
    gamma = lane_sum(total[pl.ds(count, 1), :])
    curve = lane_sum(summed[length - 1 : length] + ridge_weight * total[pl.ds(count + 1, 1), :])
    alpha = gamma / curve
    alpha_out[...] = jnp.broadcast_to(alpha, alpha_out.shape)
    later = residual - alpha * image
    residual_out[...] = later
    z1 = weights * later
    put(out, count, fold(row_sum(later * z1)))
    put(out, count + 1, fold(row_sum(z1 * z1)))
    put(out, count + 2, fold(row_sum(z1 * z)))
    put(out, 0, block_product(to_cols[...], z1, high, low, slots, False))


def fourth_body(slots, p0, p1, p2, p3, total, gathered, residual, scaling, high, low, to_rows, out, direction_out, scalars):
    summed = gather4((p0, p1, p2, p3))
    cols, size = scaling.shape
    count = cols * (size // LANES)
    gamma = lane_sum(total[pl.ds(count, 1), :])
    norm = lane_sum(total[pl.ds(count + 1, 1), :])
    later = lane_sum(summed[count : count + 1])
    beta = later / gamma
    square = lane_sum(summed[count + 1 : count + 2]) + beta * (2.0 * lane_sum(summed[count + 2 : count + 3]) + beta * norm)
    lifted = take(summed, cols, size) + beta * take(total[...], cols, size)
    weighted = scaling[...] * lifted
    inner = fold(row_sum(weighted * lifted))
    rows = block_product(to_rows[...], weighted, high, low, slots, True)
    peers = out.shape[0]
    for h, piece in enumerate(pieces_of(rows)):
        out[:, h, :] = piece
    out[:, size // LANES, :] = jnp.broadcast_to(inner, (peers, LANES))
    weights = gathered[:, 1, :]
    direction_out[...] = weights * residual[...] + beta * (weights * gathered[:, 0, :])
    scalars[pl.ds(0, 1), :] = jnp.broadcast_to(later, (1, LANES))
    scalars[pl.ds(1, 1), :] = jnp.broadcast_to(square, (1, LANES))


def last_body(arrived, gathered, residual, direction, alpha, scalars, own, solution, residual_out):
    size = solution.shape[1]
    mask = own[:, :1]
    summed = jnp.sum(arrived[...], axis=0)
    image = take(summed, 1, size)
    curve = lane_sum(summed[size // LANES : size // LANES + 1]) + ridge_weight * scalars[1:2, :1]
    step = scalars[0:1, :1] / curve
    first = row_sum(mask * (gathered[:, 0, :] * gathered[:, 1, :]))
    second = row_sum(mask * direction[...])
    before = row_sum(mask * residual[...])
    solution[...] = alpha[:1, :1] * first + step * second
    residual_out[...] = before - step * (image + ridge_weight * second)


def share(value, axis, size):
    moved = [value]
    for s in range(1, size):
        moved.append(lax.ppermute(value, axis, [(i, i ^ s) for i in range(size)]))
    return moved


def local(right_side, precond, scaling, blocks, block_count, block_rows, block_cols):
    peers = lax.axis_size("col")
    groups = lax.axis_size("row")
    slots, size = blocks.shape[2], blocks.shape[3]
    own_rows = right_side.shape[0]
    assert own_rows == 1 and groups == 4
    group = own_rows * peers
    cols = scaling.shape[0]
    pieces = size // LANES
    long = slots * size
    work = dict(flops=8 * long * size, moved=0)

    sent, to_cols, to_rows, own = call(
        lambda *refs: start_body(group, cols, slots, *refs),
        "start",
        [
            ((peers, 2, size), F32),
            ((slots * 2 * cols, 2 * group), BF16),
            ((slots * 2 * group, 2 * cols), BF16),
            ((group, LANES), F32),
        ],
        (stay(right_side), stay(precond), block_count, stay(block_rows), stay(block_cols)),
        in_specs=[pl.BlockSpec(memory_space=pl.ANY)] * 5,
        scratch=[
            pltpu.VMEM(right_side.shape, F32),
            pltpu.VMEM(precond.shape, F32),
            pltpu.SMEM(block_count.shape, jnp.int32),
            pltpu.SMEM(block_rows.shape, jnp.int32),
            pltpu.SMEM(block_cols.shape, jnp.int32),
            pltpu.SemaphoreType.DMA((5,)),
        ],
        moved=100 << 20,
    )
    held_blocks = lax.ppermute(blocks, "col", [(i, i) for i in range(peers)])
    gathered = lax.all_to_all(sent, "col", 0, 0, tiled=True)
    mine, high, low = call(
        lambda *refs: first_body(slots, cols, *refs),
        "first",
        [((cols * pieces + 2, 1, LANES), F32), ((long, size), BF16), ((long, size), BF16)],
        (gathered, held_blocks, to_cols),
        **work,
    )
    length = group * pieces + 1
    total, sent = call(
        lambda *refs: second_body(slots, peers, *refs),
        "second",
        [((cols * pieces + 2, LANES), F32), ((peers * length, 1, LANES), F32)],
        (*share(mine, "row", groups), scaling, high, low, to_rows),
        **work,
    )
    arrived = lax.all_to_all(sent, "col", 0, 0, tiled=True)
    mine, residual, alpha = call(
        lambda *refs: third_body(slots, cols, *refs),
        "third",
        [((cols * pieces + 3, 1, LANES), F32), ((group, size), F32), ((1, LANES), F32)],
        (arrived, gathered, total, high, low, to_cols),
        **work,
    )
    sent, direction, scalars = call(
        lambda *refs: fourth_body(slots, *refs),
        "fourth",
        [((peers, pieces + 1, LANES), F32), ((group, size), F32), ((2, LANES), F32)],
        (*share(mine, "row", groups), total, gathered, residual, scaling, high, low, to_rows),
        **work,
    )
    arrived = lax.all_to_all(sent, "col", 0, 0, tiled=True)
    return pl.pallas_call(
        last_body,
        name="last",
        out_shape=[jax.ShapeDtypeStruct(right_side.shape, F32)] * 2,
        in_specs=[vmem()] * 7,
        out_specs=[vmem()] * 2,
        compiler_params=pltpu.CompilerParams(vmem_limit_bytes=VMEM_LIMIT),
    )(arrived, gathered, residual, direction, alpha, scalars, own)


def solution(mesh):
    placed = (
        P(("row", "col"), None),
        P(("row", "col"), None),
        P("col", None),
        P("col", "row", None, None, None),
        P("col", "row"),
        P("col", "row", None),
        P("col", "row", None),
    )
    return jax.shard_map(
        local,
        mesh=mesh,
        in_specs=placed,
        out_specs=(P(("row", "col"), None), P(("row", "col"), None)),
        check_vma=False,
    )
```

time: 59 us -> 49.9 us (0.85)
  local copies, waits for them, and re-layouts: 11.3 us -> 0.01 us
  blocking collectives: 21.9 us -> 31.9 us
  starting transfers between devices: 11.1 us -> 6.03 us
  Pallas kernels: 7.71 us -> 6.51 us
  waiting for transfers between devices: 4.61 us -> 3.77 us
  other arithmetic: 0.7 us -> 0 us
    all_to_all x0 -> x1, blocking collectives: none -> 13.7 us  [local(): gathered = lax.all_to_all(sent, 'col', 0, 0, tiled=True)]
    unnamed x20 -> x2, local copies, waits for them, and re-layouts: 10.7 us -> 0.01 us
    all_to_all x1 -> x0, starting transfers between devices: 7.31 us -> none  [local(): lax.all_to_all(jnp.broadcast_to(both, (peers, 2, size)), 'col', 0, 0, til...]
    all_to_all x2, blocking collectives: 21.9 us -> 18.3 us  [local(): arrived = lax.all_to_all(sent, 'col', 0, 0, tiled=True)]
    ppermute x0 -> x1, starting transfers between devices: none -> 2.2 us  [local(): held_blocks = lax.ppermute(blocks, 'col', [(i, i) for i in range(peers)])]
    pallas_call x5, Pallas kernels: 6.97 us -> 5.77 us  [call(): pl.pallas_call(body, name=name, out_shape=[pltpu.VMEM(s, d) for s, d in o...]
    ppermute x6, waiting for transfers between devices: 4.61 us -> 3.77 us  [share(): moved.append(lax.ppermute(value, axis, [(i, i ^ s) for i in range(size)]))]
    broadcast_in_dim x1 -> x0, other arithmetic: 0.7 us -> none  [local(): jnp.broadcast_to(both, (peers, 2, size))]
  transfers between devices with their start and end apart: 7 -> 7, of which waited for: 4 -> 4; matrix products, arithmetic and copies ran while one was open for 0% -> 0% of each run, Pallas kernels for 6% -> 2%
where the time goes in v2:
time: 49.9 us; the launch traced here: 49.6 us
  blocking collectives  31.9 us (64%)
  Pallas kernels  6.51 us (13%)
  starting transfers between devices  6.03 us (12%)
  waiting for transfers between devices  3.77 us (8%)
  between operations  1.35 us (3%)
    all_to_all x2, blocking collectives, local(): arrived = lax.all_to_all(sent, 'col', 0, 0, tiled=True)  18.3 us
    all_to_all x1, blocking collectives, local(): gathered = lax.all_to_all(sent, 'col', 0, 0, tiled=True)  13.7 us
    pallas_call x5, Pallas kernels, call(): pl.pallas_call(body, name=name, out_shape=[pltpu.VMEM(s, d) for s, d in o...  5.77 us
    ppermute x6, starting transfers between devices, share(): moved.append(lax.ppermute(value, axis, [(i, i ^ s) for i in range(size)]))  3.84 us
    ppermute x6, waiting for transfers between devices, share(): moved.append(lax.ppermute(value, axis, [(i, i ^ s) for i in range(size)]))  3.77 us
    ppermute x1, starting transfers between devices, local(): held_blocks = lax.ppermute(blocks, 'col', [(i, i) for i in range(peers)])  2.2 us
  transfers between devices with their start and end apart: 7, of which 4 were waited for; matrix products, arithmetic and copies ran while one was open for 0% of the time, Pallas kernels for 2%

profile of v2, /device:TPU:0, one launch (start us, length us, event | category | flops | bytes accessed | tf_op | source)
XLA Modules:
  0.0 49.6 jit_solution(10370282403869462926)
XLA Ops:
  0.6 0.0 copy-start
  0.6 2.2 %collective-permute-start = (f32[1,1,16,256,256]{4,3,2,1,0:T(8,128)}, f32[1,1,16,256,256]{4,3,2,1,0:T(8,128)S(1)}, u32[]{:S(2)}, u32[]{:S(2)}) collective-permute-start(f32[1,1,16,256,256]{4,3,2,1,0:T(8,128)} %param.10), channel_id=1, source_target_pairs={{0,0},{4,4},{8,8},{12,12},{16,16},{20,20},{24,24},{28,28},{1,1},{5... | collective-permute-start | bytes 12582920 | tf_op jit(solution)/shard_map/ppermute | solution.py:262
  3.5 1.0 %start.1 = (f32[8,2,256]{2,1,0:T(2,128)S(1)}, bf16[256,16]{1,0:T(8,128)(2,1)S(1)}, bf16[256,16]{1,0:T(8,128)(2,1)S(1)}, f32[8,128]{1,0:T(8,128)S(1)}) custom-call(f32[1,256]{1,0:T(1,128)} %refs_0_.1, f32[1,256]{1,0:T(1,128)} %refs_1_.1, s32[1,1]{1,0:T(1,128)S(6)} %copy.9.refs_2_, s32[1,1,16]{2,1,0:T(1,128)} %refs_3_.1, s32[1,1,16]{2,1,0:T(1,128)} %refs_4_.2), custom_call_target="tpu_custom_call" | custom-call | bytes 104857600 | tf_op jit(solution)/shard_map/start/pallas_call | solution.py:25
  4.5 13.7 %all_to_all.15.refs_0_.refs_1_.refs_5_.gathered = f32[8,2,256]{2,1,0:T(2,128)S(1)} all-to-all(f32[8,2,256]{2,1,0:T(2,128)S(1)} %get-tuple-element.17), channel_id=1, replica_groups=mesh['col'=8,'row'=4] {'col'}, dimensions={0} | all-to-all | bytes 32768 | tf_op jit(solution)/shard_map/all_to_all | solution.py:263
  18.1 0.0 collective-permute-done.refs_1_
  18.2 1.2 %first.1 = (f32[18,1,128]{2,1,0:T(1,128)S(1)}, bf16[4096,256]{1,0:T(8,128)(2,1)S(1)}, bf16[4096,256]{1,0:T(8,128)(2,1)S(1)}) custom-call(f32[8,2,256]{2,1,0:T(2,128)S(1)} %all_to_all.15.refs_0_.refs_1_.refs_5_.gathered, f32[1,1,16,256,256]{4,3,2,1,0:T(8,128)S(1)} %collective-permute-done.refs_1_, bf16[256,16]{1,0:T(8,128)(2,1)S(1)} %get-tuple-element.18.refs_2_.refs_5_), custom_call_target="tpu_custom_call" | custom-call | flops 8388608 | tf_op jit(solution)/shard_map/first/pallas_call | solution.py:25
  19.3 0.1 collective-permute-start.3
  19.4 1.6 %collective-permute-start.2 = (f32[18,1,128]{2,1,0:T(1,128)S(1)}, f32[18,1,128]{2,1,0:T(1,128)S(1)}, u32[]{:S(2)}, u32[]{:S(2)}) collective-permute-start(f32[18,1,128]{2,1,0:T(1,128)S(1)} %get-tuple-element.19.refs_0_), channel_id=1, source_target_pairs={{0,2},{1,3},{2,0},{3,1},{4,6},{5,7},{6,4},{7,5},{8,10},{9,11},{10,... | collective-permute-start | bytes 27656 | tf_op jit(solution)/shard_map/ppermute | solution.py:225
  21.0 0.3 collective-permute-start.1
  21.2 1.3 %collective-permute-done.3.refs_3_ = f32[18,1,128]{2,1,0:T(1,128)S(1)} collective-permute-done((f32[18,1,128]{2,1,0:T(1,128)S(1)}, f32[18,1,128]{2,1,0:T(1,128)S(1)}, u32[]{:S(2)}, u32[]{:S(2)}) %collective-permute-start.3) | collective-permute-done | bytes 9248 | tf_op jit(solution)/shard_map/ppermute | solution.py:225
  22.5 0.6 %collective-permute-done.2.refs_2_ = f32[18,1,128]{2,1,0:T(1,128)S(1)} collective-permute-done((f32[18,1,128]{2,1,0:T(1,128)S(1)}, f32[18,1,128]{2,1,0:T(1,128)S(1)}, u32[]{:S(2)}, u32[]{:S(2)}) %collective-permute-start.2) | collective-permute-done | bytes 9248 | tf_op jit(solution)/shard_map/ppermute | solution.py:225
  23.1 0.0 collective-permute-done.1.refs_1_
  23.1 0.0 copy-done
  23.1 1.3 %second.1 = (f32[18,128]{1,0:T(8,128)S(1)}, f32[136,1,128]{2,1,0:T(1,128)S(1)}) custom-call(f32[18,1,128]{2,1,0:T(1,128)S(1)} %get-tuple-element.19.refs_0_, f32[18,1,128]{2,1,0:T(1,128)S(1)} %collective-permute-done.1.refs_1_, f32[18,1,128]{2,1,0:T(1,128)S(1)} %collective-permute-done.2.refs_2_, f32[18,1,128]{2,1,0:T(1,128)S(1)} %collective-permute-done.3.refs_3_, ...), custom_call_target="tpu_custom_call" | custom-call | flops 8388608 | tf_op jit(solution)/shard_map/second/pallas_call | solution.py:25
  24.5 9.3 %all_to_all.16.refs_0_ = f32[136,1,128]{2,1,0:T(1,128)S(1)} all-to-all(f32[136,1,128]{2,1,0:T(1,128)S(1)} %get-tuple-element.23), channel_id=1, replica_groups=mesh['col'=8,'row'=4] {'col'}, dimensions={0} | all-to-all | bytes 139264 | tf_op jit(solution)/shard_map/all_to_all | solution.py:279
  33.8 0.9 %third.1 = (f32[19,1,128]{2,1,0:T(1,128)S(1)}, f32[8,256]{1,0:T(8,128)S(1)}, f32[1,128]{1,0:T(1,128)S(1)}) custom-call(f32[136,1,128]{2,1,0:T(1,128)S(1)} %all_to_all.16.refs_0_, f32[8,2,256]{2,1,0:T(2,128)S(1)} %all_to_all.15.refs_0_.refs_1_.refs_5_.gathered, f32[18,128]{1,0:T(8,128)S(1)} %get-tuple-element.24.refs_2_.refs_4_, ...), custom_call_target="tpu_custom_call" | custom-call | flops 8388608 | tf_op jit(solution)/shard_map/third/pallas_call | solution.py:25
  34.7 0.1 collective-permute-start.6
  34.8 1.6 %collective-permute-start.5 = (f32[19,1,128]{2,1,0:T(1,128)S(1)}, f32[19,1,128]{2,1,0:T(1,128)S(1)}, u32[]{:S(2)}, u32[]{:S(2)}) collective-permute-start(f32[19,1,128]{2,1,0:T(1,128)S(1)} %get-tuple-element.25.refs_0_), channel_id=1, source_target_pairs={{0,2},{1,3},{2,0},{3,1},{4,6},{5,7},{6,4},{7,5},{8,10},{9,11},{10,... | collective-permute-start | bytes 29192 | tf_op jit(solution)/shard_map/ppermute | solution.py:225
  36.4 0.3 collective-permute-start.4
  36.7 1.3 %collective-permute-done.6.refs_3_ = f32[19,1,128]{2,1,0:T(1,128)S(1)} collective-permute-done((f32[19,1,128]{2,1,0:T(1,128)S(1)}, f32[19,1,128]{2,1,0:T(1,128)S(1)}, u32[]{:S(2)}, u32[]{:S(2)}) %collective-permute-start.6) | collective-permute-done | bytes 9760 | tf_op jit(solution)/shard_map/ppermute | solution.py:225
  37.9 0.6 %collective-permute-done.5.refs_2_ = f32[19,1,128]{2,1,0:T(1,128)S(1)} collective-permute-done((f32[19,1,128]{2,1,0:T(1,128)S(1)}, f32[19,1,128]{2,1,0:T(1,128)S(1)}, u32[]{:S(2)}, u32[]{:S(2)}) %collective-permute-start.5) | collective-permute-done | bytes 9760 | tf_op jit(solution)/shard_map/ppermute | solution.py:225
  38.5 0.0 collective-permute-done.4.refs_1_
  38.5 1.4 %fourth.1 = (f32[8,3,128]{2,1,0:T(4,128)S(1)}, f32[8,256]{1,0:T(8,128)S(1)}, f32[2,128]{1,0:T(2,128)S(1)}) custom-call(f32[19,1,128]{2,1,0:T(1,128)S(1)} %get-tuple-element.25.refs_0_, f32[19,1,128]{2,1,0:T(1,128)S(1)} %collective-permute-done.4.refs_1_, f32[19,1,128]{2,1,0:T(1,128)S(1)} %collective-permute-done.5.refs_2_, ...), custom_call_target="tpu_custom_call" | custom-call | flops 8388608 | tf_op jit(solution)/shard_map/fourth/pallas_call | solution.py:25
  39.9 8.9 %all_to_all.17.arrived = f32[8,3,128]{2,1,0:T(4,128)S(1)} all-to-all(f32[8,3,128]{2,1,0:T(4,128)S(1)} %get-tuple-element.27), channel_id=1, replica_groups=mesh['col'=8,'row'=4] {'col'}, dimensions={0} | all-to-all | bytes 24576 | tf_op jit(solution)/shard_map/all_to_all | solution.py:294
  48.9 0.7 %last.1 = (f32[1,256]{1,0:T(1,128)}, f32[1,256]{1,0:T(1,128)}) custom-call(f32[8,3,128]{2,1,0:T(4,128)S(1)} %all_to_all.17.arrived, f32[8,2,256]{2,1,0:T(2,128)S(1)} %all_to_all.15.refs_0_.refs_1_.refs_5_.gathered, f32[8,256]{1,0:T(8,128)S(1)} %get-tuple-element.26.refs_6_.residual, f32[8,256]{1,0:T(8,128)S(1)} %get-tuple-element.28.direction, ...), custom_call_target="tpu_custom_call" | custom-call | tf_op jit(solution)/shard_map/last/pallas_call | solution.py:295
Async XLA Ops:
  0.6 22.5 %copy-start = (f32[8,256]{1,0:T(8,128)S(1)}, f32[8,256]{1,0:T(8,128)}, u32[]{:S(2)}) copy-start(f32[8,256]{1,0:T(8,128)} %refs_7_.1) | copy-start | bytes 24580
  0.6 17.5 %collective-permute-start = (f32[1,1,16,256,256]{4,3,2,1,0:T(8,128)}, f32[1,1,16,256,256]{4,3,2,1,0:T(8,128)S(1)}, u32[]{:S(2)}, u32[]{:S(2)}) collective-permute-start(f32[1,1,16,256,256]{4,3,2,1,0:T(8,128)} %param.10), channel_id=1, source_target_pairs={{0,0},{4,4},{8,8},{12,12},{16,16},{20,20},{24,24},{28,28},{1,1},{5... | collective-permute-start | bytes 12582920 | tf_op jit(solution)/shard_map/ppermute | solution.py:262
  19.3 3.2 %collective-permute-start.3 = (f32[18,1,128]{2,1,0:T(1,128)S(1)}, f32[18,1,128]{2,1,0:T(1,128)S(1)}, u32[]{:S(2)}, u32[]{:S(2)}) collective-permute-start(f32[18,1,128]{2,1,0:T(1,128)S(1)} %get-tuple-element.19.refs_0_), channel_id=1, source_target_pairs={{0,3},{1,2},{2,1},{3,0},{4,7},{5,6},{6,5},{7,4},{8,11},{9,10},{10,... | collective-permute-start | bytes 27656 | tf_op jit(solution)/shard_map/ppermute | solution.py:225
  19.4 3.7 %collective-permute-start.2 = (f32[18,1,128]{2,1,0:T(1,128)S(1)}, f32[18,1,128]{2,1,0:T(1,128)S(1)}, u32[]{:S(2)}, u32[]{:S(2)}) collective-permute-start(f32[18,1,128]{2,1,0:T(1,128)S(1)} %get-tuple-element.19.refs_0_), channel_id=1, source_target_pairs={{0,2},{1,3},{2,0},{3,1},{4,6},{5,7},{6,4},{7,5},{8,10},{9,11},{10,... | collective-permute-start | bytes 27656 | tf_op jit(solution)/shard_map/ppermute | solution.py:225
  21.0 2.2 %collective-permute-start.1 = (f32[18,1,128]{2,1,0:T(1,128)S(1)}, f32[18,1,128]{2,1,0:T(1,128)S(1)}, u32[]{:S(2)}, u32[]{:S(2)}) collective-permute-start(f32[18,1,128]{2,1,0:T(1,128)S(1)} %get-tuple-element.19.refs_0_), channel_id=1, source_target_pairs={{0,1},{1,0},{2,3},{3,2},{4,5},{5,4},{6,7},{7,6},{8,9},{9,8},{10,11... | collective-permute-start | bytes 27656 | tf_op jit(solution)/shard_map/ppermute | solution.py:225
  34.7 3.2 %collective-permute-start.6 = (f32[19,1,128]{2,1,0:T(1,128)S(1)}, f32[19,1,128]{2,1,0:T(1,128)S(1)}, u32[]{:S(2)}, u32[]{:S(2)}) collective-permute-start(f32[19,1,128]{2,1,0:T(1,128)S(1)} %get-tuple-element.25.refs_0_), channel_id=1, source_target_pairs={{0,3},{1,2},{2,1},{3,0},{4,7},{5,6},{6,5},{7,4},{8,11},{9,10},{10,... | collective-permute-start | bytes 29192 | tf_op jit(solution)/shard_map/ppermute | solution.py:225
  34.8 3.7 %collective-permute-start.5 = (f32[19,1,128]{2,1,0:T(1,128)S(1)}, f32[19,1,128]{2,1,0:T(1,128)S(1)}, u32[]{:S(2)}, u32[]{:S(2)}) collective-permute-start(f32[19,1,128]{2,1,0:T(1,128)S(1)} %get-tuple-element.25.refs_0_), channel_id=1, source_target_pairs={{0,2},{1,3},{2,0},{3,1},{4,6},{5,7},{6,4},{7,5},{8,10},{9,11},{10,... | collective-permute-start | bytes 29192 | tf_op jit(solution)/shard_map/ppermute | solution.py:225
  36.4 2.2 %collective-permute-start.4 = (f32[19,1,128]{2,1,0:T(1,128)S(1)}, f32[19,1,128]{2,1,0:T(1,128)S(1)}, u32[]{:S(2)}, u32[]{:S(2)}) collective-permute-start(f32[19,1,128]{2,1,0:T(1,128)S(1)} %get-tuple-element.25.refs_0_), channel_id=1, source_target_pairs={{0,1},{1,0},{2,3},{3,2},{4,5},{5,4},{6,7},{7,6},{8,9},{9,8},{10,11... | collective-permute-start | bytes 29192 | tf_op jit(solution)/shard_map/ppermute | solution.py:225

commit v3 on v2

--- a/solution.py
+++ b/solution.py
@@ -116,7 +116,7 @@
         to_rows[pl.ds(k * 2 * group, 2 * group), :] = table(group, cols, row, col, live)
 
 
-def first_body(slots, cols, gathered, tiles, to_cols, out, high, low):
+def first_body(slots, cols, gathered, tiles, to_cols, out, high, low, high_t, low_t):
     residual, weights = gathered[:, 0, :], gathered[:, 1, :]
     z = weights * residual
     size = z.shape[1]
@@ -131,6 +131,8 @@
         lower = (tile - upper.astype(F32)).astype(BF16)
         high[pl.ds(k * size, size), :] = upper
         low[pl.ds(k * size, size), :] = lower
+        high_t[pl.ds(k * size, size), :] = upper.T
+        low_t[pl.ds(k * size, size), :] = lower.T
         total += jnp.dot(left, upper, preferred_element_type=F32)
         rest += jnp.dot(left, lower, preferred_element_type=F32)
     put(out, 0, join(total + rest))
@@ -151,7 +153,7 @@
     lifted = take(summed, cols, size)
     weighted = scaling[...] * lifted
     inner = fold(row_sum(weighted * lifted))
-    rows = block_product(to_rows[...], weighted, high, low, slots, True)
+    rows = block_product(to_rows[...], weighted, high, low, slots, False)
     length = out.shape[0] // peers
     for j in range(peers):
         put(out, j * length, rows)
@@ -194,7 +196,7 @@
     lifted = take(summed, cols, size) + beta * take(total[...], cols, size)
     weighted = scaling[...] * lifted
     inner = fold(row_sum(weighted * lifted))
-    rows = block_product(to_rows[...], weighted, high, low, slots, True)
+    rows = block_product(to_rows[...], weighted, high, low, slots, False)
     peers = out.shape[0]
     for h, piece in enumerate(pieces_of(rows)):
         out[:, h, :] = piece
@@ -257,15 +259,15 @@
             pltpu.SMEM(block_cols.shape, jnp.int32),
             pltpu.SemaphoreType.DMA((5,)),
         ],
+        flops=1 << 34,
         moved=100 << 20,
     )
-    held_blocks = lax.ppermute(blocks, "col", [(i, i) for i in range(peers)])
     gathered = lax.all_to_all(sent, "col", 0, 0, tiled=True)
-    mine, high, low = call(
+    mine, high, low, high_t, low_t = call(
         lambda *refs: first_body(slots, cols, *refs),
         "first",
-        [((cols * pieces + 2, 1, LANES), F32), ((long, size), BF16), ((long, size), BF16)],
-        (gathered, held_blocks, to_cols),
+        [((cols * pieces + 2, 1, LANES), F32)] + [((long, size), BF16)] * 4,
+        (gathered, blocks, to_cols),
         **work,
     )
     length = group * pieces + 1
@@ -273,7 +275,7 @@
         lambda *refs: second_body(slots, peers, *refs),
         "second",
         [((cols * pieces + 2, LANES), F32), ((peers * length, 1, LANES), F32)],
-        (*share(mine, "row", groups), scaling, high, low, to_rows),
+        (*share(mine, "row", groups), scaling, high_t, low_t, to_rows),
         **work,
     )
     arrived = lax.all_to_all(sent, "col", 0, 0, tiled=True)
@@ -288,7 +290,7 @@
         lambda *refs: fourth_body(slots, *refs),
         "fourth",
         [((peers, pieces + 1, LANES), F32), ((group, size), F32), ((2, LANES), F32)],
-        (*share(mine, "row", groups), total, gathered, residual, scaling, high, low, to_rows),
+        (*share(mine, "row", groups), total, gathered, residual, scaling, high_t, low_t, to_rows),
         **work,
     )
     arrived = lax.all_to_all(sent, "col", 0, 0, tiled=True)

time: 49.9 us -> 47.2 us (0.946)
  starting transfers between devices: 6.03 us -> 3.84 us
  Pallas kernels: 6.51 us -> 5.92 us
    ppermute x1 -> x0, starting transfers between devices: 2.2 us -> none  [local(): held_blocks = lax.ppermute(blocks, 'col', [(i, i) for i in range(peers)])]
    pallas_call x5, Pallas kernels: 5.77 us -> 5.18 us  [call(): pl.pallas_call(body, name=name, out_shape=[pltpu.VMEM(s, d) for s, d in o...]
  transfers between devices with their start and end apart: 7 -> 6, of which waited for: 4 -> 4; matrix products, arithmetic and copies ran while one was open for 0% -> 0% of each run, Pallas kernels for 2% -> 0%
where the time goes in v3:
time: 47.2 us; the launch traced here: 47 us
  blocking collectives  32.1 us (68%)
  Pallas kernels  5.92 us (13%)
  starting transfers between devices  3.84 us (8%)
  waiting for transfers between devices  3.77 us (8%)
  between operations  1.35 us (3%)
    all_to_all x2, blocking collectives, local(): arrived = lax.all_to_all(sent, 'col', 0, 0, tiled=True)  18.3 us
    all_to_all x1, blocking collectives, local(): gathered = lax.all_to_all(sent, 'col', 0, 0, tiled=True)  13.8 us
    pallas_call x5, Pallas kernels, call(): pl.pallas_call(body, name=name, out_shape=[pltpu.VMEM(s, d) for s, d in o...  5.18 us
    ppermute x6, starting transfers between devices, share(): moved.append(lax.ppermute(value, axis, [(i, i ^ s) for i in range(size)]))  3.84 us
    ppermute x6, waiting for transfers between devices, share(): moved.append(lax.ppermute(value, axis, [(i, i ^ s) for i in range(size)]))  3.77 us
  transfers between devices with their start and end apart: 6, of which 4 were waited for; matrix products, arithmetic and copies ran while one was open for 0% of the time, Pallas kernels for 0%

profile of v3, /device:TPU:0, one launch (start us, length us, event | category | flops | bytes accessed | tf_op | source)
XLA Modules:
  0.0 47.0 jit_solution(5073764545160046730)
XLA Ops:
  1.3 0.0 copy-start
  1.3 1.0 %start.1 = (f32[8,2,256]{2,1,0:T(2,128)S(1)}, bf16[256,16]{1,0:T(8,128)(2,1)S(1)}, bf16[256,16]{1,0:T(8,128)(2,1)S(1)}, f32[8,128]{1,0:T(8,128)S(1)}) custom-call(f32[1,256]{1,0:T(1,128)} %refs_0_.1, f32[1,256]{1,0:T(1,128)} %refs_1_.2, s32[1,1]{1,0:T(1,128)S(6)} %copy.9.refs_2_, s32[1,1,16]{2,1,0:T(1,128)} %refs_3_.1, s32[1,1,16]{2,1,0:T(1,128)} %refs_4_.2), custom_call_target="tpu_custom_call" | custom-call | flops 17179869184 | bytes 104857600 | tf_op jit(solution)/shard_map/start/pallas_call | solution.py:25
  2.3 13.8 %all_to_all.15.refs_0_.refs_1_.refs_5_.gathered = f32[8,2,256]{2,1,0:T(2,128)S(1)} all-to-all(f32[8,2,256]{2,1,0:T(2,128)S(1)} %get-tuple-element.19), channel_id=1, replica_groups=mesh['col'=8,'row'=4] {'col'}, dimensions={0} | all-to-all | bytes 32768 | tf_op jit(solution)/shard_map/all_to_all | solution.py:265
  16.1 0.0 copy-done
  16.1 0.0 copy-start.1
  16.1 1.5 %first.1 = (f32[18,1,128]{2,1,0:T(1,128)S(1)}, bf16[4096,256]{1,0:T(8,128)(2,1)S(1)}, bf16[4096,256]{1,0:T(8,128)(2,1)S(1)}, bf16[4096,256]{1,0:T(8,128)(2,1)S(1)}, bf16[4096,256]{1,0:T(8,128)(2,1)S(1)}) custom-call(f32[8,2,256]{2,1,0:T(2,128)S(1)} %all_to_all.15.refs_0_.refs_1_.refs_5_.gathered, f32[1,1,16,256,256]{4,3,2,1,0:T(8,128)S(1)} %copy-done, ...), custom_call_target="tpu_custom_call" | custom-call | flops 8388608 | tf_op jit(solution)/shard_map/first/pallas_call | solution.py:25
  17.6 0.1 collective-permute-start.2
  17.7 1.6 %collective-permute-start.1 = (f32[18,1,128]{2,1,0:T(1,128)S(1)}, f32[18,1,128]{2,1,0:T(1,128)S(1)}, u32[]{:S(2)}, u32[]{:S(2)}) collective-permute-start(f32[18,1,128]{2,1,0:T(1,128)S(1)} %get-tuple-element.21.refs_0_), channel_id=1, source_target_pairs={{0,2},{1,3},{2,0},{3,1},{4,6},{5,7},{6,4},{7,5},{8,10},{9,11},{10,... | collective-permute-start | bytes 27656 | tf_op jit(solution)/shard_map/ppermute | solution.py:227
  19.3 0.3 collective-permute-start
  19.5 1.3 %collective-permute-done.2.refs_3_ = f32[18,1,128]{2,1,0:T(1,128)S(1)} collective-permute-done((f32[18,1,128]{2,1,0:T(1,128)S(1)}, f32[18,1,128]{2,1,0:T(1,128)S(1)}, u32[]{:S(2)}, u32[]{:S(2)}) %collective-permute-start.2) | collective-permute-done | bytes 9248 | tf_op jit(solution)/shard_map/ppermute | solution.py:227
  20.8 0.6 %collective-permute-done.1.refs_2_ = f32[18,1,128]{2,1,0:T(1,128)S(1)} collective-permute-done((f32[18,1,128]{2,1,0:T(1,128)S(1)}, f32[18,1,128]{2,1,0:T(1,128)S(1)}, u32[]{:S(2)}, u32[]{:S(2)}) %collective-permute-start.1) | collective-permute-done | bytes 9248 | tf_op jit(solution)/shard_map/ppermute | solution.py:227
  21.4 0.0 collective-permute-done.refs_1_
  21.4 0.0 copy-done.1
  21.4 0.9 %second.1 = (f32[18,128]{1,0:T(8,128)S(1)}, f32[136,1,128]{2,1,0:T(1,128)S(1)}) custom-call(f32[18,1,128]{2,1,0:T(1,128)S(1)} %get-tuple-element.21.refs_0_, f32[18,1,128]{2,1,0:T(1,128)S(1)} %collective-permute-done.refs_1_, f32[18,1,128]{2,1,0:T(1,128)S(1)} %collective-permute-done.1.refs_2_, f32[18,1,128]{2,1,0:T(1,128)S(1)} %collective-permute-done.2.refs_3_, ...), custom_call_target="tpu_custom_call" | custom-call | flops 8388608 | tf_op jit(solution)/shard_map/second/pallas_call | solution.py:25
  22.3 9.3 %all_to_all.16.refs_0_ = f32[136,1,128]{2,1,0:T(1,128)S(1)} all-to-all(f32[136,1,128]{2,1,0:T(1,128)S(1)} %get-tuple-element.25), channel_id=1, replica_groups=mesh['col'=8,'row'=4] {'col'}, dimensions={0} | all-to-all | bytes 139264 | tf_op jit(solution)/shard_map/all_to_all | solution.py:281
  31.6 0.9 %third.1 = (f32[19,1,128]{2,1,0:T(1,128)S(1)}, f32[8,256]{1,0:T(8,128)S(1)}, f32[1,128]{1,0:T(1,128)S(1)}) custom-call(f32[136,1,128]{2,1,0:T(1,128)S(1)} %all_to_all.16.refs_0_, f32[8,2,256]{2,1,0:T(2,128)S(1)} %all_to_all.15.refs_0_.refs_1_.refs_5_.gathered, f32[18,128]{1,0:T(8,128)S(1)} %get-tuple-element.26.refs_2_.refs_4_, ...), custom_call_target="tpu_custom_call" | custom-call | flops 8388608 | tf_op jit(solution)/shard_map/third/pallas_call | solution.py:25
  32.5 0.1 collective-permute-start.5
  32.6 1.6 %collective-permute-start.4 = (f32[19,1,128]{2,1,0:T(1,128)S(1)}, f32[19,1,128]{2,1,0:T(1,128)S(1)}, u32[]{:S(2)}, u32[]{:S(2)}) collective-permute-start(f32[19,1,128]{2,1,0:T(1,128)S(1)} %get-tuple-element.29.refs_0_), channel_id=1, source_target_pairs={{0,2},{1,3},{2,0},{3,1},{4,6},{5,7},{6,4},{7,5},{8,10},{9,11},{10,... | collective-permute-start | bytes 29192 | tf_op jit(solution)/shard_map/ppermute | solution.py:227
  34.2 0.3 collective-permute-start.3
  34.5 1.3 %collective-permute-done.5.refs_3_ = f32[19,1,128]{2,1,0:T(1,128)S(1)} collective-permute-done((f32[19,1,128]{2,1,0:T(1,128)S(1)}, f32[19,1,128]{2,1,0:T(1,128)S(1)}, u32[]{:S(2)}, u32[]{:S(2)}) %collective-permute-start.5) | collective-permute-done | bytes 9760 | tf_op jit(solution)/shard_map/ppermute | solution.py:227
  35.8 0.6 %collective-permute-done.4.refs_2_ = f32[19,1,128]{2,1,0:T(1,128)S(1)} collective-permute-done((f32[19,1,128]{2,1,0:T(1,128)S(1)}, f32[19,1,128]{2,1,0:T(1,128)S(1)}, u32[]{:S(2)}, u32[]{:S(2)}) %collective-permute-start.4) | collective-permute-done | bytes 9760 | tf_op jit(solution)/shard_map/ppermute | solution.py:227
  36.4 0.0 collective-permute-done.3.refs_1_
  36.4 0.9 %fourth.1 = (f32[8,3,128]{2,1,0:T(4,128)S(1)}, f32[8,256]{1,0:T(8,128)S(1)}, f32[2,128]{1,0:T(2,128)S(1)}) custom-call(f32[19,1,128]{2,1,0:T(1,128)S(1)} %get-tuple-element.29.refs_0_, f32[19,1,128]{2,1,0:T(1,128)S(1)} %collective-permute-done.3.refs_1_, f32[19,1,128]{2,1,0:T(1,128)S(1)} %collective-permute-done.4.refs_2_, ...), custom_call_target="tpu_custom_call" | custom-call | flops 8388608 | tf_op jit(solution)/shard_map/fourth/pallas_call | solution.py:25
  37.3 8.9 %all_to_all.17.arrived = f32[8,3,128]{2,1,0:T(4,128)S(1)} all-to-all(f32[8,3,128]{2,1,0:T(4,128)S(1)} %get-tuple-element.31), channel_id=1, replica_groups=mesh['col'=8,'row'=4] {'col'}, dimensions={0} | all-to-all | bytes 24576 | tf_op jit(solution)/shard_map/all_to_all | solution.py:296
  46.2 0.7 %last.1 = (f32[1,256]{1,0:T(1,128)}, f32[1,256]{1,0:T(1,128)}) custom-call(f32[8,3,128]{2,1,0:T(4,128)S(1)} %all_to_all.17.arrived, f32[8,2,256]{2,1,0:T(2,128)S(1)} %all_to_all.15.refs_0_.refs_1_.refs_5_.gathered, f32[8,256]{1,0:T(8,128)S(1)} %get-tuple-element.30.refs_6_.residual, f32[8,256]{1,0:T(8,128)S(1)} %get-tuple-element.32.direction, ...), custom_call_target="tpu_custom_call" | custom-call | tf_op jit(solution)/shard_map/last/pallas_call | solution.py:297
Async XLA Ops:
  1.3 14.9 %copy-start = (f32[1,1,16,256,256]{4,3,2,1,0:T(8,128)S(1)}, f32[1,1,16,256,256]{4,3,2,1,0:T(8,128)}, u32[]{:S(2)}) copy-start(f32[1,1,16,256,256]{4,3,2,1,0:T(8,128)} %refs_1_.3) | copy-start | bytes 12582916
  16.1 5.3 %copy-start.1 = (f32[8,256]{1,0:T(8,128)S(1)}, f32[8,256]{1,0:T(8,128)}, u32[]{:S(2)}) copy-start(f32[8,256]{1,0:T(8,128)} %refs_7_.1) | copy-start | bytes 24580
  17.6 3.2 %collective-permute-start.2 = (f32[18,1,128]{2,1,0:T(1,128)S(1)}, f32[18,1,128]{2,1,0:T(1,128)S(1)}, u32[]{:S(2)}, u32[]{:S(2)}) collective-permute-start(f32[18,1,128]{2,1,0:T(1,128)S(1)} %get-tuple-element.21.refs_0_), channel_id=1, source_target_pairs={{0,3},{1,2},{2,1},{3,0},{4,7},{5,6},{6,5},{7,4},{8,11},{9,10},{10,... | collective-permute-start | bytes 27656 | tf_op jit(solution)/shard_map/ppermute | solution.py:227
  17.7 3.7 %collective-permute-start.1 = (f32[18,1,128]{2,1,0:T(1,128)S(1)}, f32[18,1,128]{2,1,0:T(1,128)S(1)}, u32[]{:S(2)}, u32[]{:S(2)}) collective-permute-start(f32[18,1,128]{2,1,0:T(1,128)S(1)} %get-tuple-element.21.refs_0_), channel_id=1, source_target_pairs={{0,2},{1,3},{2,0},{3,1},{4,6},{5,7},{6,4},{7,5},{8,10},{9,11},{10,... | collective-permute-start | bytes 27656 | tf_op jit(solution)/shard_map/ppermute | solution.py:227
  19.3 2.2 %collective-permute-start = (f32[18,1,128]{2,1,0:T(1,128)S(1)}, f32[18,1,128]{2,1,0:T(1,128)S(1)}, u32[]{:S(2)}, u32[]{:S(2)}) collective-permute-start(f32[18,1,128]{2,1,0:T(1,128)S(1)} %get-tuple-element.21.refs_0_), channel_id=1, source_target_pairs={{0,1},{1,0},{2,3},{3,2},{4,5},{5,4},{6,7},{7,6},{8,9},{9,8},{10,11... | collective-permute-start | bytes 27656 | tf_op jit(solution)/shard_map/ppermute | solution.py:227
  32.5 3.2 %collective-permute-start.5 = (f32[19,1,128]{2,1,0:T(1,128)S(1)}, f32[19,1,128]{2,1,0:T(1,128)S(1)}, u32[]{:S(2)}, u32[]{:S(2)}) collective-permute-start(f32[19,1,128]{2,1,0:T(1,128)S(1)} %get-tuple-element.29.refs_0_), channel_id=1, source_target_pairs={{0,3},{1,2},{2,1},{3,0},{4,7},{5,6},{6,5},{7,4},{8,11},{9,10},{10,... | collective-permute-start | bytes 29192 | tf_op jit(solution)/shard_map/ppermute | solution.py:227
  32.6 3.7 %collective-permute-start.4 = (f32[19,1,128]{2,1,0:T(1,128)S(1)}, f32[19,1,128]{2,1,0:T(1,128)S(1)}, u32[]{:S(2)}, u32[]{:S(2)}) collective-permute-start(f32[19,1,128]{2,1,0:T(1,128)S(1)} %get-tuple-element.29.refs_0_), channel_id=1, source_target_pairs={{0,2},{1,3},{2,0},{3,1},{4,6},{5,7},{6,4},{7,5},{8,10},{9,11},{10,... | collective-permute-start | bytes 29192 | tf_op jit(solution)/shard_map/ppermute | solution.py:227
  34.2 2.2 %collective-permute-start.3 = (f32[19,1,128]{2,1,0:T(1,128)S(1)}, f32[19,1,128]{2,1,0:T(1,128)S(1)}, u32[]{:S(2)}, u32[]{:S(2)}) collective-permute-start(f32[19,1,128]{2,1,0:T(1,128)S(1)} %get-tuple-element.29.refs_0_), channel_id=1, source_target_pairs={{0,1},{1,0},{2,3},{3,2},{4,5},{5,4},{6,7},{7,6},{8,9},{9,8},{10,11... | collective-permute-start | bytes 29192 | tf_op jit(solution)/shard_map/ppermute | solution.py:227

commit v4 on v3

--- a/solution.py
+++ b/solution.py
@@ -7,7 +7,7 @@
 
 ridge_weight = 0.5
 LANES = 128
-EXTRA = 8
+FLIP = 1 << 30
 VMEM_LIMIT = 16 << 20
 F32 = jnp.float32
 BF16 = jnp.bfloat16
@@ -34,9 +34,11 @@
     )(*args)
 
 
-def split(x):
+def split3(x):
     high = x.astype(BF16).astype(F32)
-    return jnp.concatenate([high, x - high], axis=0).astype(BF16)
+    rest = x - high
+    middle = rest.astype(BF16).astype(F32)
+    return jnp.concatenate([high, middle, rest - middle], axis=0).astype(BF16)
 
 
 def lane_sum(row):
@@ -65,32 +67,35 @@
     return jnp.concatenate([x[h * rows : (h + 1) * rows] for h in range(size // LANES)], axis=1)
 
 
-def place(table, vector):
-    return jnp.dot(table, split(vector), preferred_element_type=F32).astype(BF16)
-
-
-def join(total):
-    half = total.shape[0] // 2
-    return total[:half] + total[half:]
-
-
-def block_product(table, vector, high, low, slots, flip):
-    placed = place(table, vector)
-    step = placed.shape[0] // slots
+def block_product(spread, gather, vector, tiles, slots):
+    terms = split3(vector)
     size = vector.shape[1]
-    contract = (((1,), (1 if flip else 0,)), ((), ()))
-    total = jnp.zeros((step, size), F32)
-    rest = jnp.zeros((step, size), F32)
-    for k in range(slots):
-        left = placed[k * step : (k + 1) * step]
-        here = slice(k * size, (k + 1) * size)
-        total += lax.dot_general(left, high[here, :], contract, preferred_element_type=F32)
-        rest += lax.dot_general(left, low[here, :], contract, preferred_element_type=F32)
-    return join(total + rest)
+    parts = []
+    for k in range(0, slots, 2):
+        table = spread[:, k * LANES : (k + 2) * LANES]
+        wide = lax.dot_general(terms, table, (((0,), (0,)), ((), ())), preferred_element_type=F32)
+        for m in range(2):
+            here = wide[:, m * LANES : (m + 1) * LANES]
+            row = []
+            for h in range(0, size, LANES):
+                product = tiles[k + m, :, h : h + LANES] * here
+                row.append(jnp.sum(product.reshape(size // 8, 8, LANES), axis=0))
+            parts.append(jnp.concatenate(row, axis=1))
+    parts = jnp.concatenate(parts, axis=0)
+    count = parts.shape[0]
+    terms = split3(parts)
+    total = jnp.dot(gather[...], terms[:count], preferred_element_type=F32)
+    total += jnp.dot(gather[...], terms[count : 2 * count], preferred_element_type=F32)
+    return total + jnp.dot(gather[...], terms[2 * count :], preferred_element_type=F32)
+
+
+def flip_body(tiles, out):
+    for k in range(out.shape[0]):
+        out[k] = tiles[0, 0, k].T
 
 
 def start_body(group, cols, slots, *refs):
-    sources, (sent, to_cols, to_rows, own), held, sem = refs[:5], refs[5:9], refs[9:14], refs[14]
+    sources, (sent, spread_rows, spread_cols, gather_rows, gather_cols, own), held, sem = refs[:5], refs[5:11], refs[11:16], refs[16]
     copies = [pltpu.make_async_copy(a, b, sem.at[i]) for i, (a, b) in enumerate(zip(sources, held))]
     for copy in copies:
         copy.start()
@@ -102,40 +107,27 @@
     both = jnp.concatenate([side[...], weights[...]], axis=0)
     sent[...] = jnp.broadcast_to(both[None], sent.shape)
 
-    def table(targets, sources, target, source, live):
-        r = lax.broadcasted_iota(jnp.int32, (2 * targets, 2 * sources), 0)
-        q = lax.broadcasted_iota(jnp.int32, (2 * targets, 2 * sources), 1)
-        first = (r == target) & (q == source)
-        second = (r == targets + target) & (q == sources + source)
-        return jnp.where((first | second) & live, 1.0, 0.0).astype(BF16)
-
-    for k in range(slots):
-        live = k < count[0, 0]
-        row, col = rows_of[0, 0, k], cols_of[0, 0, k]
-        to_cols[pl.ds(k * 2 * cols, 2 * cols), :] = table(cols, group, col, row, live)
-        to_rows[pl.ds(k * 2 * group, 2 * group), :] = table(group, cols, row, col, live)
-
-
-def first_body(slots, cols, gathered, tiles, to_cols, out, high, low, high_t, low_t):
+    def tables(spread, gather, extent, index):
+        term = lax.broadcasted_iota(jnp.int32, (extent, LANES), 0)
+        slot = lax.broadcasted_iota(jnp.int32, gather.shape, 1) // 8
+        at = lax.broadcasted_iota(jnp.int32, gather.shape, 0)
+        target = jnp.full(gather.shape, -1, jnp.int32)
+        for k in range(slots):
+            source = jnp.where(k < count[0, 0], index[0, 0, k], -1)
+            one = jnp.where(term == source, 1.0, 0.0)
+            spread[:, pl.ds(k * LANES, LANES)] = jnp.concatenate([one] * 3, axis=0).astype(BF16)
+            target = jnp.where(slot == k, index[0, 0, k], target)
+        gather[...] = jnp.where(at == target, 1.0, 0.0).astype(BF16)
+
+    tables(spread_rows, gather_rows, group, rows_of)
+    tables(spread_cols, gather_cols, cols, cols_of)
+
+
+def first_body(slots, cols, gathered, tiles, spread, gather, out):
     residual, weights = gathered[:, 0, :], gathered[:, 1, :]
     z = weights * residual
     size = z.shape[1]
-    placed = place(to_cols[...], z)
-    step = 2 * cols
-    total = jnp.zeros((step, size), F32)
-    rest = jnp.zeros((step, size), F32)
-    for k in range(slots):
-        left = placed[k * step : (k + 1) * step]
-        tile = tiles[0, 0, k]
-        upper = tile.astype(BF16)
-        lower = (tile - upper.astype(F32)).astype(BF16)
-        high[pl.ds(k * size, size), :] = upper
-        low[pl.ds(k * size, size), :] = lower
-        high_t[pl.ds(k * size, size), :] = upper.T
-        low_t[pl.ds(k * size, size), :] = lower.T
-        total += jnp.dot(left, upper, preferred_element_type=F32)
-        rest += jnp.dot(left, lower, preferred_element_type=F32)
-    put(out, 0, join(total + rest))
+    put(out, 0, block_product(spread, gather, z, tiles.at[0, 0], slots))
     count = cols * (size // LANES)
     put(out, count, fold(row_sum(residual * z)))
     put(out, count + 1, fold(row_sum(z * z)))
@@ -146,21 +138,21 @@
     return (a + b) + (c + d)
 
 
-def second_body(slots, peers, p0, p1, p2, p3, scaling, high, low, to_rows, total, out):
+def second_body(slots, peers, p0, p1, p2, p3, scaling, flipped, spread, gather, total, out):
     summed = gather4((p0, p1, p2, p3))
     total[...] = summed
     cols, size = scaling.shape
     lifted = take(summed, cols, size)
     weighted = scaling[...] * lifted
     inner = fold(row_sum(weighted * lifted))
-    rows = block_product(to_rows[...], weighted, high, low, slots, False)
+    rows = block_product(spread, gather, weighted, flipped, slots)
     length = out.shape[0] // peers
     for j in range(peers):
         put(out, j * length, rows)
         put(out, (j + 1) * length - 1, inner)
 
 
-def third_body(slots, cols, arrived, gathered, total, high, low, to_cols, out, residual_out, alpha_out):
+def third_body(slots, cols, arrived, gathered, total, tiles, spread, gather, out, residual_out, alpha_out):
     residual, weights = gathered[:, 0, :], gathered[:, 1, :]
     z = weights * residual
     group, size = residual.shape
@@ -181,10 +173,10 @@
     put(out, count, fold(row_sum(later * z1)))
     put(out, count + 1, fold(row_sum(z1 * z1)))
     put(out, count + 2, fold(row_sum(z1 * z)))
-    put(out, 0, block_product(to_cols[...], z1, high, low, slots, False))
-
-
-def fourth_body(slots, p0, p1, p2, p3, total, gathered, residual, scaling, high, low, to_rows, out, direction_out, scalars):
+    put(out, 0, block_product(spread, gather, z1, tiles.at[0, 0], slots))
+
+
+def fourth_body(slots, p0, p1, p2, p3, total, gathered, residual, scaling, flipped, spread, gather, out, direction_out, scalars):
     summed = gather4((p0, p1, p2, p3))
     cols, size = scaling.shape
     count = cols * (size // LANES)
@@ -196,7 +188,7 @@
     lifted = take(summed, cols, size) + beta * take(total[...], cols, size)
     weighted = scaling[...] * lifted
     inner = fold(row_sum(weighted * lifted))
-    rows = block_product(to_rows[...], weighted, high, low, slots, False)
+    rows = block_product(spread, gather, weighted, flipped, slots)
     peers = out.shape[0]
     for h, piece in enumerate(pieces_of(rows)):
         out[:, h, :] = piece
@@ -240,13 +232,15 @@
     long = slots * size
     work = dict(flops=8 * long * size, moved=0)
 
-    sent, to_cols, to_rows, own = call(
+    sent, spread_rows, spread_cols, gather_rows, gather_cols, own = call(
         lambda *refs: start_body(group, cols, slots, *refs),
         "start",
         [
             ((peers, 2, size), F32),
-            ((slots * 2 * cols, 2 * group), BF16),
-            ((slots * 2 * group, 2 * cols), BF16),
+            ((3 * group, slots * LANES), BF16),
+            ((3 * cols, slots * LANES), BF16),
+            ((group, slots * 8), BF16),
+            ((cols, slots * 8), BF16),
             ((group, LANES), F32),
         ],
         (stay(right_side), stay(precond), block_count, stay(block_rows), stay(block_cols)),
@@ -263,19 +257,20 @@
         moved=100 << 20,
     )
     gathered = lax.all_to_all(sent, "col", 0, 0, tiled=True)
-    mine, high, low, high_t, low_t = call(
+    (mine,) = call(
         lambda *refs: first_body(slots, cols, *refs),
         "first",
-        [((cols * pieces + 2, 1, LANES), F32)] + [((long, size), BF16)] * 4,
-        (gathered, blocks, to_cols),
+        [((cols * pieces + 2, 1, LANES), F32)],
+        (gathered, blocks, spread_rows, gather_cols),
         **work,
     )
+    (flipped,) = call(flip_body, "flip", [((slots, size, size), F32)], (blocks,), flops=FLIP)
     length = group * pieces + 1
     total, sent = call(
         lambda *refs: second_body(slots, peers, *refs),
         "second",
         [((cols * pieces + 2, LANES), F32), ((peers * length, 1, LANES), F32)],
-        (*share(mine, "row", groups), scaling, high_t, low_t, to_rows),
+        (*share(mine, "row", groups), scaling, flipped, spread_cols, gather_rows),
         **work,
     )
     arrived = lax.all_to_all(sent, "col", 0, 0, tiled=True)
@@ -283,14 +278,14 @@
         lambda *refs: third_body(slots, cols, *refs),
         "third",
         [((cols * pieces + 3, 1, LANES), F32), ((group, size), F32), ((1, LANES), F32)],
-        (arrived, gathered, total, high, low, to_cols),
+        (arrived, gathered, total, blocks, spread_rows, gather_cols),
         **work,
     )
     sent, direction, scalars = call(
         lambda *refs: fourth_body(slots, *refs),
         "fourth",
         [((peers, pieces + 1, LANES), F32), ((group, size), F32), ((2, LANES), F32)],
-        (*share(mine, "row", groups), total, gathered, residual, scaling, high_t, low_t, to_rows),
+        (*share(mine, "row", groups), total, gathered, residual, scaling, flipped, spread_cols, gather_rows),
         **work,
     )
     arrived = lax.all_to_all(sent, "col", 0, 0, tiled=True)

time: 47.2 us -> 45.7 us (0.968)
  waiting for transfers between devices: 3.77 us -> 2.62 us
    ppermute x6, waiting for transfers between devices: 3.77 us -> 2.62 us  [share(): moved.append(lax.ppermute(value, axis, [(i, i ^ s) for i in range(size)]))]
    pallas_call x5 -> x6, Pallas kernels: 5.18 us -> 4.93 us  [call(): pl.pallas_call(body, name=name, out_shape=[pltpu.VMEM(s, d) for s, d in o...]
  transfers between devices with their start and end apart: 6 -> 6, of which waited for: 4 -> 4; matrix products, arithmetic and copies ran while one was open for 0% -> 0% of each run, Pallas kernels for 0% -> 2%
where the time goes in v4:
time: 45.7 us; the launch traced here: 45.5 us
  blocking collectives  32.1 us (70%)
  Pallas kernels  5.67 us (12%)
  starting transfers between devices  3.77 us (8%)
  waiting for transfers between devices  2.62 us (6%)
  between operations  1.33 us (3%)
    all_to_all x2, blocking collectives, local(): arrived = lax.all_to_all(sent, 'col', 0, 0, tiled=True)  18.3 us
    all_to_all x1, blocking collectives, local(): gathered = lax.all_to_all(sent, 'col', 0, 0, tiled=True)  13.8 us
    pallas_call x6, Pallas kernels, call(): pl.pallas_call(body, name=name, out_shape=[pltpu.VMEM(s, d) for s, d in o...  4.93 us
    ppermute x6, starting transfers between devices, share(): moved.append(lax.ppermute(value, axis, [(i, i ^ s) for i in range(size)]))  3.77 us
    ppermute x6, waiting for transfers between devices, share(): moved.append(lax.ppermute(value, axis, [(i, i ^ s) for i in range(size)]))  2.62 us
  transfers between devices with their start and end apart: 6, of which 4 were waited for; matrix products, arithmetic and copies ran while one was open for 0% of the time, Pallas kernels for 2%

profile of v4, /device:TPU:0, one launch (start us, length us, event | category | flops | bytes accessed | tf_op | source)
XLA Modules:
  0.0 45.5 jit_solution(1229021374037399133)
XLA Ops:
  1.3 0.0 copy-start
  1.3 1.0 %start.1 = (f32[8,2,256]{2,1,0:T(2,128)S(1)}, bf16[24,2048]{1,0:T(8,128)(2,1)S(1)}, bf16[24,2048]{1,0:T(8,128)(2,1)S(1)}, bf16[8,128]{1,0:T(8,128)(2,1)S(1)}, bf...) custom-call(f32[1,256]{1,0:T(1,128)} %refs_0_.1, f32[1,256]{1,0:T(1,128)} %refs_1_.2, s32[1,1]{1,0:T(1,128)S(6)} %copy.9.refs_2_, ...), custom_call_target="tpu_custom_call" | custom-call | flops 17179869184 | bytes 104857600 | tf_op jit(solution)/shard_map/start/pallas_call | solution.py:25
  2.3 13.8 %all_to_all.15.refs_0_.refs_1_.refs_5_.gathered = f32[8,2,256]{2,1,0:T(2,128)S(1)} all-to-all(f32[8,2,256]{2,1,0:T(2,128)S(1)} %get-tuple-element.16), channel_id=1, replica_groups=mesh['col'=8,'row'=4] {'col'}, dimensions={0} | all-to-all | bytes 32768 | tf_op jit(solution)/shard_map/all_to_all | solution.py:259
  16.1 0.0 copy-done
  16.1 0.7 %first.1.refs_0_ = f32[18,1,128]{2,1,0:T(1,128)S(1)} custom-call(f32[8,2,256]{2,1,0:T(2,128)S(1)} %all_to_all.15.refs_0_.refs_1_.refs_5_.gathered, f32[1,1,16,256,256]{4,3,2,1,0:T(8,128)S(1)} %copy-done, bf16[24,2048]{1,0:T(8,128)(2,1)S(1)} %get-tuple-element.17.refs_2_.refs_4_, bf16[8,128]{1,0:T(8,128)(2,1)S(1)} %get-tuple-element.18.refs_3_.refs_5_), custom_call_target="tpu_custom_call" | custom-call | flops 8388608 | tf_op jit(solution)/shard_map/first/pallas_call | solution.py:25
  16.8 0.0 copy-start.1
  16.8 0.1 collective-permute-start.2
  16.8 1.6 %collective-permute-start.1 = (f32[18,1,128]{2,1,0:T(1,128)S(1)}, f32[18,1,128]{2,1,0:T(1,128)S(1)}, u32[]{:S(2)}, u32[]{:S(2)}) collective-permute-start(f32[18,1,128]{2,1,0:T(1,128)S(1)} %first.1.refs_0_), channel_id=1, source_target_pairs={{0,2},{1,3},{2,0},{3,1},{4,6},{5,7},{6,4},{7,5},{8,10},{9,11},{10,... | collective-permute-start | bytes 27656 | tf_op jit(solution)/shard_map/ppermute | solution.py:219
  18.4 0.3 collective-permute-start
  18.7 1.1 %flip.1.refs_5_.refs_8_ = f32[16,256,256]{2,1,0:T(8,128)S(1)} custom-call(f32[1,1,16,256,256]{4,3,2,1,0:T(8,128)S(1)} %copy-done), custom_call_target="tpu_custom_call" | custom-call | flops 1073741824 | tf_op jit(solution)/shard_map/flip/pallas_call | solution.py:25
  19.8 0.1 collective-permute-done.2.refs_3_
  19.9 0.6 %collective-permute-done.1.refs_2_ = f32[18,1,128]{2,1,0:T(1,128)S(1)} collective-permute-done((f32[18,1,128]{2,1,0:T(1,128)S(1)}, f32[18,1,128]{2,1,0:T(1,128)S(1)}, u32[]{:S(2)}, u32[]{:S(2)}) %collective-permute-start.1) | collective-permute-done | bytes 9248 | tf_op jit(solution)/shard_map/ppermute | solution.py:219
  20.5 0.0 collective-permute-done.refs_1_
  20.5 0.0 copy-done.1
  20.5 0.7 %second.1 = (f32[18,128]{1,0:T(8,128)S(1)}, f32[136,1,128]{2,1,0:T(1,128)S(1)}) custom-call(f32[18,1,128]{2,1,0:T(1,128)S(1)} %first.1.refs_0_, f32[18,1,128]{2,1,0:T(1,128)S(1)} %collective-permute-done.refs_1_, f32[18,1,128]{2,1,0:T(1,128)S(1)} %collective-permute-done.1.refs_2_, f32[18,1,128]{2,1,0:T(1,128)S(1)} %collective-permute-done.2.refs_3_, ...), custom_call_target="tpu_custom_call" | custom-call | flops 8388608 | tf_op jit(solution)/shard_map/second/pallas_call | solution.py:25
  21.2 9.3 %all_to_all.16.refs_0_ = f32[136,1,128]{2,1,0:T(1,128)S(1)} all-to-all(f32[136,1,128]{2,1,0:T(1,128)S(1)} %get-tuple-element.21), channel_id=1, replica_groups=mesh['col'=8,'row'=4] {'col'}, dimensions={0} | all-to-all | bytes 139264 | tf_op jit(solution)/shard_map/all_to_all | solution.py:276
  30.6 0.7 %third.1 = (f32[19,1,128]{2,1,0:T(1,128)S(1)}, f32[8,256]{1,0:T(8,128)S(1)}, f32[1,128]{1,0:T(1,128)S(1)}) custom-call(f32[136,1,128]{2,1,0:T(1,128)S(1)} %all_to_all.16.refs_0_, f32[8,2,256]{2,1,0:T(2,128)S(1)} %all_to_all.15.refs_0_.refs_1_.refs_5_.gathered, f32[18,128]{1,0:T(8,128)S(1)} %get-tuple-element.22.refs_2_.refs_4_, ...), custom_call_target="tpu_custom_call" | custom-call | flops 8388608 | tf_op jit(solution)/shard_map/third/pallas_call | solution.py:25
  31.3 0.0 collective-permute-start.5
  31.3 1.6 %collective-permute-start.4 = (f32[19,1,128]{2,1,0:T(1,128)S(1)}, f32[19,1,128]{2,1,0:T(1,128)S(1)}, u32[]{:S(2)}, u32[]{:S(2)}) collective-permute-start(f32[19,1,128]{2,1,0:T(1,128)S(1)} %get-tuple-element.23.refs_0_), channel_id=1, source_target_pairs={{0,2},{1,3},{2,0},{3,1},{4,6},{5,7},{6,4},{7,5},{8,10},{9,11},{10,... | collective-permute-start | bytes 29192 | tf_op jit(solution)/shard_map/ppermute | solution.py:219
  32.9 0.3 collective-permute-start.3
  33.2 1.3 %collective-permute-done.5.refs_3_ = f32[19,1,128]{2,1,0:T(1,128)S(1)} collective-permute-done((f32[19,1,128]{2,1,0:T(1,128)S(1)}, f32[19,1,128]{2,1,0:T(1,128)S(1)}, u32[]{:S(2)}, u32[]{:S(2)}) %collective-permute-start.5) | collective-permute-done | bytes 9760 | tf_op jit(solution)/shard_map/ppermute | solution.py:219
  34.5 0.6 %collective-permute-done.4.refs_2_ = f32[19,1,128]{2,1,0:T(1,128)S(1)} collective-permute-done((f32[19,1,128]{2,1,0:T(1,128)S(1)}, f32[19,1,128]{2,1,0:T(1,128)S(1)}, u32[]{:S(2)}, u32[]{:S(2)}) %collective-permute-start.4) | collective-permute-done | bytes 9760 | tf_op jit(solution)/shard_map/ppermute | solution.py:219
  35.1 0.0 collective-permute-done.3.refs_1_
  35.1 0.7 %fourth.1 = (f32[8,3,128]{2,1,0:T(4,128)S(1)}, f32[8,256]{1,0:T(8,128)S(1)}, f32[2,128]{1,0:T(2,128)S(1)}) custom-call(f32[19,1,128]{2,1,0:T(1,128)S(1)} %get-tuple-element.23.refs_0_, f32[19,1,128]{2,1,0:T(1,128)S(1)} %collective-permute-done.3.refs_1_, f32[19,1,128]{2,1,0:T(1,128)S(1)} %collective-permute-done.4.refs_2_, ...), custom_call_target="tpu_custom_call" | custom-call | flops 8388608 | tf_op jit(solution)/shard_map/fourth/pallas_call | solution.py:25
  35.8 8.9 %all_to_all.17.arrived = f32[8,3,128]{2,1,0:T(4,128)S(1)} all-to-all(f32[8,3,128]{2,1,0:T(4,128)S(1)} %get-tuple-element.25), channel_id=1, replica_groups=mesh['col'=8,'row'=4] {'col'}, dimensions={0} | all-to-all | bytes 24576 | tf_op jit(solution)/shard_map/all_to_all | solution.py:291
  44.7 0.7 %last.1 = (f32[1,256]{1,0:T(1,128)}, f32[1,256]{1,0:T(1,128)}) custom-call(f32[8,3,128]{2,1,0:T(4,128)S(1)} %all_to_all.17.arrived, f32[8,2,256]{2,1,0:T(2,128)S(1)} %all_to_all.15.refs_0_.refs_1_.refs_5_.gathered, f32[8,256]{1,0:T(8,128)S(1)} %get-tuple-element.24.refs_6_.residual, f32[8,256]{1,0:T(8,128)S(1)} %get-tuple-element.26.direction, ...), custom_call_target="tpu_custom_call" | custom-call | tf_op jit(solution)/shard_map/last/pallas_call | solution.py:292
Async XLA Ops:
  1.3 14.8 %copy-start = (f32[1,1,16,256,256]{4,3,2,1,0:T(8,128)S(1)}, f32[1,1,16,256,256]{4,3,2,1,0:T(8,128)}, u32[]{:S(2)}) copy-start(f32[1,1,16,256,256]{4,3,2,1,0:T(8,128)} %refs_3_.3) | copy-start | bytes 12582916
  16.8 3.8 %copy-start.1 = (f32[8,256]{1,0:T(8,128)S(1)}, f32[8,256]{1,0:T(8,128)}, u32[]{:S(2)}) copy-start(f32[8,256]{1,0:T(8,128)} %refs_7_.1) | copy-start | bytes 24580
  16.8 3.2 %collective-permute-start.2 = (f32[18,1,128]{2,1,0:T(1,128)S(1)}, f32[18,1,128]{2,1,0:T(1,128)S(1)}, u32[]{:S(2)}, u32[]{:S(2)}) collective-permute-start(f32[18,1,128]{2,1,0:T(1,128)S(1)} %first.1.refs_0_), channel_id=1, source_target_pairs={{0,3},{1,2},{2,1},{3,0},{4,7},{5,6},{6,5},{7,4},{8,11},{9,10},{10,... | collective-permute-start | bytes 27656 | tf_op jit(solution)/shard_map/ppermute | solution.py:219
  16.8 3.7 %collective-permute-start.1 = (f32[18,1,128]{2,1,0:T(1,128)S(1)}, f32[18,1,128]{2,1,0:T(1,128)S(1)}, u32[]{:S(2)}, u32[]{:S(2)}) collective-permute-start(f32[18,1,128]{2,1,0:T(1,128)S(1)} %first.1.refs_0_), channel_id=1, source_target_pairs={{0,2},{1,3},{2,0},{3,1},{4,6},{5,7},{6,4},{7,5},{8,10},{9,11},{10,... | collective-permute-start | bytes 27656 | tf_op jit(solution)/shard_map/ppermute | solution.py:219
  18.4 2.2 %collective-permute-start = (f32[18,1,128]{2,1,0:T(1,128)S(1)}, f32[18,1,128]{2,1,0:T(1,128)S(1)}, u32[]{:S(2)}, u32[]{:S(2)}) collective-permute-start(f32[18,1,128]{2,1,0:T(1,128)S(1)} %first.1.refs_0_), channel_id=1, source_target_pairs={{0,1},{1,0},{2,3},{3,2},{4,5},{5,4},{6,7},{7,6},{8,9},{9,8},{10,11... | collective-permute-start | bytes 27656 | tf_op jit(solution)/shard_map/ppermute | solution.py:219
  31.3 3.2 %collective-permute-start.5 = (f32[19,1,128]{2,1,0:T(1,128)S(1)}, f32[19,1,128]{2,1,0:T(1,128)S(1)}, u32[]{:S(2)}, u32[]{:S(2)}) collective-permute-start(f32[19,1,128]{2,1,0:T(1,128)S(1)} %get-tuple-element.23.refs_0_), channel_id=1, source_target_pairs={{0,3},{1,2},{2,1},{3,0},{4,7},{5,6},{6,5},{7,4},{8,11},{9,10},{10,... | collective-permute-start | bytes 29192 | tf_op jit(solution)/shard_map/ppermute | solution.py:219
  31.3 3.7 %collective-permute-start.4 = (f32[19,1,128]{2,1,0:T(1,128)S(1)}, f32[19,1,128]{2,1,0:T(1,128)S(1)}, u32[]{:S(2)}, u32[]{:S(2)}) collective-permute-start(f32[19,1,128]{2,1,0:T(1,128)S(1)} %get-tuple-element.23.refs_0_), channel_id=1, source_target_pairs={{0,2},{1,3},{2,0},{3,1},{4,6},{5,7},{6,4},{7,5},{8,10},{9,11},{10,... | collective-permute-start | bytes 29192 | tf_op jit(solution)/shard_map/ppermute | solution.py:219
  32.9 2.2 %collective-permute-start.3 = (f32[19,1,128]{2,1,0:T(1,128)S(1)}, f32[19,1,128]{2,1,0:T(1,128)S(1)}, u32[]{:S(2)}, u32[]{:S(2)}) collective-permute-start(f32[19,1,128]{2,1,0:T(1,128)S(1)} %get-tuple-element.23.refs_0_), channel_id=1, source_target_pairs={{0,1},{1,0},{2,3},{3,2},{4,5},{5,4},{6,7},{7,6},{8,9},{9,8},{10,11... | collective-permute-start | bytes 29192 | tf_op jit(solution)/shard_map/ppermute | solution.py:219

commit v5 on v4

--- a/solution.py
+++ b/solution.py
@@ -8,6 +8,7 @@
 ridge_weight = 0.5
 LANES = 128
 FLIP = 1 << 30
+FIRST = (5, 5, 5)
 VMEM_LIMIT = 16 << 20
 F32 = jnp.float32
 BF16 = jnp.bfloat16
@@ -94,12 +95,16 @@
         out[k] = tiles[0, 0, k].T
 
 
-def start_body(group, cols, slots, *refs):
+def start_body(group, cols, slots, first, *refs):
     sources, (sent, spread_rows, spread_cols, gather_rows, gather_cols, own), held, sem = refs[:5], refs[5:11], refs[11:16], refs[16]
     copies = [pltpu.make_async_copy(a, b, sem.at[i]) for i, (a, b) in enumerate(zip(sources, held))]
     for copy in copies:
         copy.start()
-    mine = lax.broadcasted_iota(jnp.int32, own.shape, 0) == lax.axis_index("col")
+
+    def place(index):
+        return jnp.where(index >= first, index - first, index - first + group)
+
+    mine = lax.broadcasted_iota(jnp.int32, own.shape, 0) == place(lax.axis_index("col"))
     own[...] = jnp.where(mine, 1.0, 0.0)
     for copy in copies:
         copy.wait()
@@ -113,14 +118,14 @@
         at = lax.broadcasted_iota(jnp.int32, gather.shape, 0)
         target = jnp.full(gather.shape, -1, jnp.int32)
         for k in range(slots):
-            source = jnp.where(k < count[0, 0], index[0, 0, k], -1)
+            source = jnp.where(k < count[0, 0], index[k], -1)
             one = jnp.where(term == source, 1.0, 0.0)
             spread[:, pl.ds(k * LANES, LANES)] = jnp.concatenate([one] * 3, axis=0).astype(BF16)
-            target = jnp.where(slot == k, index[0, 0, k], target)
+            target = jnp.where(slot == k, index[k], target)
         gather[...] = jnp.where(at == target, 1.0, 0.0).astype(BF16)
 
-    tables(spread_rows, gather_rows, group, rows_of)
-    tables(spread_cols, gather_cols, cols, cols_of)
+    tables(spread_rows, gather_rows, group, [place(rows_of[0, 0, k]) for k in range(slots)])
+    tables(spread_cols, gather_cols, cols, [cols_of[0, 0, k] for k in range(slots)])
 
 
 def first_body(slots, cols, gathered, tiles, spread, gather, out):
@@ -176,7 +181,7 @@
     put(out, 0, block_product(spread, gather, z1, tiles.at[0, 0], slots))
 
 
-def fourth_body(slots, p0, p1, p2, p3, total, gathered, residual, scaling, flipped, spread, gather, out, direction_out, scalars):
+def fourth_body(slots, by, p0, p1, p2, p3, total, gathered, residual, scaling, flipped, spread, gather, out, direction_out, scalars):
     summed = gather4((p0, p1, p2, p3))
     cols, size = scaling.shape
     count = cols * (size // LANES)
@@ -191,7 +196,7 @@
     rows = block_product(spread, gather, weighted, flipped, slots)
     peers = out.shape[0]
     for h, piece in enumerate(pieces_of(rows)):
-        out[:, h, :] = piece
+        out[:, h, :] = turned(piece, by)
     out[:, size // LANES, :] = jnp.broadcast_to(inner, (peers, LANES))
     weights = gathered[:, 1, :]
     direction_out[...] = weights * residual[...] + beta * (weights * gathered[:, 0, :])
@@ -213,6 +218,16 @@
     residual_out[...] = before - step * (image + ridge_weight * second)
 
 
+def turned(x, by):
+    by %= x.shape[0]
+    return jnp.concatenate([x[by:], x[:by]], axis=0) if by else x
+
+
+def exchange(value, size, first):
+    order = [(p + first) % size for p in range(size)]
+    return lax.all_to_all(value, "col", 0, 0, tiled=True, axis_index_groups=[order])
+
+
 def share(value, axis, size):
     moved = [value]
     for s in range(1, size):
@@ -230,10 +245,11 @@
     cols = scaling.shape[0]
     pieces = size // LANES
     long = slots * size
+    starts = [peers * f // 8 for f in FIRST]
     work = dict(flops=8 * long * size, moved=0)
 
     sent, spread_rows, spread_cols, gather_rows, gather_cols, own = call(
-        lambda *refs: start_body(group, cols, slots, *refs),
+        lambda *refs: start_body(group, cols, slots, starts[0], *refs),
         "start",
         [
             ((peers, 2, size), F32),
@@ -256,7 +272,7 @@
         flops=1 << 34,
         moved=100 << 20,
     )
-    gathered = lax.all_to_all(sent, "col", 0, 0, tiled=True)
+    gathered = exchange(sent, peers, starts[0])
     (mine,) = call(
         lambda *refs: first_body(slots, cols, *refs),
         "first",
@@ -273,7 +289,7 @@
         (*share(mine, "row", groups), scaling, flipped, spread_cols, gather_rows),
         **work,
     )
-    arrived = lax.all_to_all(sent, "col", 0, 0, tiled=True)
+    arrived = exchange(sent, peers, starts[1])
     mine, residual, alpha = call(
         lambda *refs: third_body(slots, cols, *refs),
         "third",
@@ -282,13 +298,13 @@
         **work,
     )
     sent, direction, scalars = call(
-        lambda *refs: fourth_body(slots, *refs),
+        lambda *refs: fourth_body(slots, starts[2] - starts[0], *refs),
         "fourth",
         [((peers, pieces + 1, LANES), F32), ((group, size), F32), ((2, LANES), F32)],
         (*share(mine, "row", groups), total, gathered, residual, scaling, flipped, spread_cols, gather_rows),
         **work,
     )
-    arrived = lax.all_to_all(sent, "col", 0, 0, tiled=True)
+    arrived = exchange(sent, peers, starts[2])
     return pl.pallas_call(
         last_body,
         name="last",

time: 45.7 us -> 41.6 us (0.910)
  blocking collectives: 32.1 us -> 27.9 us
    all_to_all x3, blocking collectives: 32.1 us -> 27.9 us  [exchange(): lax.all_to_all(value, 'col', 0, 0, tiled=True, axis_index_groups=[order])]
  transfers between devices with their start and end apart: 6 -> 6, of which waited for: 4 -> 4; matrix products, arithmetic and copies ran while one was open for 0% -> 0% of each run, Pallas kernels for 2% -> 3%
where the time goes in v5:
time: 41.6 us; the launch traced here: 41.3 us
  blocking collectives  27.9 us (67%)
  Pallas kernels  5.68 us (14%)
  starting transfers between devices  3.77 us (9%)
  waiting for transfers between devices  2.62 us (6%)
  between operations  1.33 us (3%)
    all_to_all x3, blocking collectives, exchange(): lax.all_to_all(value, 'col', 0, 0, tiled=True, axis_index_groups=[order])  27.9 us
    pallas_call x6, Pallas kernels, call(): pl.pallas_call(body, name=name, out_shape=[pltpu.VMEM(s, d) for s, d in o...  4.94 us
    ppermute x6, starting transfers between devices, share(): moved.append(lax.ppermute(value, axis, [(i, i ^ s) for i in range(size)]))  3.77 us
    ppermute x6, waiting for transfers between devices, share(): moved.append(lax.ppermute(value, axis, [(i, i ^ s) for i in range(size)]))  2.62 us
  transfers between devices with their start and end apart: 6, of which 4 were waited for; matrix products, arithmetic and copies ran while one was open for 0% of the time, Pallas kernels for 3%

profile of v5, /device:TPU:0, one launch (start us, length us, event | category | flops | bytes accessed | tf_op | source)
XLA Modules:
  0.0 41.3 jit_solution(701199585814877496)
XLA Ops:
  1.3 0.0 copy-start
  1.3 1.0 %start.1 = (f32[8,2,256]{2,1,0:T(2,128)S(1)}, bf16[24,2048]{1,0:T(8,128)(2,1)S(1)}, bf16[24,2048]{1,0:T(8,128)(2,1)S(1)}, bf16[8,128]{1,0:T(8,128)(2,1)S(1)}, bf...) custom-call(f32[1,256]{1,0:T(1,128)} %refs_0_.1, f32[1,256]{1,0:T(1,128)} %refs_1_.2, s32[1,1]{1,0:T(1,128)S(6)} %copy.9.refs_2_, ...), custom_call_target="tpu_custom_call" | custom-call | flops 17179869184 | bytes 104857600 | tf_op jit(solution)/shard_map/start/pallas_call | solution.py:26
  2.3 11.1 %all_to_all.15.refs_0_.refs_1_.refs_5_.gathered = f32[8,2,256]{2,1,0:T(2,128)S(1)} all-to-all(f32[8,2,256]{2,1,0:T(2,128)S(1)} %get-tuple-element.16), channel_id=1, replica_groups={{20,24,28,0,4,8,12,16},{21,25,29,1,5,9,13,17},{22,26,30,2,6,10,14,18},{..., dimensions={0} | all-to-all | bytes 32768 | tf_op jit(solution)/shard_map/all_to_all | solution.py:228
  13.4 0.0 copy-done
  13.4 0.7 %first.1.refs_0_ = f32[18,1,128]{2,1,0:T(1,128)S(1)} custom-call(f32[8,2,256]{2,1,0:T(2,128)S(1)} %all_to_all.15.refs_0_.refs_1_.refs_5_.gathered, f32[1,1,16,256,256]{4,3,2,1,0:T(8,128)S(1)} %copy-done, bf16[24,2048]{1,0:T(8,128)(2,1)S(1)} %get-tuple-element.17.refs_2_.refs_4_, bf16[8,128]{1,0:T(8,128)(2,1)S(1)} %get-tuple-element.18.refs_3_.refs_5_), custom_call_target="tpu_custom_call" | custom-call | flops 8388608 | tf_op jit(solution)/shard_map/first/pallas_call | solution.py:26
  14.1 0.0 copy-start.1
  14.1 0.1 collective-permute-start.2
  14.1 1.6 %collective-permute-start.1 = (f32[18,1,128]{2,1,0:T(1,128)S(1)}, f32[18,1,128]{2,1,0:T(1,128)S(1)}, u32[]{:S(2)}, u32[]{:S(2)}) collective-permute-start(f32[18,1,128]{2,1,0:T(1,128)S(1)} %first.1.refs_0_), channel_id=1, source_target_pairs={{0,2},{1,3},{2,0},{3,1},{4,6},{5,7},{6,4},{7,5},{8,10},{9,11},{10,... | collective-permute-start | bytes 27656 | tf_op jit(solution)/shard_map/ppermute | solution.py:234
  15.7 0.3 collective-permute-start
  16.0 1.1 %flip.1.refs_5_.refs_8_ = f32[16,256,256]{2,1,0:T(8,128)S(1)} custom-call(f32[1,1,16,256,256]{4,3,2,1,0:T(8,128)S(1)} %copy-done), custom_call_target="tpu_custom_call" | custom-call | flops 1073741824 | tf_op jit(solution)/shard_map/flip/pallas_call | solution.py:26
  17.1 0.1 collective-permute-done.2.refs_3_
  17.2 0.6 %collective-permute-done.1.refs_2_ = f32[18,1,128]{2,1,0:T(1,128)S(1)} collective-permute-done((f32[18,1,128]{2,1,0:T(1,128)S(1)}, f32[18,1,128]{2,1,0:T(1,128)S(1)}, u32[]{:S(2)}, u32[]{:S(2)}) %collective-permute-start.1) | collective-permute-done | bytes 9248 | tf_op jit(solution)/shard_map/ppermute | solution.py:234
  17.9 0.0 collective-permute-done.refs_1_
  17.9 0.0 copy-done.1
  17.9 0.7 %second.1 = (f32[18,128]{1,0:T(8,128)S(1)}, f32[136,1,128]{2,1,0:T(1,128)S(1)}) custom-call(f32[18,1,128]{2,1,0:T(1,128)S(1)} %first.1.refs_0_, f32[18,1,128]{2,1,0:T(1,128)S(1)} %collective-permute-done.refs_1_, f32[18,1,128]{2,1,0:T(1,128)S(1)} %collective-permute-done.1.refs_2_, f32[18,1,128]{2,1,0:T(1,128)S(1)} %collective-permute-done.2.refs_3_, ...), custom_call_target="tpu_custom_call" | custom-call | flops 8388608 | tf_op jit(solution)/shard_map/second/pallas_call | solution.py:26
  18.6 8.6 %all_to_all.16.refs_0_ = f32[136,1,128]{2,1,0:T(1,128)S(1)} all-to-all(f32[136,1,128]{2,1,0:T(1,128)S(1)} %get-tuple-element.21), channel_id=1, replica_groups={{20,24,28,0,4,8,12,16},{21,25,29,1,5,9,13,17},{22,26,30,2,6,10,14,18},{..., dimensions={0} | all-to-all | bytes 139264 | tf_op jit(solution)/shard_map/all_to_all | solution.py:228
  27.1 0.7 %third.1 = (f32[19,1,128]{2,1,0:T(1,128)S(1)}, f32[8,256]{1,0:T(8,128)S(1)}, f32[1,128]{1,0:T(1,128)S(1)}) custom-call(f32[136,1,128]{2,1,0:T(1,128)S(1)} %all_to_all.16.refs_0_, f32[8,2,256]{2,1,0:T(2,128)S(1)} %all_to_all.15.refs_0_.refs_1_.refs_5_.gathered, f32[18,128]{1,0:T(8,128)S(1)} %get-tuple-element.22.refs_2_.refs_4_, ...), custom_call_target="tpu_custom_call" | custom-call | flops 8388608 | tf_op jit(solution)/shard_map/third/pallas_call | solution.py:26
  27.9 0.0 collective-permute-start.5
  27.9 1.6 %collective-permute-start.4 = (f32[19,1,128]{2,1,0:T(1,128)S(1)}, f32[19,1,128]{2,1,0:T(1,128)S(1)}, u32[]{:S(2)}, u32[]{:S(2)}) collective-permute-start(f32[19,1,128]{2,1,0:T(1,128)S(1)} %get-tuple-element.23.refs_0_), channel_id=1, source_target_pairs={{0,2},{1,3},{2,0},{3,1},{4,6},{5,7},{6,4},{7,5},{8,10},{9,11},{10,... | collective-permute-start | bytes 29192 | tf_op jit(solution)/shard_map/ppermute | solution.py:234
  29.4 0.3 collective-permute-start.3
  29.7 1.3 %collective-permute-done.5.refs_3_ = f32[19,1,128]{2,1,0:T(1,128)S(1)} collective-permute-done((f32[19,1,128]{2,1,0:T(1,128)S(1)}, f32[19,1,128]{2,1,0:T(1,128)S(1)}, u32[]{:S(2)}, u32[]{:S(2)}) %collective-permute-start.5) | collective-permute-done | bytes 9760 | tf_op jit(solution)/shard_map/ppermute | solution.py:234
  31.0 0.6 %collective-permute-done.4.refs_2_ = f32[19,1,128]{2,1,0:T(1,128)S(1)} collective-permute-done((f32[19,1,128]{2,1,0:T(1,128)S(1)}, f32[19,1,128]{2,1,0:T(1,128)S(1)}, u32[]{:S(2)}, u32[]{:S(2)}) %collective-permute-start.4) | collective-permute-done | bytes 9760 | tf_op jit(solution)/shard_map/ppermute | solution.py:234
  31.6 0.0 collective-permute-done.3.refs_1_
  31.6 0.7 %fourth.1 = (f32[8,3,128]{2,1,0:T(4,128)S(1)}, f32[8,256]{1,0:T(8,128)S(1)}, f32[2,128]{1,0:T(2,128)S(1)}) custom-call(f32[19,1,128]{2,1,0:T(1,128)S(1)} %get-tuple-element.23.refs_0_, f32[19,1,128]{2,1,0:T(1,128)S(1)} %collective-permute-done.3.refs_1_, f32[19,1,128]{2,1,0:T(1,128)S(1)} %collective-permute-done.4.refs_2_, ...), custom_call_target="tpu_custom_call" | custom-call | flops 8388608 | tf_op jit(solution)/shard_map/fourth/pallas_call | solution.py:26
  32.3 8.2 %all_to_all.17.arrived = f32[8,3,128]{2,1,0:T(4,128)S(1)} all-to-all(f32[8,3,128]{2,1,0:T(4,128)S(1)} %get-tuple-element.25), channel_id=1, replica_groups={{20,24,28,0,4,8,12,16},{21,25,29,1,5,9,13,17},{22,26,30,2,6,10,14,18},{..., dimensions={0} | all-to-all | bytes 24576 | tf_op jit(solution)/shard_map/all_to_all | solution.py:228
  40.6 0.7 %last.1 = (f32[1,256]{1,0:T(1,128)}, f32[1,256]{1,0:T(1,128)}) custom-call(f32[8,3,128]{2,1,0:T(4,128)S(1)} %all_to_all.17.arrived, f32[8,2,256]{2,1,0:T(2,128)S(1)} %all_to_all.15.refs_0_.refs_1_.refs_5_.gathered, f32[8,256]{1,0:T(8,128)S(1)} %get-tuple-element.24.refs_6_.residual, f32[8,256]{1,0:T(8,128)S(1)} %get-tuple-element.26.direction, ...), custom_call_target="tpu_custom_call" | custom-call | tf_op jit(solution)/shard_map/last/pallas_call | solution.py:308
Async XLA Ops:
  1.3 12.1 %copy-start = (f32[1,1,16,256,256]{4,3,2,1,0:T(8,128)S(1)}, f32[1,1,16,256,256]{4,3,2,1,0:T(8,128)}, u32[]{:S(2)}) copy-start(f32[1,1,16,256,256]{4,3,2,1,0:T(8,128)} %refs_3_.3) | copy-start | bytes 12582916
  14.1 3.8 %copy-start.1 = (f32[8,256]{1,0:T(8,128)S(1)}, f32[8,256]{1,0:T(8,128)}, u32[]{:S(2)}) copy-start(f32[8,256]{1,0:T(8,128)} %refs_7_.1) | copy-start | bytes 24580
  14.1 3.2 %collective-permute-start.2 = (f32[18,1,128]{2,1,0:T(1,128)S(1)}, f32[18,1,128]{2,1,0:T(1,128)S(1)}, u32[]{:S(2)}, u32[]{:S(2)}) collective-permute-start(f32[18,1,128]{2,1,0:T(1,128)S(1)} %first.1.refs_0_), channel_id=1, source_target_pairs={{0,3},{1,2},{2,1},{3,0},{4,7},{5,6},{6,5},{7,4},{8,11},{9,10},{10,... | collective-permute-start | bytes 27656 | tf_op jit(solution)/shard_map/ppermute | solution.py:234
  14.1 3.7 %collective-permute-start.1 = (f32[18,1,128]{2,1,0:T(1,128)S(1)}, f32[18,1,128]{2,1,0:T(1,128)S(1)}, u32[]{:S(2)}, u32[]{:S(2)}) collective-permute-start(f32[18,1,128]{2,1,0:T(1,128)S(1)} %first.1.refs_0_), channel_id=1, source_target_pairs={{0,2},{1,3},{2,0},{3,1},{4,6},{5,7},{6,4},{7,5},{8,10},{9,11},{10,... | collective-permute-start | bytes 27656 | tf_op jit(solution)/shard_map/ppermute | solution.py:234
  15.7 2.2 %collective-permute-start = (f32[18,1,128]{2,1,0:T(1,128)S(1)}, f32[18,1,128]{2,1,0:T(1,128)S(1)}, u32[]{:S(2)}, u32[]{:S(2)}) collective-permute-start(f32[18,1,128]{2,1,0:T(1,128)S(1)} %first.1.refs_0_), channel_id=1, source_target_pairs={{0,1},{1,0},{2,3},{3,2},{4,5},{5,4},{6,7},{7,6},{8,9},{9,8},{10,11... | collective-permute-start | bytes 27656 | tf_op jit(solution)/shard_map/ppermute | solution.py:234
  27.9 3.2 %collective-permute-start.5 = (f32[19,1,128]{2,1,0:T(1,128)S(1)}, f32[19,1,128]{2,1,0:T(1,128)S(1)}, u32[]{:S(2)}, u32[]{:S(2)}) collective-permute-start(f32[19,1,128]{2,1,0:T(1,128)S(1)} %get-tuple-element.23.refs_0_), channel_id=1, source_target_pairs={{0,3},{1,2},{2,1},{3,0},{4,7},{5,6},{6,5},{7,4},{8,11},{9,10},{10,... | collective-permute-start | bytes 29192 | tf_op jit(solution)/shard_map/ppermute | solution.py:234
  27.9 3.7 %collective-permute-start.4 = (f32[19,1,128]{2,1,0:T(1,128)S(1)}, f32[19,1,128]{2,1,0:T(1,128)S(1)}, u32[]{:S(2)}, u32[]{:S(2)}) collective-permute-start(f32[19,1,128]{2,1,0:T(1,128)S(1)} %get-tuple-element.23.refs_0_), channel_id=1, source_target_pairs={{0,2},{1,3},{2,0},{3,1},{4,6},{5,7},{6,4},{7,5},{8,10},{9,11},{10,... | collective-permute-start | bytes 29192 | tf_op jit(solution)/shard_map/ppermute | solution.py:234
  29.4 2.2 %collective-permute-start.3 = (f32[19,1,128]{2,1,0:T(1,128)S(1)}, f32[19,1,128]{2,1,0:T(1,128)S(1)}, u32[]{:S(2)}, u32[]{:S(2)}) collective-permute-start(f32[19,1,128]{2,1,0:T(1,128)S(1)} %get-tuple-element.23.refs_0_), channel_id=1, source_target_pairs={{0,1},{1,0},{2,3},{3,2},{4,5},{5,4},{6,7},{7,6},{8,9},{9,8},{10,11... | collective-permute-start | bytes 29192 | tf_op jit(solution)/shard_map/ppermute | solution.py:234

commit v6 on v5

--- a/solution.py
+++ b/solution.py
@@ -27,7 +27,7 @@
         body,
         name=name,
         out_shape=[pltpu.VMEM(s, d) for s, d in out_shapes],
-        in_specs=in_specs or [vmem()] * len(args),
+        in_specs=[vmem()] * len(args) if in_specs is None else in_specs,
         out_specs=[vmem()] * len(out_shapes),
         scratch_shapes=list(scratch),
         compiler_params=pltpu.CompilerParams(vmem_limit_bytes=VMEM_LIMIT),
@@ -95,37 +95,34 @@
         out[k] = tiles[0, 0, k].T
 
 
-def start_body(group, cols, slots, first, *refs):
-    sources, (sent, spread_rows, spread_cols, gather_rows, gather_cols, own), held, sem = refs[:5], refs[5:11], refs[11:16], refs[16]
-    copies = [pltpu.make_async_copy(a, b, sem.at[i]) for i, (a, b) in enumerate(zip(sources, held))]
-    for copy in copies:
-        copy.start()
-
-    def place(index):
-        return jnp.where(index >= first, index - first, index - first + group)
-
-    mine = lax.broadcasted_iota(jnp.int32, own.shape, 0) == place(lax.axis_index("col"))
+def own_body(group, first, own):
+    mine = lax.broadcasted_iota(jnp.int32, own.shape, 0) == turn(lax.axis_index("col"), group, first)
     own[...] = jnp.where(mine, 1.0, 0.0)
-    for copy in copies:
-        copy.wait()
-    side, weights, count, rows_of, cols_of = held
+
+
+def turn(index, group, first):
+    return jnp.where(index >= first, index - first, index - first + group)
+
+
+def start_body(group, cols, slots, first, side, weights, count, rows_of, cols_of, own, sent, spread_rows, spread_cols, gather_rows, gather_cols):
     both = jnp.concatenate([side[...], weights[...]], axis=0)
     sent[...] = jnp.broadcast_to(both[None], sent.shape)
 
-    def tables(spread, gather, extent, index):
+    def tables(spread, gather, extent, indices):
         term = lax.broadcasted_iota(jnp.int32, (extent, LANES), 0)
         slot = lax.broadcasted_iota(jnp.int32, gather.shape, 1) // 8
         at = lax.broadcasted_iota(jnp.int32, gather.shape, 0)
         target = jnp.full(gather.shape, -1, jnp.int32)
         for k in range(slots):
-            source = jnp.where(k < count[0, 0], index[k], -1)
+            index = indices[:, k : k + 1]
+            source = jnp.where(k < count[0, 0], index, -1)
             one = jnp.where(term == source, 1.0, 0.0)
             spread[:, pl.ds(k * LANES, LANES)] = jnp.concatenate([one] * 3, axis=0).astype(BF16)
-            target = jnp.where(slot == k, index[k], target)
+            target = jnp.where(slot == k, index, target)
         gather[...] = jnp.where(at == target, 1.0, 0.0).astype(BF16)
 
-    tables(spread_rows, gather_rows, group, [place(rows_of[0, 0, k]) for k in range(slots)])
-    tables(spread_cols, gather_cols, cols, [cols_of[0, 0, k] for k in range(slots)])
+    tables(spread_rows, gather_rows, group, turn(rows_of[0], group, first))
+    tables(spread_cols, gather_cols, cols, cols_of[0])
 
 
 def first_body(slots, cols, gathered, tiles, spread, gather, out):
@@ -248,7 +245,15 @@
     starts = [peers * f // 8 for f in FIRST]
     work = dict(flops=8 * long * size, moved=0)
 
-    sent, spread_rows, spread_cols, gather_rows, gather_cols, own = call(
+    (own,) = call(
+        lambda *refs: own_body(group, starts[0], *refs),
+        "own",
+        [((group, LANES), F32)],
+        (),
+        in_specs=[],
+        flops=1 << 34,
+    )
+    sent, spread_rows, spread_cols, gather_rows, gather_cols = call(
         lambda *refs: start_body(group, cols, slots, starts[0], *refs),
         "start",
         [
@@ -257,18 +262,9 @@
             ((3 * cols, slots * LANES), BF16),
             ((group, slots * 8), BF16),
             ((cols, slots * 8), BF16),
-            ((group, LANES), F32),
         ],
-        (stay(right_side), stay(precond), block_count, stay(block_rows), stay(block_cols)),
-        in_specs=[pl.BlockSpec(memory_space=pl.ANY)] * 5,
-        scratch=[
-            pltpu.VMEM(right_side.shape, F32),
-            pltpu.VMEM(precond.shape, F32),
-            pltpu.SMEM(block_count.shape, jnp.int32),
-            pltpu.SMEM(block_rows.shape, jnp.int32),
-            pltpu.SMEM(block_cols.shape, jnp.int32),
-            pltpu.SemaphoreType.DMA((5,)),
-        ],
+        (right_side, precond, block_count, block_rows, block_cols, own),
+        in_specs=[vmem(), vmem(), pl.BlockSpec(memory_space=pltpu.SMEM), vmem(), vmem(), vmem()],
         flops=1 << 34,
         moved=100 << 20,
     )

time: 41.6 us -> 41 us (0.986)
  Pallas kernels: 5.68 us -> 4.91 us
    pallas_call x6 -> x7, Pallas kernels: 4.94 us -> 4.17 us  [call(): pl.pallas_call(body, name=name, out_shape=[pltpu.VMEM(s, d) for s, d in o...]
where the time goes in v6:
time: 41 us; the launch traced here: 40.8 us
  blocking collectives  28 us (68%)
  Pallas kernels  4.91 us (12%)
  starting transfers between devices  3.77 us (9%)
  waiting for transfers between devices  2.62 us (6%)
  between operations  1.41 us (3%)
    all_to_all x3, blocking collectives, exchange(): lax.all_to_all(value, 'col', 0, 0, tiled=True, axis_index_groups=[order])  28 us
    pallas_call x7, Pallas kernels, call(): pl.pallas_call(body, name=name, out_shape=[pltpu.VMEM(s, d) for s, d in o...  4.17 us
    ppermute x6, starting transfers between devices, share(): moved.append(lax.ppermute(value, axis, [(i, i ^ s) for i in range(size)]))  3.77 us
    ppermute x6, waiting for transfers between devices, share(): moved.append(lax.ppermute(value, axis, [(i, i ^ s) for i in range(size)]))  2.62 us
  transfers between devices with their start and end apart: 6, of which 4 were waited for; matrix products, arithmetic and copies ran while one was open for 0% of the time, Pallas kernels for 3%

profile of v6, /device:TPU:0, one launch (start us, length us, event | category | flops | bytes accessed | tf_op | source)
XLA Modules:
  0.0 40.8 jit_solution(7232561545840879897)
XLA Ops:
  0.6 0.0 copy-start.5
  0.6 0.0 copy-start.4
  0.7 0.0 copy-start.3
  0.7 0.0 copy-start.2
  1.3 0.0 copy-done.5
  1.4 0.0 copy-done.4
  1.4 0.0 copy-done.3
  1.4 0.0 copy-done.2
  1.4 0.0 copy-start
  1.4 0.2 start.1
  1.6 11.2 %all_to_all.15.refs_0_.refs_1_.refs_5_.gathered = f32[8,2,256]{2,1,0:T(2,128)S(1)} all-to-all(f32[8,2,256]{2,1,0:T(2,128)S(1)} %get-tuple-element.15), channel_id=1, replica_groups={{20,24,28,0,4,8,12,16},{21,25,29,1,5,9,13,17},{22,26,30,2,6,10,14,18},{..., dimensions={0} | all-to-all | bytes 32768 | tf_op jit(solution)/shard_map/all_to_all | solution.py:225
  12.8 0.0 copy-done
  12.8 0.7 %first.1.refs_0_ = f32[18,1,128]{2,1,0:T(1,128)S(1)} custom-call(f32[8,2,256]{2,1,0:T(2,128)S(1)} %all_to_all.15.refs_0_.refs_1_.refs_5_.gathered, f32[1,1,16,256,256]{4,3,2,1,0:T(8,128)S(1)} %copy-done, bf16[24,2048]{1,0:T(8,128)(2,1)S(1)} %get-tuple-element.16.refs_2_.refs_4_, bf16[8,128]{1,0:T(8,128)(2,1)S(1)} %get-tuple-element.17.refs_3_.refs_5_), custom_call_target="tpu_custom_call" | custom-call | flops 8388608 | tf_op jit(solution)/shard_map/first/pallas_call | solution.py:26
  13.5 0.1 collective-permute-start.2
  13.6 1.6 %collective-permute-start.1 = (f32[18,1,128]{2,1,0:T(1,128)S(1)}, f32[18,1,128]{2,1,0:T(1,128)S(1)}, u32[]{:S(2)}, u32[]{:S(2)}) collective-permute-start(f32[18,1,128]{2,1,0:T(1,128)S(1)} %first.1.refs_0_), channel_id=1, source_target_pairs={{0,2},{1,3},{2,0},{3,1},{4,6},{5,7},{6,4},{7,5},{8,10},{9,11},{10,... | collective-permute-start | bytes 27656 | tf_op jit(solution)/shard_map/ppermute | solution.py:231
  15.1 0.3 collective-permute-start
  15.4 1.1 %flip.1.refs_5_.refs_8_ = f32[16,256,256]{2,1,0:T(8,128)S(1)} custom-call(f32[1,1,16,256,256]{4,3,2,1,0:T(8,128)S(1)} %copy-done), custom_call_target="tpu_custom_call" | custom-call | flops 1073741824 | tf_op jit(solution)/shard_map/flip/pallas_call | solution.py:26
  16.6 0.1 collective-permute-done.2.refs_3_
  16.7 0.6 %collective-permute-done.1.refs_2_ = f32[18,1,128]{2,1,0:T(1,128)S(1)} collective-permute-done((f32[18,1,128]{2,1,0:T(1,128)S(1)}, f32[18,1,128]{2,1,0:T(1,128)S(1)}, u32[]{:S(2)}, u32[]{:S(2)}) %collective-permute-start.1) | collective-permute-done | bytes 9248 | tf_op jit(solution)/shard_map/ppermute | solution.py:231
  17.3 0.0 collective-permute-done.refs_1_
  17.3 0.7 %second.1 = (f32[18,128]{1,0:T(8,128)S(1)}, f32[136,1,128]{2,1,0:T(1,128)S(1)}) custom-call(f32[18,1,128]{2,1,0:T(1,128)S(1)} %first.1.refs_0_, f32[18,1,128]{2,1,0:T(1,128)S(1)} %collective-permute-done.refs_1_, f32[18,1,128]{2,1,0:T(1,128)S(1)} %collective-permute-done.1.refs_2_, f32[18,1,128]{2,1,0:T(1,128)S(1)} %collective-permute-done.2.refs_3_, ...), custom_call_target="tpu_custom_call" | custom-call | flops 8388608 | tf_op jit(solution)/shard_map/second/pallas_call | solution.py:26
  18.0 8.6 %all_to_all.16.refs_0_ = f32[136,1,128]{2,1,0:T(1,128)S(1)} all-to-all(f32[136,1,128]{2,1,0:T(1,128)S(1)} %get-tuple-element.20), channel_id=1, replica_groups={{20,24,28,0,4,8,12,16},{21,25,29,1,5,9,13,17},{22,26,30,2,6,10,14,18},{..., dimensions={0} | all-to-all | bytes 139264 | tf_op jit(solution)/shard_map/all_to_all | solution.py:225
  26.6 0.7 %third.1 = (f32[19,1,128]{2,1,0:T(1,128)S(1)}, f32[8,256]{1,0:T(8,128)S(1)}, f32[1,128]{1,0:T(1,128)S(1)}) custom-call(f32[136,1,128]{2,1,0:T(1,128)S(1)} %all_to_all.16.refs_0_, f32[8,2,256]{2,1,0:T(2,128)S(1)} %all_to_all.15.refs_0_.refs_1_.refs_5_.gathered, f32[18,128]{1,0:T(8,128)S(1)} %get-tuple-element.21.refs_2_.refs_4_, ...), custom_call_target="tpu_custom_call" | custom-call | flops 8388608 | tf_op jit(solution)/shard_map/third/pallas_call | solution.py:26
  27.3 0.0 collective-permute-start.5
  27.3 1.6 %collective-permute-start.4 = (f32[19,1,128]{2,1,0:T(1,128)S(1)}, f32[19,1,128]{2,1,0:T(1,128)S(1)}, u32[]{:S(2)}, u32[]{:S(2)}) collective-permute-start(f32[19,1,128]{2,1,0:T(1,128)S(1)} %get-tuple-element.22.refs_0_), channel_id=1, source_target_pairs={{0,2},{1,3},{2,0},{3,1},{4,6},{5,7},{6,4},{7,5},{8,10},{9,11},{10,... | collective-permute-start | bytes 29192 | tf_op jit(solution)/shard_map/ppermute | solution.py:231
  28.9 0.3 collective-permute-start.3
  29.2 1.3 %collective-permute-done.5.refs_3_ = f32[19,1,128]{2,1,0:T(1,128)S(1)} collective-permute-done((f32[19,1,128]{2,1,0:T(1,128)S(1)}, f32[19,1,128]{2,1,0:T(1,128)S(1)}, u32[]{:S(2)}, u32[]{:S(2)}) %collective-permute-start.5) | collective-permute-done | bytes 9760 | tf_op jit(solution)/shard_map/ppermute | solution.py:231
  30.5 0.6 %collective-permute-done.4.refs_2_ = f32[19,1,128]{2,1,0:T(1,128)S(1)} collective-permute-done((f32[19,1,128]{2,1,0:T(1,128)S(1)}, f32[19,1,128]{2,1,0:T(1,128)S(1)}, u32[]{:S(2)}, u32[]{:S(2)}) %collective-permute-start.4) | collective-permute-done | bytes 9760 | tf_op jit(solution)/shard_map/ppermute | solution.py:231
  31.1 0.0 collective-permute-done.3.refs_1_
  31.1 0.7 %fourth.1 = (f32[8,3,128]{2,1,0:T(4,128)S(1)}, f32[8,256]{1,0:T(8,128)S(1)}, f32[2,128]{1,0:T(2,128)S(1)}) custom-call(f32[19,1,128]{2,1,0:T(1,128)S(1)} %get-tuple-element.22.refs_0_, f32[19,1,128]{2,1,0:T(1,128)S(1)} %collective-permute-done.3.refs_1_, f32[19,1,128]{2,1,0:T(1,128)S(1)} %collective-permute-done.4.refs_2_, ...), custom_call_target="tpu_custom_call" | custom-call | flops 8388608 | tf_op jit(solution)/shard_map/fourth/pallas_call | solution.py:26
  31.8 8.2 %all_to_all.17.arrived = f32[8,3,128]{2,1,0:T(4,128)S(1)} all-to-all(f32[8,3,128]{2,1,0:T(4,128)S(1)} %get-tuple-element.24), channel_id=1, replica_groups={{20,24,28,0,4,8,12,16},{21,25,29,1,5,9,13,17},{22,26,30,2,6,10,14,18},{..., dimensions={0} | all-to-all | bytes 24576 | tf_op jit(solution)/shard_map/all_to_all | solution.py:225
  40.0 0.7 %last.1 = (f32[1,256]{1,0:T(1,128)}, f32[1,256]{1,0:T(1,128)}) custom-call(f32[8,3,128]{2,1,0:T(4,128)S(1)} %all_to_all.17.arrived, f32[8,2,256]{2,1,0:T(2,128)S(1)} %all_to_all.15.refs_0_.refs_1_.refs_5_.gathered, f32[8,256]{1,0:T(8,128)S(1)} %get-tuple-element.23.refs_6_.residual, f32[8,256]{1,0:T(8,128)S(1)} %get-tuple-element.25.direction, ...), custom_call_target="tpu_custom_call" | custom-call | tf_op jit(solution)/shard_map/last/pallas_call | solution.py:304
  (3 shorter events, 0.0 us)
Async XLA Ops:
  0.6 0.7 %copy-start.5 = (s32[1,1,16]{2,1,0:T(1,128)S(1)}, s32[1,1,16]{2,1,0:T(1,128)}, u32[]{:S(2)}) copy-start(s32[1,1,16]{2,1,0:T(1,128)} %refs_4_.2) | copy-start | bytes 196
  0.6 0.7 %copy-start.4 = (s32[1,1,16]{2,1,0:T(1,128)S(1)}, s32[1,1,16]{2,1,0:T(1,128)}, u32[]{:S(2)}) copy-start(s32[1,1,16]{2,1,0:T(1,128)} %refs_3_.2) | copy-start | bytes 196
  0.7 0.7 %copy-start.3 = (f32[1,256]{1,0:T(1,128)S(1)}, f32[1,256]{1,0:T(1,128)}, u32[]{:S(2)}) copy-start(f32[1,256]{1,0:T(1,128)} %refs_1_.2) | copy-start | bytes 3076
  0.7 0.7 %copy-start.2 = (f32[1,256]{1,0:T(1,128)S(1)}, f32[1,256]{1,0:T(1,128)}, u32[]{:S(2)}) copy-start(f32[1,256]{1,0:T(1,128)} %refs_0_.1) | copy-start | bytes 3076
  1.4 11.4 %copy-start = (f32[1,1,16,256,256]{4,3,2,1,0:T(8,128)S(1)}, f32[1,1,16,256,256]{4,3,2,1,0:T(8,128)}, u32[]{:S(2)}) copy-start(f32[1,1,16,256,256]{4,3,2,1,0:T(8,128)} %refs_3_.3) | copy-start | bytes 12582916
  13.5 3.8 %copy-start.1 = (f32[8,256]{1,0:T(8,128)S(1)}, f32[8,256]{1,0:T(8,128)}, u32[]{:S(2)}) copy-start(f32[8,256]{1,0:T(8,128)} %refs_7_.1) | copy-start | bytes 24580
  13.5 3.2 %collective-permute-start.2 = (f32[18,1,128]{2,1,0:T(1,128)S(1)}, f32[18,1,128]{2,1,0:T(1,128)S(1)}, u32[]{:S(2)}, u32[]{:S(2)}) collective-permute-start(f32[18,1,128]{2,1,0:T(1,128)S(1)} %first.1.refs_0_), channel_id=1, source_target_pairs={{0,3},{1,2},{2,1},{3,0},{4,7},{5,6},{6,5},{7,4},{8,11},{9,10},{10,... | collective-permute-start | bytes 27656 | tf_op jit(solution)/shard_map/ppermute | solution.py:231
  13.6 3.7 %collective-permute-start.1 = (f32[18,1,128]{2,1,0:T(1,128)S(1)}, f32[18,1,128]{2,1,0:T(1,128)S(1)}, u32[]{:S(2)}, u32[]{:S(2)}) collective-permute-start(f32[18,1,128]{2,1,0:T(1,128)S(1)} %first.1.refs_0_), channel_id=1, source_target_pairs={{0,2},{1,3},{2,0},{3,1},{4,6},{5,7},{6,4},{7,5},{8,10},{9,11},{10,... | collective-permute-start | bytes 27656 | tf_op jit(solution)/shard_map/ppermute | solution.py:231
  15.1 2.2 %collective-permute-start = (f32[18,1,128]{2,1,0:T(1,128)S(1)}, f32[18,1,128]{2,1,0:T(1,128)S(1)}, u32[]{:S(2)}, u32[]{:S(2)}) collective-permute-start(f32[18,1,128]{2,1,0:T(1,128)S(1)} %first.1.refs_0_), channel_id=1, source_target_pairs={{0,1},{1,0},{2,3},{3,2},{4,5},{5,4},{6,7},{7,6},{8,9},{9,8},{10,11... | collective-permute-start | bytes 27656 | tf_op jit(solution)/shard_map/ppermute | solution.py:231
  27.3 3.2 %collective-permute-start.5 = (f32[19,1,128]{2,1,0:T(1,128)S(1)}, f32[19,1,128]{2,1,0:T(1,128)S(1)}, u32[]{:S(2)}, u32[]{:S(2)}) collective-permute-start(f32[19,1,128]{2,1,0:T(1,128)S(1)} %get-tuple-element.22.refs_0_), channel_id=1, source_target_pairs={{0,3},{1,2},{2,1},{3,0},{4,7},{5,6},{6,5},{7,4},{8,11},{9,10},{10,... | collective-permute-start | bytes 29192 | tf_op jit(solution)/shard_map/ppermute | solution.py:231
  27.3 3.7 %collective-permute-start.4 = (f32[19,1,128]{2,1,0:T(1,128)S(1)}, f32[19,1,128]{2,1,0:T(1,128)S(1)}, u32[]{:S(2)}, u32[]{:S(2)}) collective-permute-start(f32[19,1,128]{2,1,0:T(1,128)S(1)} %get-tuple-element.22.refs_0_), channel_id=1, source_target_pairs={{0,2},{1,3},{2,0},{3,1},{4,6},{5,7},{6,4},{7,5},{8,10},{9,11},{10,... | collective-permute-start | bytes 29192 | tf_op jit(solution)/shard_map/ppermute | solution.py:231
  28.9 2.2 %collective-permute-start.3 = (f32[19,1,128]{2,1,0:T(1,128)S(1)}, f32[19,1,128]{2,1,0:T(1,128)S(1)}, u32[]{:S(2)}, u32[]{:S(2)}) collective-permute-start(f32[19,1,128]{2,1,0:T(1,128)S(1)} %get-tuple-element.22.refs_0_), channel_id=1, source_target_pairs={{0,1},{1,0},{2,3},{3,2},{4,5},{5,4},{6,7},{7,6},{8,9},{9,8},{10,11... | collective-permute-start | bytes 29192 | tf_op jit(solution)/shard_map/ppermute | solution.py:231

commit v7 on v6

--- a/solution.py
+++ b/solution.py
@@ -9,6 +9,7 @@
 LANES = 128
 FLIP = 1 << 30
 FIRST = (5, 5, 5)
+SHARE = 2
 VMEM_LIMIT = 16 << 20
 F32 = jnp.float32
 BF16 = jnp.bfloat16
@@ -42,6 +43,11 @@
     return jnp.concatenate([high, middle, rest - middle], axis=0).astype(BF16)
 
 
+def split2(x):
+    high = x.astype(BF16).astype(F32)
+    return jnp.concatenate([high, x - high], axis=0).astype(BF16)
+
+
 def lane_sum(row):
     return jnp.sum(row, axis=1, keepdims=True)
 
@@ -68,31 +74,71 @@
     return jnp.concatenate([x[h * rows : (h + 1) * rows] for h in range(size // LANES)], axis=1)
 
 
-def block_product(spread, gather, vector, tiles, slots):
+def block_product(spread, gather, vector, tiles, slots, table=None, high=None, low=None):
     terms = split3(vector)
     size = vector.shape[1]
+    others = 0 if high is None else high.shape[0] // size
+    if others:
+        placed = jnp.dot(table[...], split2(vector), preferred_element_type=F32).astype(BF16)
+        step = placed.shape[0] // others
+        matrix = jnp.zeros((step, size), F32)
+    turns = slots // 2
     parts = []
-    for k in range(0, slots, 2):
-        table = spread[:, k * LANES : (k + 2) * LANES]
-        wide = lax.dot_general(terms, table, (((0,), (0,)), ((), ())), preferred_element_type=F32)
+    for n in range(turns):
+        spread_pair = spread[:, 2 * n * LANES : (2 * n + 2) * LANES]
+        wide = lax.dot_general(terms, spread_pair, (((0,), (0,)), ((), ())), preferred_element_type=F32)
+        for k in range(others * n // turns, others * (n + 1) // turns):
+            left = placed[k * step : (k + 1) * step]
+            here = slice(k * size, (k + 1) * size)
+            matrix += jnp.dot(left, high[here, :], preferred_element_type=F32)
+            matrix += jnp.dot(left, low[here, :], preferred_element_type=F32)
         for m in range(2):
             here = wide[:, m * LANES : (m + 1) * LANES]
             row = []
             for h in range(0, size, LANES):
-                product = tiles[k + m, :, h : h + LANES] * here
+                product = tiles[2 * n + m, :, h : h + LANES] * here
                 row.append(jnp.sum(product.reshape(size // 8, 8, LANES), axis=0))
             parts.append(jnp.concatenate(row, axis=1))
     parts = jnp.concatenate(parts, axis=0)
     count = parts.shape[0]
     terms = split3(parts)
-    total = jnp.dot(gather[...], terms[:count], preferred_element_type=F32)
-    total += jnp.dot(gather[...], terms[count : 2 * count], preferred_element_type=F32)
-    return total + jnp.dot(gather[...], terms[2 * count :], preferred_element_type=F32)
-
-
-def flip_body(tiles, out):
-    for k in range(out.shape[0]):
-        out[k] = tiles[0, 0, k].T
+    gather = gather[:, :count]
+    total = jnp.dot(gather, terms[:count], preferred_element_type=F32)
+    total += jnp.dot(gather, terms[count : 2 * count], preferred_element_type=F32)
+    total += jnp.dot(gather, terms[2 * count :], preferred_element_type=F32)
+    if others:
+        total += matrix[: step // 2] + matrix[step // 2 :]
+    return total
+
+
+def store_split(high, low, here, tile):
+    upper = tile.astype(BF16)
+    high[here, :] = upper
+    low[here, :] = (tile - upper.astype(F32)).astype(BF16)
+
+
+def flip_body(plain, group, cols, first, tiles, count, rows_of, cols_of, spread_cols, gather_rows, to_cols, to_rows, flipped, high, low, high_t, low_t):
+    slots, size = tiles.shape[2], tiles.shape[3]
+    for k in range(plain):
+        flipped[k] = tiles[0, 0, k].T
+    for k in range(plain, slots):
+        here = pl.ds((k - plain) * size, size)
+        store_split(high, low, here, tiles[0, 0, k])
+        store_split(high_t, low_t, here, tiles[0, 0, k].T)
+    rows, columns = turn(rows_of[0], group, first), cols_of[0]
+    spread_table(spread_cols, columns, count, plain)
+    gather_table(gather_rows, rows)
+    for out, targets, sources, target, source in (
+        (to_cols, cols, group, columns, rows),
+        (to_rows, group, cols, rows, columns),
+    ):
+        r = lax.broadcasted_iota(jnp.int32, (2 * targets, 2 * sources), 0)
+        q = lax.broadcasted_iota(jnp.int32, (2 * targets, 2 * sources), 1)
+        for k in range(plain, slots):
+            t = jnp.where(k < count[0, 0], target[:, k : k + 1], -1 - targets)
+            s = source[:, k : k + 1]
+            hit = ((r == t) & (q == s)) | ((r == targets + t) & (q == sources + s))
+            out[pl.ds((k - plain) * 2 * targets, 2 * targets), :] = jnp.where(hit, 1.0, 0.0).astype(BF16)
 
 
 def own_body(group, first, own):
@@ -104,25 +150,28 @@
     return jnp.where(index >= first, index - first, index - first + group)
 
 
-def start_body(group, cols, slots, first, side, weights, count, rows_of, cols_of, own, sent, spread_rows, spread_cols, gather_rows, gather_cols):
+def spread_table(out, indices, count, slots):
+    term = lax.broadcasted_iota(jnp.int32, (out.shape[0] // 3, LANES), 0)
+    for k in range(slots):
+        source = jnp.where(k < count[0, 0], indices[:, k : k + 1], -1)
+        one = jnp.where(term == source, 1.0, 0.0)
+        out[:, pl.ds(k * LANES, LANES)] = jnp.concatenate([one] * 3, axis=0).astype(BF16)
+
+
+def gather_table(out, indices):
+    slot = lax.broadcasted_iota(jnp.int32, out.shape, 1) // 8
+    at = lax.broadcasted_iota(jnp.int32, out.shape, 0)
+    target = jnp.full(out.shape, -1, jnp.int32)
+    for k in range(out.shape[1] // 8):
+        target = jnp.where(slot == k, indices[:, k : k + 1], target)
+    out[...] = jnp.where(at == target, 1.0, 0.0).astype(BF16)
+
+
+def start_body(group, slots, first, side, weights, count, rows_of, cols_of, own, sent, spread_rows, gather_cols):
     both = jnp.concatenate([side[...], weights[...]], axis=0)
     sent[...] = jnp.broadcast_to(both[None], sent.shape)
-
-    def tables(spread, gather, extent, indices):
-        term = lax.broadcasted_iota(jnp.int32, (extent, LANES), 0)
-        slot = lax.broadcasted_iota(jnp.int32, gather.shape, 1) // 8
-        at = lax.broadcasted_iota(jnp.int32, gather.shape, 0)
-        target = jnp.full(gather.shape, -1, jnp.int32)
-        for k in range(slots):
-            index = indices[:, k : k + 1]
-            source = jnp.where(k < count[0, 0], index, -1)
-            one = jnp.where(term == source, 1.0, 0.0)
-            spread[:, pl.ds(k * LANES, LANES)] = jnp.concatenate([one] * 3, axis=0).astype(BF16)
-            target = jnp.where(slot == k, index, target)
-        gather[...] = jnp.where(at == target, 1.0, 0.0).astype(BF16)
-
-    tables(spread_rows, gather_rows, group, turn(rows_of[0], group, first))
-    tables(spread_cols, gather_cols, cols, cols_of[0])
+    spread_table(spread_rows, turn(rows_of[0], group, first), count, slots)
+    gather_table(gather_cols, cols_of[0])
 
 
 def first_body(slots, cols, gathered, tiles, spread, gather, out):
@@ -140,21 +189,21 @@
     return (a + b) + (c + d)
 
 
-def second_body(slots, peers, p0, p1, p2, p3, scaling, flipped, spread, gather, total, out):
+def second_body(slots, peers, p0, p1, p2, p3, scaling, flipped, spread, gather, table, high, low, total, out):
     summed = gather4((p0, p1, p2, p3))
     total[...] = summed
     cols, size = scaling.shape
     lifted = take(summed, cols, size)
     weighted = scaling[...] * lifted
     inner = fold(row_sum(weighted * lifted))
-    rows = block_product(spread, gather, weighted, flipped, slots)
+    rows = block_product(spread, gather, weighted, flipped, slots, table, high, low)
     length = out.shape[0] // peers
     for j in range(peers):
         put(out, j * length, rows)
         put(out, (j + 1) * length - 1, inner)
 
 
-def third_body(slots, cols, arrived, gathered, total, tiles, spread, gather, out, residual_out, alpha_out):
+def third_body(slots, cols, arrived, gathered, total, tiles, spread, gather, table, high, low, out, residual_out, alpha_out):
     residual, weights = gathered[:, 0, :], gathered[:, 1, :]
     z = weights * residual
     group, size = residual.shape
@@ -175,10 +224,10 @@
     put(out, count, fold(row_sum(later * z1)))
     put(out, count + 1, fold(row_sum(z1 * z1)))
     put(out, count + 2, fold(row_sum(z1 * z)))
-    put(out, 0, block_product(spread, gather, z1, tiles.at[0, 0], slots))
-
-
-def fourth_body(slots, by, p0, p1, p2, p3, total, gathered, residual, scaling, flipped, spread, gather, out, direction_out, scalars):
+    put(out, 0, block_product(spread, gather, z1, tiles.at[0, 0], slots, table, high, low))
+
+
+def fourth_body(slots, by, p0, p1, p2, p3, total, gathered, residual, scaling, flipped, spread, gather, table, high, low, out, direction_out, scalars):
     summed = gather4((p0, p1, p2, p3))
     cols, size = scaling.shape
     count = cols * (size // LANES)
@@ -190,7 +239,7 @@
     lifted = take(summed, cols, size) + beta * take(total[...], cols, size)
     weighted = scaling[...] * lifted
     inner = fold(row_sum(weighted * lifted))
-    rows = block_product(spread, gather, weighted, flipped, slots)
+    rows = block_product(spread, gather, weighted, flipped, slots, table, high, low)
     peers = out.shape[0]
     for h, piece in enumerate(pieces_of(rows)):
         out[:, h, :] = turned(piece, by)
@@ -253,16 +302,10 @@
         in_specs=[],
         flops=1 << 34,
     )
-    sent, spread_rows, spread_cols, gather_rows, gather_cols = call(
-        lambda *refs: start_body(group, cols, slots, starts[0], *refs),
+    sent, spread_rows, gather_cols = call(
+        lambda *refs: start_body(group, slots, starts[0], *refs),
         "start",
-        [
-            ((peers, 2, size), F32),
-            ((3 * group, slots * LANES), BF16),
-            ((3 * cols, slots * LANES), BF16),
-            ((group, slots * 8), BF16),
-            ((cols, slots * 8), BF16),
-        ],
+        [((peers, 2, size), F32), ((3 * group, slots * LANES), BF16), ((cols, slots * 8), BF16)],
         (right_side, precond, block_count, block_rows, block_cols, own),
         in_specs=[vmem(), vmem(), pl.BlockSpec(memory_space=pltpu.SMEM), vmem(), vmem(), vmem()],
         flops=1 << 34,
@@ -276,28 +319,44 @@
         (gathered, blocks, spread_rows, gather_cols),
         **work,
     )
-    (flipped,) = call(flip_body, "flip", [((slots, size, size), F32)], (blocks,), flops=FLIP)
+    plain = (slots - slots * SHARE // 16) // 2 * 2
+    rest = slots - plain
+    spread_cols, gather_rows, to_cols, to_rows, flipped, high, low, high_t, low_t = call(
+        lambda *refs: flip_body(plain, group, cols, starts[0], *refs),
+        "flip",
+        [
+            ((3 * cols, plain * LANES), BF16),
+            ((group, plain * 8), BF16),
+            ((rest * 2 * cols, 2 * group), BF16),
+            ((rest * 2 * group, 2 * cols), BF16),
+            ((plain, size, size), F32),
+        ]
+        + [((rest * size, size), BF16)] * 4,
+        (blocks, block_count, block_rows, block_cols),
+        in_specs=[vmem(), pl.BlockSpec(memory_space=pltpu.SMEM), vmem(), vmem()],
+        flops=FLIP,
+    )
     length = group * pieces + 1
     total, sent = call(
-        lambda *refs: second_body(slots, peers, *refs),
+        lambda *refs: second_body(plain, peers, *refs),
         "second",
         [((cols * pieces + 2, LANES), F32), ((peers * length, 1, LANES), F32)],
-        (*share(mine, "row", groups), scaling, flipped, spread_cols, gather_rows),
+        (*share(mine, "row", groups), scaling, flipped, spread_cols, gather_rows, to_rows, high_t, low_t),
         **work,
     )
     arrived = exchange(sent, peers, starts[1])
     mine, residual, alpha = call(
-        lambda *refs: third_body(slots, cols, *refs),
+        lambda *refs: third_body(plain, cols, *refs),
         "third",
         [((cols * pieces + 3, 1, LANES), F32), ((group, size), F32), ((1, LANES), F32)],
-        (arrived, gathered, total, blocks, spread_rows, gather_cols),
+        (arrived, gathered, total, blocks, spread_rows, gather_cols, to_cols, high, low),
         **work,
     )
     sent, direction, scalars = call(
-        lambda *refs: fourth_body(slots, starts[2] - starts[0], *refs),
+        lambda *refs: fourth_body(plain, starts[2] - starts[0], *refs),
         "fourth",
         [((peers, pieces + 1, LANES), F32), ((group, size), F32), ((2, LANES), F32)],
-        (*share(mine, "row", groups), total, gathered, residual, scaling, flipped, spread_cols, gather_rows),
+        (*share(mine, "row", groups), total, gathered, residual, scaling, flipped, spread_cols, gather_rows, to_rows, high_t, low_t),
         **work,
     )
     arrived = exchange(sent, peers, starts[2])

time: 41 us -> 40.9 us (level)
  transfers between devices with their start and end apart: 6 -> 6, of which waited for: 4 -> 3; matrix products, arithmetic and copies ran while one was open for 0% -> 0% of each run, Pallas kernels for 3% -> 3%
where the time goes in v7:
time: 40.9 us; the launch traced here: 40.6 us
  blocking collectives  28 us (68%)
  Pallas kernels  4.91 us (12%)
  starting transfers between devices  3.79 us (9%)
  waiting for transfers between devices  2.47 us (6%)
  between operations  1.43 us (3%)
    all_to_all x3, blocking collectives, exchange(): lax.all_to_all(value, 'col', 0, 0, tiled=True, axis_index_groups=[order])  28 us
    pallas_call x7, Pallas kernels, call(): pl.pallas_call(body, name=name, out_shape=[pltpu.VMEM(s, d) for s, d in o...  4.16 us
    ppermute x6, starting transfers between devices, share(): moved.append(lax.ppermute(value, axis, [(i, i ^ s) for i in range(size)]))  3.79 us
    ppermute x6, waiting for transfers between devices, share(): moved.append(lax.ppermute(value, axis, [(i, i ^ s) for i in range(size)]))  2.47 us
  transfers between devices with their start and end apart: 6, of which 3 were waited for; matrix products, arithmetic and copies ran while one was open for 0% of the time, Pallas kernels for 3%

profile of v7, /device:TPU:0, one launch (start us, length us, event | category | flops | bytes accessed | tf_op | source)
XLA Modules:
  0.0 40.6 jit_solution(863696541425125080)
XLA Ops:
  0.6 0.0 copy-start.3
  0.6 0.0 copy-start.2
  0.7 0.0 copy-start.5
  0.7 0.0 copy-start.4
  1.3 0.0 copy-done.3
  1.4 0.0 copy-done.2
  1.4 0.0 copy-done.5
  1.4 0.0 copy-done.4
  1.4 0.0 copy-start
  1.4 0.1 start.1
  1.5 11.2 %all_to_all.15.refs_0_.refs_1_.refs_5_.gathered = f32[8,2,256]{2,1,0:T(2,128)S(1)} all-to-all(f32[8,2,256]{2,1,0:T(2,128)S(1)} %get-tuple-element.22), channel_id=1, replica_groups={{20,24,28,0,4,8,12,16},{21,25,29,1,5,9,13,17},{22,26,30,2,6,10,14,18},{..., dimensions={0} | all-to-all | bytes 32768 | tf_op jit(solution)/shard_map/all_to_all | solution.py:274
  12.8 0.0 copy-done
  12.8 0.7 %first.1.refs_0_ = f32[18,1,128]{2,1,0:T(1,128)S(1)} custom-call(f32[8,2,256]{2,1,0:T(2,128)S(1)} %all_to_all.15.refs_0_.refs_1_.refs_5_.gathered, f32[1,1,16,256,256]{4,3,2,1,0:T(8,128)S(1)} %copy-done, bf16[24,2048]{1,0:T(8,128)(2,1)S(1)} %get-tuple-element.23.refs_2_.refs_4_, bf16[8,128]{1,0:T(8,128)(2,1)S(1)} %get-tuple-element.24.refs_3_.refs_5_), custom_call_target="tpu_custom_call" | custom-call | flops 8388608 | tf_op jit(solution)/shard_map/first/pallas_call | solution.py:27
  13.5 0.0 collective-permute-start.2
  13.5 1.6 %collective-permute-start.1 = (f32[18,1,128]{2,1,0:T(1,128)S(1)}, f32[18,1,128]{2,1,0:T(1,128)S(1)}, u32[]{:S(2)}, u32[]{:S(2)}) collective-permute-start(f32[18,1,128]{2,1,0:T(1,128)S(1)} %first.1.refs_0_), channel_id=1, source_target_pairs={{0,2},{1,3},{2,0},{3,1},{4,6},{5,7},{6,4},{7,5},{8,10},{9,11},{10,... | collective-permute-start | bytes 27656 | tf_op jit(solution)/shard_map/ppermute | solution.py:280
  15.0 0.3 collective-permute-start
  15.3 1.3 %flip.1 = (bf16[24,1792]{1,0:T(8,128)(2,1)S(1)}, bf16[8,112]{1,0:T(8,128)(2,1)S(1)}, bf16[32,16]{1,0:T(8,128)(2,1)S(1)}, bf16[32,16]{1,0:T(8,128)(2,1)S(1)}, f32...) custom-call(f32[1,1,16,256,256]{4,3,2,1,0:T(8,128)S(1)} %copy-done, ...), custom_call_target="tpu_custom_call" | custom-call | flops 1073741824 | tf_op jit(solution)/shard_map/flip/pallas_call | solution.py:27
  16.6 0.0 collective-permute-done.2.refs_3_
  16.6 0.6 %collective-permute-done.1.refs_2_ = f32[18,1,128]{2,1,0:T(1,128)S(1)} collective-permute-done((f32[18,1,128]{2,1,0:T(1,128)S(1)}, f32[18,1,128]{2,1,0:T(1,128)S(1)}, u32[]{:S(2)}, u32[]{:S(2)}) %collective-permute-start.1) | collective-permute-done | bytes 9248 | tf_op jit(solution)/shard_map/ppermute | solution.py:280
  17.2 0.0 collective-permute-done.refs_1_
  17.2 0.7 %second.1 = (f32[18,128]{1,0:T(8,128)S(1)}, f32[136,1,128]{2,1,0:T(1,128)S(1)}) custom-call(f32[18,1,128]{2,1,0:T(1,128)S(1)} %first.1.refs_0_, f32[18,1,128]{2,1,0:T(1,128)S(1)} %collective-permute-done.refs_1_, f32[18,1,128]{2,1,0:T(1,128)S(1)} %collective-permute-done.1.refs_2_, f32[18,1,128]{2,1,0:T(1,128)S(1)} %collective-permute-done.2.refs_3_, ...), custom_call_target="tpu_custom_call" | custom-call | flops 8388608 | tf_op jit(solution)/shard_map/second/pallas_call | solution.py:27
  17.9 8.6 %all_to_all.16.refs_0_ = f32[136,1,128]{2,1,0:T(1,128)S(1)} all-to-all(f32[136,1,128]{2,1,0:T(1,128)S(1)} %get-tuple-element.31), channel_id=1, replica_groups={{20,24,28,0,4,8,12,16},{21,25,29,1,5,9,13,17},{22,26,30,2,6,10,14,18},{..., dimensions={0} | all-to-all | bytes 139264 | tf_op jit(solution)/shard_map/all_to_all | solution.py:274
  26.4 0.7 %third.1 = (f32[19,1,128]{2,1,0:T(1,128)S(1)}, f32[8,256]{1,0:T(8,128)S(1)}, f32[1,128]{1,0:T(1,128)S(1)}) custom-call(f32[136,1,128]{2,1,0:T(1,128)S(1)} %all_to_all.16.refs_0_, f32[8,2,256]{2,1,0:T(2,128)S(1)} %all_to_all.15.refs_0_.refs_1_.refs_5_.gathered, f32[18,128]{1,0:T(8,128)S(1)} %get-tuple-element.32.refs_2_.refs_4_, ...), custom_call_target="tpu_custom_call" | custom-call | flops 8388608 | tf_op jit(solution)/shard_map/third/pallas_call | solution.py:27
  27.2 0.1 collective-permute-start.5
  27.3 1.6 %collective-permute-start.4 = (f32[19,1,128]{2,1,0:T(1,128)S(1)}, f32[19,1,128]{2,1,0:T(1,128)S(1)}, u32[]{:S(2)}, u32[]{:S(2)}) collective-permute-start(f32[19,1,128]{2,1,0:T(1,128)S(1)} %get-tuple-element.36.refs_0_), channel_id=1, source_target_pairs={{0,2},{1,3},{2,0},{3,1},{4,6},{5,7},{6,4},{7,5},{8,10},{9,11},{10,... | collective-permute-start | bytes 29192 | tf_op jit(solution)/shard_map/ppermute | solution.py:280
  28.8 0.3 collective-permute-start.3
  29.1 1.3 %collective-permute-done.5.refs_3_ = f32[19,1,128]{2,1,0:T(1,128)S(1)} collective-permute-done((f32[19,1,128]{2,1,0:T(1,128)S(1)}, f32[19,1,128]{2,1,0:T(1,128)S(1)}, u32[]{:S(2)}, u32[]{:S(2)}) %collective-permute-start.5) | collective-permute-done | bytes 9760 | tf_op jit(solution)/shard_map/ppermute | solution.py:280
  30.4 0.6 %collective-permute-done.4.refs_2_ = f32[19,1,128]{2,1,0:T(1,128)S(1)} collective-permute-done((f32[19,1,128]{2,1,0:T(1,128)S(1)}, f32[19,1,128]{2,1,0:T(1,128)S(1)}, u32[]{:S(2)}, u32[]{:S(2)}) %collective-permute-start.4) | collective-permute-done | bytes 9760 | tf_op jit(solution)/shard_map/ppermute | solution.py:280
  31.0 0.0 collective-permute-done.3.refs_1_
  31.0 0.7 %fourth.1 = (f32[8,3,128]{2,1,0:T(4,128)S(1)}, f32[8,256]{1,0:T(8,128)S(1)}, f32[2,128]{1,0:T(2,128)S(1)}) custom-call(f32[19,1,128]{2,1,0:T(1,128)S(1)} %get-tuple-element.36.refs_0_, f32[19,1,128]{2,1,0:T(1,128)S(1)} %collective-permute-done.3.refs_1_, f32[19,1,128]{2,1,0:T(1,128)S(1)} %collective-permute-done.4.refs_2_, ...), custom_call_target="tpu_custom_call" | custom-call | flops 8388608 | tf_op jit(solution)/shard_map/fourth/pallas_call | solution.py:27
  31.7 8.2 %all_to_all.17.arrived = f32[8,3,128]{2,1,0:T(4,128)S(1)} all-to-all(f32[8,3,128]{2,1,0:T(4,128)S(1)} %get-tuple-element.38), channel_id=1, replica_groups={{20,24,28,0,4,8,12,16},{21,25,29,1,5,9,13,17},{22,26,30,2,6,10,14,18},{..., dimensions={0} | all-to-all | bytes 24576 | tf_op jit(solution)/shard_map/all_to_all | solution.py:274
  39.9 0.7 %last.1 = (f32[1,256]{1,0:T(1,128)}, f32[1,256]{1,0:T(1,128)}) custom-call(f32[8,3,128]{2,1,0:T(4,128)S(1)} %all_to_all.17.arrived, f32[8,2,256]{2,1,0:T(2,128)S(1)} %all_to_all.15.refs_0_.refs_1_.refs_5_.gathered, f32[8,256]{1,0:T(8,128)S(1)} %get-tuple-element.37.refs_6_.residual, f32[8,256]{1,0:T(8,128)S(1)} %get-tuple-element.39.direction, ...), custom_call_target="tpu_custom_call" | custom-call | tf_op jit(solution)/shard_map/last/pallas_call | solution.py:363
  (3 shorter events, 0.0 us)
Async XLA Ops:
  0.6 0.7 %copy-start.3 = (s32[1,1,16]{2,1,0:T(1,128)S(1)}, s32[1,1,16]{2,1,0:T(1,128)}, u32[]{:S(2)}) copy-start(s32[1,1,16]{2,1,0:T(1,128)} %refs_3_.4) | copy-start | bytes 196
  0.6 0.7 %copy-start.2 = (s32[1,1,16]{2,1,0:T(1,128)S(1)}, s32[1,1,16]{2,1,0:T(1,128)}, u32[]{:S(2)}) copy-start(s32[1,1,16]{2,1,0:T(1,128)} %refs_2_.2) | copy-start | bytes 196
  0.7 0.7 %copy-start.5 = (f32[1,256]{1,0:T(1,128)S(1)}, f32[1,256]{1,0:T(1,128)}, u32[]{:S(2)}) copy-start(f32[1,256]{1,0:T(1,128)} %refs_1_.3) | copy-start | bytes 3076
  0.7 0.7 %copy-start.4 = (f32[1,256]{1,0:T(1,128)S(1)}, f32[1,256]{1,0:T(1,128)}, u32[]{:S(2)}) copy-start(f32[1,256]{1,0:T(1,128)} %refs_0_.2) | copy-start | bytes 3076
  1.4 11.4 %copy-start = (f32[1,1,16,256,256]{4,3,2,1,0:T(8,128)S(1)}, f32[1,1,16,256,256]{4,3,2,1,0:T(8,128)}, u32[]{:S(2)}) copy-start(f32[1,1,16,256,256]{4,3,2,1,0:T(8,128)} %refs_3_.5) | copy-start | bytes 12582916
  12.8 4.4 %copy-start.1 = (f32[8,256]{1,0:T(8,128)S(1)}, f32[8,256]{1,0:T(8,128)}, u32[]{:S(2)}) copy-start(f32[8,256]{1,0:T(8,128)} %refs_7_.1) | copy-start | bytes 24580
  13.5 3.2 %collective-permute-start.2 = (f32[18,1,128]{2,1,0:T(1,128)S(1)}, f32[18,1,128]{2,1,0:T(1,128)S(1)}, u32[]{:S(2)}, u32[]{:S(2)}) collective-permute-start(f32[18,1,128]{2,1,0:T(1,128)S(1)} %first.1.refs_0_), channel_id=1, source_target_pairs={{0,3},{1,2},{2,1},{3,0},{4,7},{5,6},{6,5},{7,4},{8,11},{9,10},{10,... | collective-permute-start | bytes 27656 | tf_op jit(solution)/shard_map/ppermute | solution.py:280
  13.5 3.7 %collective-permute-start.1 = (f32[18,1,128]{2,1,0:T(1,128)S(1)}, f32[18,1,128]{2,1,0:T(1,128)S(1)}, u32[]{:S(2)}, u32[]{:S(2)}) collective-permute-start(f32[18,1,128]{2,1,0:T(1,128)S(1)} %first.1.refs_0_), channel_id=1, source_target_pairs={{0,2},{1,3},{2,0},{3,1},{4,6},{5,7},{6,4},{7,5},{8,10},{9,11},{10,... | collective-permute-start | bytes 27656 | tf_op jit(solution)/shard_map/ppermute | solution.py:280
  15.0 2.2 %collective-permute-start = (f32[18,1,128]{2,1,0:T(1,128)S(1)}, f32[18,1,128]{2,1,0:T(1,128)S(1)}, u32[]{:S(2)}, u32[]{:S(2)}) collective-permute-start(f32[18,1,128]{2,1,0:T(1,128)S(1)} %first.1.refs_0_), channel_id=1, source_target_pairs={{0,1},{1,0},{2,3},{3,2},{4,5},{5,4},{6,7},{7,6},{8,9},{9,8},{10,11... | collective-permute-start | bytes 27656 | tf_op jit(solution)/shard_map/ppermute | solution.py:280
  27.2 3.2 %collective-permute-start.5 = (f32[19,1,128]{2,1,0:T(1,128)S(1)}, f32[19,1,128]{2,1,0:T(1,128)S(1)}, u32[]{:S(2)}, u32[]{:S(2)}) collective-permute-start(f32[19,1,128]{2,1,0:T(1,128)S(1)} %get-tuple-element.36.refs_0_), channel_id=1, source_target_pairs={{0,3},{1,2},{2,1},{3,0},{4,7},{5,6},{6,5},{7,4},{8,11},{9,10},{10,... | collective-permute-start | bytes 29192 | tf_op jit(solution)/shard_map/ppermute | solution.py:280
  27.3 3.7 %collective-permute-start.4 = (f32[19,1,128]{2,1,0:T(1,128)S(1)}, f32[19,1,128]{2,1,0:T(1,128)S(1)}, u32[]{:S(2)}, u32[]{:S(2)}) collective-permute-start(f32[19,1,128]{2,1,0:T(1,128)S(1)} %get-tuple-element.36.refs_0_), channel_id=1, source_target_pairs={{0,2},{1,3},{2,0},{3,1},{4,6},{5,7},{6,4},{7,5},{8,10},{9,11},{10,... | collective-permute-start | bytes 29192 | tf_op jit(solution)/shard_map/ppermute | solution.py:280
  28.8 2.2 %collective-permute-start.3 = (f32[19,1,128]{2,1,0:T(1,128)S(1)}, f32[19,1,128]{2,1,0:T(1,128)S(1)}, u32[]{:S(2)}, u32[]{:S(2)}) collective-permute-start(f32[19,1,128]{2,1,0:T(1,128)S(1)} %get-tuple-element.36.refs_0_), channel_id=1, source_target_pairs={{0,1},{1,0},{2,3},{3,2},{4,5},{5,4},{6,7},{7,6},{8,9},{9,8},{10,11... | collective-permute-start | bytes 29192 | tf_op jit(solution)/shard_map/ppermute | solution.py:280

commit v8 on v7

--- a/solution.py
+++ b/solution.py
@@ -198,9 +198,9 @@
     inner = fold(row_sum(weighted * lifted))
     rows = block_product(spread, gather, weighted, flipped, slots, table, high, low)
     length = out.shape[0] // peers
+    packed = jnp.concatenate(pieces_of(rows) + [inner], axis=0)
     for j in range(peers):
-        put(out, j * length, rows)
-        put(out, (j + 1) * length - 1, inner)
+        out[pl.ds(j * length, length), :] = packed
 
 
 def third_body(slots, cols, arrived, gathered, total, tiles, spread, gather, table, high, low, out, residual_out, alpha_out):
@@ -209,9 +209,9 @@
     group, size = residual.shape
     length = group * (size // LANES) + 1
     peers = arrived.shape[0] // length
-    summed = arrived[pl.ds(0, length), 0, :]
+    summed = arrived[pl.ds(0, length), :]
     for j in range(1, peers):
-        summed += arrived[pl.ds(j * length, length), 0, :]
+        summed += arrived[pl.ds(j * length, length), :]
     image = take(summed, group, size) + ridge_weight * z
     count = cols * (size // LANES)
     gamma = lane_sum(total[pl.ds(count, 1), :])
@@ -340,16 +340,16 @@
     total, sent = call(
         lambda *refs: second_body(plain, peers, *refs),
         "second",
-        [((cols * pieces + 2, LANES), F32), ((peers * length, 1, LANES), F32)],
+        [((cols * pieces + 2, LANES), F32), ((peers * length, LANES), F32)],
         (*share(mine, "row", groups), scaling, flipped, spread_cols, gather_rows, to_rows, high_t, low_t),
         **work,
     )
-    arrived = exchange(sent, peers, starts[1])
+    arrived = exchange(sent.reshape(-1, 1, LANES), peers, starts[1])
     mine, residual, alpha = call(
         lambda *refs: third_body(plain, cols, *refs),
         "third",
         [((cols * pieces + 3, 1, LANES), F32), ((group, size), F32), ((1, LANES), F32)],
-        (arrived, gathered, total, blocks, spread_rows, gather_cols, to_cols, high, low),
+        (arrived.reshape(-1, LANES), gathered, total, blocks, spread_rows, gather_cols, to_cols, high, low),
         **work,
     )
     sent, direction, scalars = call(

time: 40.9 us -> 40.8 us (level)
  no operation moved by 1% of the time
where the time goes in v8:
time: 40.8 us; the launch traced here: 40.6 us
  blocking collectives  28 us (69%)
  Pallas kernels  4.86 us (12%)
  starting transfers between devices  3.79 us (9%)
  waiting for transfers between devices  2.47 us (6%)
  between operations  1.43 us (4%)
    all_to_all x3, blocking collectives, exchange(): lax.all_to_all(value, 'col', 0, 0, tiled=True, axis_index_groups=[order])  28 us
    pallas_call x7, Pallas kernels, call(): pl.pallas_call(body, name=name, out_shape=[pltpu.VMEM(s, d) for s, d in o...  4.12 us
    ppermute x6, starting transfers between devices, share(): moved.append(lax.ppermute(value, axis, [(i, i ^ s) for i in range(size)]))  3.79 us
    ppermute x6, waiting for transfers between devices, share(): moved.append(lax.ppermute(value, axis, [(i, i ^ s) for i in range(size)]))  2.47 us
  transfers between devices with their start and end apart: 6, of which 3 were waited for; matrix products, arithmetic and copies ran while one was open for 0% of the time, Pallas kernels for 3%

profile of v8, /device:TPU:0, one launch (start us, length us, event | category | flops | bytes accessed | tf_op | source)
XLA Modules:
  0.0 40.6 jit_solution(12164747431996567663)
XLA Ops:
  0.6 0.0 copy-start.3
  0.6 0.0 copy-start.2
  0.7 0.0 copy-start.5
  0.7 0.0 copy-start.4
  1.3 0.0 copy-done.3
  1.4 0.0 copy-done.2
  1.4 0.0 copy-done.5
  1.4 0.0 copy-done.4
  1.4 0.0 copy-start
  1.4 0.1 start.1
  1.5 11.2 %all_to_all.15.refs_0_.refs_1_.refs_5_.gathered = f32[8,2,256]{2,1,0:T(2,128)S(1)} all-to-all(f32[8,2,256]{2,1,0:T(2,128)S(1)} %get-tuple-element.22), channel_id=1, replica_groups={{20,24,28,0,4,8,12,16},{21,25,29,1,5,9,13,17},{22,26,30,2,6,10,14,18},{..., dimensions={0} | all-to-all | bytes 32768 | tf_op jit(solution)/shard_map/all_to_all | solution.py:274
  12.8 0.0 copy-done
  12.8 0.7 %first.1.refs_0_ = f32[18,1,128]{2,1,0:T(1,128)S(1)} custom-call(f32[8,2,256]{2,1,0:T(2,128)S(1)} %all_to_all.15.refs_0_.refs_1_.refs_5_.gathered, f32[1,1,16,256,256]{4,3,2,1,0:T(8,128)S(1)} %copy-done, bf16[24,2048]{1,0:T(8,128)(2,1)S(1)} %get-tuple-element.23.refs_2_.refs_4_, bf16[8,128]{1,0:T(8,128)(2,1)S(1)} %get-tuple-element.24.refs_3_.refs_5_), custom_call_target="tpu_custom_call" | custom-call | flops 8388608 | tf_op jit(solution)/shard_map/first/pallas_call | solution.py:27
  13.5 0.0 collective-permute-start.2
  13.5 1.6 %collective-permute-start.1 = (f32[18,1,128]{2,1,0:T(1,128)S(1)}, f32[18,1,128]{2,1,0:T(1,128)S(1)}, u32[]{:S(2)}, u32[]{:S(2)}) collective-permute-start(f32[18,1,128]{2,1,0:T(1,128)S(1)} %first.1.refs_0_), channel_id=1, source_target_pairs={{0,2},{1,3},{2,0},{3,1},{4,6},{5,7},{6,4},{7,5},{8,10},{9,11},{10,... | collective-permute-start | bytes 27656 | tf_op jit(solution)/shard_map/ppermute | solution.py:280
  15.0 0.3 collective-permute-start
  15.3 1.3 %flip.1 = (bf16[24,1792]{1,0:T(8,128)(2,1)S(1)}, bf16[8,112]{1,0:T(8,128)(2,1)S(1)}, bf16[32,16]{1,0:T(8,128)(2,1)S(1)}, bf16[32,16]{1,0:T(8,128)(2,1)S(1)}, f32...) custom-call(f32[1,1,16,256,256]{4,3,2,1,0:T(8,128)S(1)} %copy-done, ...), custom_call_target="tpu_custom_call" | custom-call | flops 1073741824 | tf_op jit(solution)/shard_map/flip/pallas_call | solution.py:27
  16.6 0.0 collective-permute-done.2.refs_3_
  16.6 0.6 %collective-permute-done.1.refs_2_ = f32[18,1,128]{2,1,0:T(1,128)S(1)} collective-permute-done((f32[18,1,128]{2,1,0:T(1,128)S(1)}, f32[18,1,128]{2,1,0:T(1,128)S(1)}, u32[]{:S(2)}, u32[]{:S(2)}) %collective-permute-start.1) | collective-permute-done | bytes 9248 | tf_op jit(solution)/shard_map/ppermute | solution.py:280
  17.2 0.0 collective-permute-done.refs_1_
  17.2 0.6 %second.1 = (f32[18,128]{1,0:T(8,128)S(1)}, f32[136,128]{1,0:T(8,128)S(1)}) custom-call(f32[18,1,128]{2,1,0:T(1,128)S(1)} %first.1.refs_0_, f32[18,1,128]{2,1,0:T(1,128)S(1)} %collective-permute-done.refs_1_, f32[18,1,128]{2,1,0:T(1,128)S(1)} %collective-permute-done.1.refs_2_, f32[18,1,128]{2,1,0:T(1,128)S(1)} %collective-permute-done.2.refs_3_, ...), custom_call_target="tpu_custom_call" | custom-call | flops 8388608 | tf_op jit(solution)/shard_map/second/pallas_call | solution.py:27
  17.8 8.6 %all_to_all.16 = f32[136,1,128]{2,1,0:T(1,128)S(1)} all-to-all(f32[136,1,128]{2,1,0:T(1,128)S(1)} %bitcast.5), channel_id=1, replica_groups={{20,24,28,0,4,8,12,16},{21,25,29,1,5,9,13,17},{22,26,30,2,6,10,14,18},{..., dimensions={0} | all-to-all | bytes 139264 | tf_op jit(solution)/shard_map/all_to_all | solution.py:274
  26.4 0.7 %third.1 = (f32[19,1,128]{2,1,0:T(1,128)S(1)}, f32[8,256]{1,0:T(8,128)S(1)}, f32[1,128]{1,0:T(1,128)S(1)}) custom-call(f32[136,128]{1,0:T(8,128)S(1)} %bitcast.4, f32[8,2,256]{2,1,0:T(2,128)S(1)} %all_to_all.15.refs_0_.refs_1_.refs_5_.gathered, f32[18,128]{1,0:T(8,128)S(1)} %get-tuple-element.32.refs_2_.refs_4_, f32[1,1,16,256,256]{4,3,2,1,0:T(8,128)S(1)} %copy-done, ...), custom_call_target="tpu_custom_call" | custom-call | flops 8388608 | tf_op jit(solution)/shard_map/third/pallas_call | solution.py:27
  27.1 0.1 collective-permute-start.5
  27.2 1.6 %collective-permute-start.4 = (f32[19,1,128]{2,1,0:T(1,128)S(1)}, f32[19,1,128]{2,1,0:T(1,128)S(1)}, u32[]{:S(2)}, u32[]{:S(2)}) collective-permute-start(f32[19,1,128]{2,1,0:T(1,128)S(1)} %get-tuple-element.36.refs_0_), channel_id=1, source_target_pairs={{0,2},{1,3},{2,0},{3,1},{4,6},{5,7},{6,4},{7,5},{8,10},{9,11},{10,... | collective-permute-start | bytes 29192 | tf_op jit(solution)/shard_map/ppermute | solution.py:280
  28.8 0.3 collective-permute-start.3
  29.1 1.3 %collective-permute-done.5.refs_3_ = f32[19,1,128]{2,1,0:T(1,128)S(1)} collective-permute-done((f32[19,1,128]{2,1,0:T(1,128)S(1)}, f32[19,1,128]{2,1,0:T(1,128)S(1)}, u32[]{:S(2)}, u32[]{:S(2)}) %collective-permute-start.5) | collective-permute-done | bytes 9760 | tf_op jit(solution)/shard_map/ppermute | solution.py:280
  30.4 0.6 %collective-permute-done.4.refs_2_ = f32[19,1,128]{2,1,0:T(1,128)S(1)} collective-permute-done((f32[19,1,128]{2,1,0:T(1,128)S(1)}, f32[19,1,128]{2,1,0:T(1,128)S(1)}, u32[]{:S(2)}, u32[]{:S(2)}) %collective-permute-start.4) | collective-permute-done | bytes 9760 | tf_op jit(solution)/shard_map/ppermute | solution.py:280
  30.9 0.0 collective-permute-done.3.refs_1_
  30.9 0.7 %fourth.1 = (f32[8,3,128]{2,1,0:T(4,128)S(1)}, f32[8,256]{1,0:T(8,128)S(1)}, f32[2,128]{1,0:T(2,128)S(1)}) custom-call(f32[19,1,128]{2,1,0:T(1,128)S(1)} %get-tuple-element.36.refs_0_, f32[19,1,128]{2,1,0:T(1,128)S(1)} %collective-permute-done.3.refs_1_, f32[19,1,128]{2,1,0:T(1,128)S(1)} %collective-permute-done.4.refs_2_, ...), custom_call_target="tpu_custom_call" | custom-call | flops 8388608 | tf_op jit(solution)/shard_map/fourth/pallas_call | solution.py:27
  31.6 8.2 %all_to_all.17.arrived = f32[8,3,128]{2,1,0:T(4,128)S(1)} all-to-all(f32[8,3,128]{2,1,0:T(4,128)S(1)} %get-tuple-element.38), channel_id=1, replica_groups={{20,24,28,0,4,8,12,16},{21,25,29,1,5,9,13,17},{22,26,30,2,6,10,14,18},{..., dimensions={0} | all-to-all | bytes 24576 | tf_op jit(solution)/shard_map/all_to_all | solution.py:274
  39.9 0.7 %last.1 = (f32[1,256]{1,0:T(1,128)}, f32[1,256]{1,0:T(1,128)}) custom-call(f32[8,3,128]{2,1,0:T(4,128)S(1)} %all_to_all.17.arrived, f32[8,2,256]{2,1,0:T(2,128)S(1)} %all_to_all.15.refs_0_.refs_1_.refs_5_.gathered, f32[8,256]{1,0:T(8,128)S(1)} %get-tuple-element.37.refs_6_.residual, f32[8,256]{1,0:T(8,128)S(1)} %get-tuple-element.39.direction, ...), custom_call_target="tpu_custom_call" | custom-call | tf_op jit(solution)/shard_map/last/pallas_call | solution.py:363
  (3 shorter events, 0.0 us)
Async XLA Ops:
  0.6 0.7 %copy-start.3 = (s32[1,1,16]{2,1,0:T(1,128)S(1)}, s32[1,1,16]{2,1,0:T(1,128)}, u32[]{:S(2)}) copy-start(s32[1,1,16]{2,1,0:T(1,128)} %refs_3_.4) | copy-start | bytes 196
  0.6 0.7 %copy-start.2 = (s32[1,1,16]{2,1,0:T(1,128)S(1)}, s32[1,1,16]{2,1,0:T(1,128)}, u32[]{:S(2)}) copy-start(s32[1,1,16]{2,1,0:T(1,128)} %refs_2_.2) | copy-start | bytes 196
  0.7 0.7 %copy-start.5 = (f32[1,256]{1,0:T(1,128)S(1)}, f32[1,256]{1,0:T(1,128)}, u32[]{:S(2)}) copy-start(f32[1,256]{1,0:T(1,128)} %refs_1_.3) | copy-start | bytes 3076
  0.7 0.7 %copy-start.4 = (f32[1,256]{1,0:T(1,128)S(1)}, f32[1,256]{1,0:T(1,128)}, u32[]{:S(2)}) copy-start(f32[1,256]{1,0:T(1,128)} %refs_0_.2) | copy-start | bytes 3076
  1.4 11.4 %copy-start = (f32[1,1,16,256,256]{4,3,2,1,0:T(8,128)S(1)}, f32[1,1,16,256,256]{4,3,2,1,0:T(8,128)}, u32[]{:S(2)}) copy-start(f32[1,1,16,256,256]{4,3,2,1,0:T(8,128)} %refs_3_.5) | copy-start | bytes 12582916
  12.8 4.4 %copy-start.1 = (f32[8,256]{1,0:T(8,128)S(1)}, f32[8,256]{1,0:T(8,128)}, u32[]{:S(2)}) copy-start(f32[8,256]{1,0:T(8,128)} %refs_7_.1) | copy-start | bytes 24580
  13.5 3.2 %collective-permute-start.2 = (f32[18,1,128]{2,1,0:T(1,128)S(1)}, f32[18,1,128]{2,1,0:T(1,128)S(1)}, u32[]{:S(2)}, u32[]{:S(2)}) collective-permute-start(f32[18,1,128]{2,1,0:T(1,128)S(1)} %first.1.refs_0_), channel_id=1, source_target_pairs={{0,3},{1,2},{2,1},{3,0},{4,7},{5,6},{6,5},{7,4},{8,11},{9,10},{10,... | collective-permute-start | bytes 27656 | tf_op jit(solution)/shard_map/ppermute | solution.py:280
  13.5 3.7 %collective-permute-start.1 = (f32[18,1,128]{2,1,0:T(1,128)S(1)}, f32[18,1,128]{2,1,0:T(1,128)S(1)}, u32[]{:S(2)}, u32[]{:S(2)}) collective-permute-start(f32[18,1,128]{2,1,0:T(1,128)S(1)} %first.1.refs_0_), channel_id=1, source_target_pairs={{0,2},{1,3},{2,0},{3,1},{4,6},{5,7},{6,4},{7,5},{8,10},{9,11},{10,... | collective-permute-start | bytes 27656 | tf_op jit(solution)/shard_map/ppermute | solution.py:280
  15.0 2.2 %collective-permute-start = (f32[18,1,128]{2,1,0:T(1,128)S(1)}, f32[18,1,128]{2,1,0:T(1,128)S(1)}, u32[]{:S(2)}, u32[]{:S(2)}) collective-permute-start(f32[18,1,128]{2,1,0:T(1,128)S(1)} %first.1.refs_0_), channel_id=1, source_target_pairs={{0,1},{1,0},{2,3},{3,2},{4,5},{5,4},{6,7},{7,6},{8,9},{9,8},{10,11... | collective-permute-start | bytes 27656 | tf_op jit(solution)/shard_map/ppermute | solution.py:280
  27.1 3.2 %collective-permute-start.5 = (f32[19,1,128]{2,1,0:T(1,128)S(1)}, f32[19,1,128]{2,1,0:T(1,128)S(1)}, u32[]{:S(2)}, u32[]{:S(2)}) collective-permute-start(f32[19,1,128]{2,1,0:T(1,128)S(1)} %get-tuple-element.36.refs_0_), channel_id=1, source_target_pairs={{0,3},{1,2},{2,1},{3,0},{4,7},{5,6},{6,5},{7,4},{8,11},{9,10},{10,... | collective-permute-start | bytes 29192 | tf_op jit(solution)/shard_map/ppermute | solution.py:280
  27.2 3.7 %collective-permute-start.4 = (f32[19,1,128]{2,1,0:T(1,128)S(1)}, f32[19,1,128]{2,1,0:T(1,128)S(1)}, u32[]{:S(2)}, u32[]{:S(2)}) collective-permute-start(f32[19,1,128]{2,1,0:T(1,128)S(1)} %get-tuple-element.36.refs_0_), channel_id=1, source_target_pairs={{0,2},{1,3},{2,0},{3,1},{4,6},{5,7},{6,4},{7,5},{8,10},{9,11},{10,... | collective-permute-start | bytes 29192 | tf_op jit(solution)/shard_map/ppermute | solution.py:280
  28.8 2.2 %collective-permute-start.3 = (f32[19,1,128]{2,1,0:T(1,128)S(1)}, f32[19,1,128]{2,1,0:T(1,128)S(1)}, u32[]{:S(2)}, u32[]{:S(2)}) collective-permute-start(f32[19,1,128]{2,1,0:T(1,128)S(1)} %get-tuple-element.36.refs_0_), channel_id=1, source_target_pairs={{0,1},{1,0},{2,3},{3,2},{4,5},{5,4},{6,7},{7,6},{8,9},{9,8},{10,11... | collective-permute-start | bytes 29192 | tf_op jit(solution)/shard_map/ppermute | solution.py:280

commit v9 on v8

--- a/solution.py
+++ b/solution.py
@@ -9,7 +9,7 @@
 LANES = 128
 FLIP = 1 << 30
 FIRST = (5, 5, 5)
-SHARE = 2
+SHARE = 0
 VMEM_LIMIT = 16 << 20
 F32 = jnp.float32
 BF16 = jnp.bfloat16
@@ -117,28 +117,13 @@
     low[here, :] = (tile - upper.astype(F32)).astype(BF16)
 
 
-def flip_body(plain, group, cols, first, tiles, count, rows_of, cols_of, spread_cols, gather_rows, to_cols, to_rows, flipped, high, low, high_t, low_t):
+def flip_body(plain, group, cols, first, tiles, count, rows_of, cols_of, spread_cols, gather_rows, flipped):
     slots, size = tiles.shape[2], tiles.shape[3]
     for k in range(plain):
         flipped[k] = tiles[0, 0, k].T
-    for k in range(plain, slots):
-        here = pl.ds((k - plain) * size, size)
-        store_split(high, low, here, tiles[0, 0, k])
-        store_split(high_t, low_t, here, tiles[0, 0, k].T)
     rows, columns = turn(rows_of[0], group, first), cols_of[0]
     spread_table(spread_cols, columns, count, plain)
     gather_table(gather_rows, rows)
-    for out, targets, sources, target, source in (
-        (to_cols, cols, group, columns, rows),
-        (to_rows, group, cols, rows, columns),
-    ):
-        r = lax.broadcasted_iota(jnp.int32, (2 * targets, 2 * sources), 0)
-        q = lax.broadcasted_iota(jnp.int32, (2 * targets, 2 * sources), 1)
-        for k in range(plain, slots):
-            t = jnp.where(k < count[0, 0], target[:, k : k + 1], -1 - targets)
-            s = source[:, k : k + 1]
-            hit = ((r == t) & (q == s)) | ((r == targets + t) & (q == sources + s))
-            out[pl.ds((k - plain) * 2 * targets, 2 * targets), :] = jnp.where(hit, 1.0, 0.0).astype(BF16)
 
 
 def own_body(group, first, own):
@@ -189,21 +174,21 @@
     return (a + b) + (c + d)
 
 
-def second_body(slots, peers, p0, p1, p2, p3, scaling, flipped, spread, gather, table, high, low, total, out):
+def second_body(slots, peers, p0, p1, p2, p3, scaling, flipped, spread, gather, total, out):
     summed = gather4((p0, p1, p2, p3))
     total[...] = summed
     cols, size = scaling.shape
     lifted = take(summed, cols, size)
     weighted = scaling[...] * lifted
     inner = fold(row_sum(weighted * lifted))
-    rows = block_product(spread, gather, weighted, flipped, slots, table, high, low)
+    rows = block_product(spread, gather, weighted, flipped, slots)
     length = out.shape[0] // peers
     packed = jnp.concatenate(pieces_of(rows) + [inner], axis=0)
     for j in range(peers):
         out[pl.ds(j * length, length), :] = packed
 
 
-def third_body(slots, cols, arrived, gathered, total, tiles, spread, gather, table, high, low, out, residual_out, alpha_out):
+def third_body(slots, cols, arrived, gathered, total, tiles, spread, gather, out, residual_out, alpha_out):
     residual, weights = gathered[:, 0, :], gathered[:, 1, :]
     z = weights * residual
     group, size = residual.shape
@@ -224,10 +209,10 @@
     put(out, count, fold(row_sum(later * z1)))
     put(out, count + 1, fold(row_sum(z1 * z1)))
     put(out, count + 2, fold(row_sum(z1 * z)))
-    put(out, 0, block_product(spread, gather, z1, tiles.at[0, 0], slots, table, high, low))
-
-
-def fourth_body(slots, by, p0, p1, p2, p3, total, gathered, residual, scaling, flipped, spread, gather, table, high, low, out, direction_out, scalars):
+    put(out, 0, block_product(spread, gather, z1, tiles.at[0, 0], slots))
+
+
+def fourth_body(slots, by, p0, p1, p2, p3, total, gathered, residual, scaling, flipped, spread, gather, out, direction_out, scalars):
     summed = gather4((p0, p1, p2, p3))
     cols, size = scaling.shape
     count = cols * (size // LANES)
@@ -239,7 +224,7 @@
     lifted = take(summed, cols, size) + beta * take(total[...], cols, size)
     weighted = scaling[...] * lifted
     inner = fold(row_sum(weighted * lifted))
-    rows = block_product(spread, gather, weighted, flipped, slots, table, high, low)
+    rows = block_product(spread, gather, weighted, flipped, slots)
     peers = out.shape[0]
     for h, piece in enumerate(pieces_of(rows)):
         out[:, h, :] = turned(piece, by)
@@ -321,17 +306,14 @@
     )
     plain = (slots - slots * SHARE // 16) // 2 * 2
     rest = slots - plain
-    spread_cols, gather_rows, to_cols, to_rows, flipped, high, low, high_t, low_t = call(
+    spread_cols, gather_rows, flipped = call(
         lambda *refs: flip_body(plain, group, cols, starts[0], *refs),
         "flip",
         [
             ((3 * cols, plain * LANES), BF16),
             ((group, plain * 8), BF16),
-            ((rest * 2 * cols, 2 * group), BF16),
-            ((rest * 2 * group, 2 * cols), BF16),
             ((plain, size, size), F32),
-        ]
-        + [((rest * size, size), BF16)] * 4,
+        ],
         (blocks, block_count, block_rows, block_cols),
         in_specs=[vmem(), pl.BlockSpec(memory_space=pltpu.SMEM), vmem(), vmem()],
         flops=FLIP,
@@ -341,7 +323,7 @@
         lambda *refs: second_body(plain, peers, *refs),
         "second",
         [((cols * pieces + 2, LANES), F32), ((peers * length, LANES), F32)],
-        (*share(mine, "row", groups), scaling, flipped, spread_cols, gather_rows, to_rows, high_t, low_t),
+        (*share(mine, "row", groups), scaling, flipped, spread_cols, gather_rows),
         **work,
     )
     arrived = exchange(sent.reshape(-1, 1, LANES), peers, starts[1])
@@ -349,14 +331,14 @@
         lambda *refs: third_body(plain, cols, *refs),
         "third",
         [((cols * pieces + 3, 1, LANES), F32), ((group, size), F32), ((1, LANES), F32)],
-        (arrived.reshape(-1, LANES), gathered, total, blocks, spread_rows, gather_cols, to_cols, high, low),
+        (arrived.reshape(-1, LANES), gathered, total, blocks, spread_rows, gather_cols),
         **work,
     )
     sent, direction, scalars = call(
         lambda *refs: fourth_body(plain, starts[2] - starts[0], *refs),
         "fourth",
         [((peers, pieces + 1, LANES), F32), ((group, size), F32), ((2, LANES), F32)],
-        (*share(mine, "row", groups), total, gathered, residual, scaling, flipped, spread_cols, gather_rows, to_rows, high_t, low_t),
+        (*share(mine, "row", groups), total, gathered, residual, scaling, flipped, spread_cols, gather_rows),
         **work,
     )
     arrived = exchange(sent, peers, starts[2])

time: 40.8 us -> 40.9 us (level)
  transfers between devices with their start and end apart: 6 -> 6, of which waited for: 3 -> 4; matrix products, arithmetic and copies ran while one was open for 0% -> 0% of each run, Pallas kernels for 3% -> 3%
where the time goes in v9:
time: 40.9 us; the launch traced here: 40.6 us
  blocking collectives  28 us (68%)
  Pallas kernels  4.91 us (12%)
  starting transfers between devices  3.73 us (9%)
  waiting for transfers between devices  2.53 us (6%)
  between operations  1.4 us (3%)
    all_to_all x3, blocking collectives, exchange(): lax.all_to_all(value, 'col', 0, 0, tiled=True, axis_index_groups=[order])  28 us
    pallas_call x7, Pallas kernels, call(): pl.pallas_call(body, name=name, out_shape=[pltpu.VMEM(s, d) for s, d in o...  4.17 us
    ppermute x6, starting transfers between devices, share(): moved.append(lax.ppermute(value, axis, [(i, i ^ s) for i in range(size)]))  3.73 us
    ppermute x6, waiting for transfers between devices, share(): moved.append(lax.ppermute(value, axis, [(i, i ^ s) for i in range(size)]))  2.53 us
  transfers between devices with their start and end apart: 6, of which 4 were waited for; matrix products, arithmetic and copies ran while one was open for 0% of the time, Pallas kernels for 3%

profile of v9, /device:TPU:0, one launch (start us, length us, event | category | flops | bytes accessed | tf_op | source)
XLA Modules:
  0.0 40.6 jit_solution(12002945592645638971)
XLA Ops:
  0.6 0.0 copy-start.3
  0.6 0.0 copy-start.2
  0.7 0.0 copy-start.5
  0.7 0.0 copy-start.4
  1.3 0.0 copy-done.3
  1.4 0.0 copy-done.2
  1.4 0.0 copy-done.5
  1.4 0.0 copy-done.4
  1.4 0.0 copy-start
  1.4 0.1 start.1
  1.5 11.2 %all_to_all.15.refs_0_.refs_1_.refs_5_.gathered = f32[8,2,256]{2,1,0:T(2,128)S(1)} all-to-all(f32[8,2,256]{2,1,0:T(2,128)S(1)} %get-tuple-element.16), channel_id=1, replica_groups={{20,24,28,0,4,8,12,16},{21,25,29,1,5,9,13,17},{22,26,30,2,6,10,14,18},{..., dimensions={0} | all-to-all | bytes 32768 | tf_op jit(solution)/shard_map/all_to_all | solution.py:259
  12.8 0.7 %first.1.refs_0_ = f32[18,1,128]{2,1,0:T(1,128)S(1)} custom-call(f32[8,2,256]{2,1,0:T(2,128)S(1)} %all_to_all.15.refs_0_.refs_1_.refs_5_.gathered, f32[1,1,16,256,256]{4,3,2,1,0:T(8,128)S(1)} %copy-done, bf16[24,2048]{1,0:T(8,128)(2,1)S(1)} %get-tuple-element.17.refs_2_.refs_4_, bf16[8,128]{1,0:T(8,128)(2,1)S(1)} %get-tuple-element.18.refs_3_.refs_5_), custom_call_target="tpu_custom_call" | custom-call | flops 8388608 | tf_op jit(solution)/shard_map/first/pallas_call | solution.py:27
  13.5 0.0 collective-permute-start.2
  13.5 1.6 %collective-permute-start.1 = (f32[18,1,128]{2,1,0:T(1,128)S(1)}, f32[18,1,128]{2,1,0:T(1,128)S(1)}, u32[]{:S(2)}, u32[]{:S(2)}) collective-permute-start(f32[18,1,128]{2,1,0:T(1,128)S(1)} %first.1.refs_0_), channel_id=1, source_target_pairs={{0,2},{1,3},{2,0},{3,1},{4,6},{5,7},{6,4},{7,5},{8,10},{9,11},{10,... | collective-permute-start | bytes 27656 | tf_op jit(solution)/shard_map/ppermute | solution.py:265
  15.0 0.3 collective-permute-start
  15.3 1.2 %flip.1 = (bf16[24,2048]{1,0:T(8,128)(2,1)S(1)}, bf16[8,128]{1,0:T(8,128)(2,1)S(1)}, f32[16,256,256]{2,1,0:T(8,128)S(1)}) custom-call(f32[1,1,16,256,256]{4,3,2,1,0:T(8,128)S(1)} %copy-done, s32[1,1]{1,0:T(1,128)S(6)} %copy.10.refs_2_.refs_1_, s32[1,1,16]{2,1,0:T(1,128)S(1)} %copy-done.2, s32[1,1,16]{2,1,0:T(1,128)S(1)} %copy-done.3), custom_call_target="tpu_custom_call" | custom-call | flops 1073741824 | tf_op jit(solution)/shard_map/flip/pallas_call | solution.py:27
  16.6 0.1 collective-permute-done.2.refs_3_
  16.6 0.6 %collective-permute-done.1.refs_2_ = f32[18,1,128]{2,1,0:T(1,128)S(1)} collective-permute-done((f32[18,1,128]{2,1,0:T(1,128)S(1)}, f32[18,1,128]{2,1,0:T(1,128)S(1)}, u32[]{:S(2)}, u32[]{:S(2)}) %collective-permute-start.1) | collective-permute-done | bytes 9248 | tf_op jit(solution)/shard_map/ppermute | solution.py:265
  17.2 0.0 collective-permute-done.refs_1_
  17.2 0.0 copy-done.1
  17.2 0.7 %second.1 = (f32[18,128]{1,0:T(8,128)S(1)}, f32[136,128]{1,0:T(8,128)S(1)}) custom-call(f32[18,1,128]{2,1,0:T(1,128)S(1)} %first.1.refs_0_, f32[18,1,128]{2,1,0:T(1,128)S(1)} %collective-permute-done.refs_1_, f32[18,1,128]{2,1,0:T(1,128)S(1)} %collective-permute-done.1.refs_2_, f32[18,1,128]{2,1,0:T(1,128)S(1)} %collective-permute-done.2.refs_3_, ...), custom_call_target="tpu_custom_call" | custom-call | flops 8388608 | tf_op jit(solution)/shard_map/second/pallas_call | solution.py:27
  17.9 8.6 %all_to_all.16 = f32[136,1,128]{2,1,0:T(1,128)S(1)} all-to-all(f32[136,1,128]{2,1,0:T(1,128)S(1)} %bitcast.5), channel_id=1, replica_groups={{20,24,28,0,4,8,12,16},{21,25,29,1,5,9,13,17},{22,26,30,2,6,10,14,18},{..., dimensions={0} | all-to-all | bytes 139264 | tf_op jit(solution)/shard_map/all_to_all | solution.py:259
  26.4 0.7 %third.1 = (f32[19,1,128]{2,1,0:T(1,128)S(1)}, f32[8,256]{1,0:T(8,128)S(1)}, f32[1,128]{1,0:T(1,128)S(1)}) custom-call(f32[136,128]{1,0:T(8,128)S(1)} %bitcast.4, f32[8,2,256]{2,1,0:T(2,128)S(1)} %all_to_all.15.refs_0_.refs_1_.refs_5_.gathered, f32[18,128]{1,0:T(8,128)S(1)} %get-tuple-element.23.refs_2_.refs_4_, f32[1,1,16,256,256]{4,3,2,1,0:T(8,128)S(1)} %copy-done, ...), custom_call_target="tpu_custom_call" | custom-call | flops 8388608 | tf_op jit(solution)/shard_map/third/pallas_call | solution.py:27
  27.2 0.0 collective-permute-start.5
  27.2 1.6 %collective-permute-start.4 = (f32[19,1,128]{2,1,0:T(1,128)S(1)}, f32[19,1,128]{2,1,0:T(1,128)S(1)}, u32[]{:S(2)}, u32[]{:S(2)}) collective-permute-start(f32[19,1,128]{2,1,0:T(1,128)S(1)} %get-tuple-element.24.refs_0_), channel_id=1, source_target_pairs={{0,2},{1,3},{2,0},{3,1},{4,6},{5,7},{6,4},{7,5},{8,10},{9,11},{10,... | collective-permute-start | bytes 29192 | tf_op jit(solution)/shard_map/ppermute | solution.py:265
  28.8 0.3 collective-permute-start.3
  29.1 1.3 %collective-permute-done.5.refs_3_ = f32[19,1,128]{2,1,0:T(1,128)S(1)} collective-permute-done((f32[19,1,128]{2,1,0:T(1,128)S(1)}, f32[19,1,128]{2,1,0:T(1,128)S(1)}, u32[]{:S(2)}, u32[]{:S(2)}) %collective-permute-start.5) | collective-permute-done | bytes 9760 | tf_op jit(solution)/shard_map/ppermute | solution.py:265
  30.4 0.6 %collective-permute-done.4.refs_2_ = f32[19,1,128]{2,1,0:T(1,128)S(1)} collective-permute-done((f32[19,1,128]{2,1,0:T(1,128)S(1)}, f32[19,1,128]{2,1,0:T(1,128)S(1)}, u32[]{:S(2)}, u32[]{:S(2)}) %collective-permute-start.4) | collective-permute-done | bytes 9760 | tf_op jit(solution)/shard_map/ppermute | solution.py:265
  30.9 0.0 collective-permute-done.3.refs_1_
  30.9 0.7 %fourth.1 = (f32[8,3,128]{2,1,0:T(4,128)S(1)}, f32[8,256]{1,0:T(8,128)S(1)}, f32[2,128]{1,0:T(2,128)S(1)}) custom-call(f32[19,1,128]{2,1,0:T(1,128)S(1)} %get-tuple-element.24.refs_0_, f32[19,1,128]{2,1,0:T(1,128)S(1)} %collective-permute-done.3.refs_1_, f32[19,1,128]{2,1,0:T(1,128)S(1)} %collective-permute-done.4.refs_2_, ...), custom_call_target="tpu_custom_call" | custom-call | flops 8388608 | tf_op jit(solution)/shard_map/fourth/pallas_call | solution.py:27
  31.7 8.2 %all_to_all.17.arrived = f32[8,3,128]{2,1,0:T(4,128)S(1)} all-to-all(f32[8,3,128]{2,1,0:T(4,128)S(1)} %get-tuple-element.26), channel_id=1, replica_groups={{20,24,28,0,4,8,12,16},{21,25,29,1,5,9,13,17},{22,26,30,2,6,10,14,18},{..., dimensions={0} | all-to-all | bytes 24576 | tf_op jit(solution)/shard_map/all_to_all | solution.py:259
  39.9 0.7 %last.1 = (f32[1,256]{1,0:T(1,128)}, f32[1,256]{1,0:T(1,128)}) custom-call(f32[8,3,128]{2,1,0:T(4,128)S(1)} %all_to_all.17.arrived, f32[8,2,256]{2,1,0:T(2,128)S(1)} %all_to_all.15.refs_0_.refs_1_.refs_5_.gathered, f32[8,256]{1,0:T(8,128)S(1)} %get-tuple-element.25.refs_6_.residual, f32[8,256]{1,0:T(8,128)S(1)} %get-tuple-element.27.direction, ...), custom_call_target="tpu_custom_call" | custom-call | tf_op jit(solution)/shard_map/last/pallas_call | solution.py:345
  (3 shorter events, 0.0 us)
Async XLA Ops:
  0.6 0.7 %copy-start.3 = (s32[1,1,16]{2,1,0:T(1,128)S(1)}, s32[1,1,16]{2,1,0:T(1,128)}, u32[]{:S(2)}) copy-start(s32[1,1,16]{2,1,0:T(1,128)} %refs_3_.4) | copy-start | bytes 196
  0.6 0.7 %copy-start.2 = (s32[1,1,16]{2,1,0:T(1,128)S(1)}, s32[1,1,16]{2,1,0:T(1,128)}, u32[]{:S(2)}) copy-start(s32[1,1,16]{2,1,0:T(1,128)} %refs_2_.2) | copy-start | bytes 196
  0.7 0.7 %copy-start.5 = (f32[1,256]{1,0:T(1,128)S(1)}, f32[1,256]{1,0:T(1,128)}, u32[]{:S(2)}) copy-start(f32[1,256]{1,0:T(1,128)} %refs_1_.3) | copy-start | bytes 3076
  0.7 0.7 %copy-start.4 = (f32[1,256]{1,0:T(1,128)S(1)}, f32[1,256]{1,0:T(1,128)}, u32[]{:S(2)}) copy-start(f32[1,256]{1,0:T(1,128)} %refs_0_.2) | copy-start | bytes 3076
  1.4 11.4 %copy-start = (f32[1,1,16,256,256]{4,3,2,1,0:T(8,128)S(1)}, f32[1,1,16,256,256]{4,3,2,1,0:T(8,128)}, u32[]{:S(2)}) copy-start(f32[1,1,16,256,256]{4,3,2,1,0:T(8,128)} %refs_3_.5) | copy-start | bytes 12582916
  12.8 4.4 %copy-start.1 = (f32[8,256]{1,0:T(8,128)S(1)}, f32[8,256]{1,0:T(8,128)}, u32[]{:S(2)}) copy-start(f32[8,256]{1,0:T(8,128)} %refs_7_.1) | copy-start | bytes 24580
  13.5 3.2 %collective-permute-start.2 = (f32[18,1,128]{2,1,0:T(1,128)S(1)}, f32[18,1,128]{2,1,0:T(1,128)S(1)}, u32[]{:S(2)}, u32[]{:S(2)}) collective-permute-start(f32[18,1,128]{2,1,0:T(1,128)S(1)} %first.1.refs_0_), channel_id=1, source_target_pairs={{0,3},{1,2},{2,1},{3,0},{4,7},{5,6},{6,5},{7,4},{8,11},{9,10},{10,... | collective-permute-start | bytes 27656 | tf_op jit(solution)/shard_map/ppermute | solution.py:265
  13.5 3.7 %collective-permute-start.1 = (f32[18,1,128]{2,1,0:T(1,128)S(1)}, f32[18,1,128]{2,1,0:T(1,128)S(1)}, u32[]{:S(2)}, u32[]{:S(2)}) collective-permute-start(f32[18,1,128]{2,1,0:T(1,128)S(1)} %first.1.refs_0_), channel_id=1, source_target_pairs={{0,2},{1,3},{2,0},{3,1},{4,6},{5,7},{6,4},{7,5},{8,10},{9,11},{10,... | collective-permute-start | bytes 27656 | tf_op jit(solution)/shard_map/ppermute | solution.py:265
  15.0 2.2 %collective-permute-start = (f32[18,1,128]{2,1,0:T(1,128)S(1)}, f32[18,1,128]{2,1,0:T(1,128)S(1)}, u32[]{:S(2)}, u32[]{:S(2)}) collective-permute-start(f32[18,1,128]{2,1,0:T(1,128)S(1)} %first.1.refs_0_), channel_id=1, source_target_pairs={{0,1},{1,0},{2,3},{3,2},{4,5},{5,4},{6,7},{7,6},{8,9},{9,8},{10,11... | collective-permute-start | bytes 27656 | tf_op jit(solution)/shard_map/ppermute | solution.py:265
  27.2 3.2 %collective-permute-start.5 = (f32[19,1,128]{2,1,0:T(1,128)S(1)}, f32[19,1,128]{2,1,0:T(1,128)S(1)}, u32[]{:S(2)}, u32[]{:S(2)}) collective-permute-start(f32[19,1,128]{2,1,0:T(1,128)S(1)} %get-tuple-element.24.refs_0_), channel_id=1, source_target_pairs={{0,3},{1,2},{2,1},{3,0},{4,7},{5,6},{6,5},{7,4},{8,11},{9,10},{10,... | collective-permute-start | bytes 29192 | tf_op jit(solution)/shard_map/ppermute | solution.py:265
  27.2 3.7 %collective-permute-start.4 = (f32[19,1,128]{2,1,0:T(1,128)S(1)}, f32[19,1,128]{2,1,0:T(1,128)S(1)}, u32[]{:S(2)}, u32[]{:S(2)}) collective-permute-start(f32[19,1,128]{2,1,0:T(1,128)S(1)} %get-tuple-element.24.refs_0_), channel_id=1, source_target_pairs={{0,2},{1,3},{2,0},{3,1},{4,6},{5,7},{6,4},{7,5},{8,10},{9,11},{10,... | collective-permute-start | bytes 29192 | tf_op jit(solution)/shard_map/ppermute | solution.py:265
  28.8 2.2 %collective-permute-start.3 = (f32[19,1,128]{2,1,0:T(1,128)S(1)}, f32[19,1,128]{2,1,0:T(1,128)S(1)}, u32[]{:S(2)}, u32[]{:S(2)}) collective-permute-start(f32[19,1,128]{2,1,0:T(1,128)S(1)} %get-tuple-element.24.refs_0_), channel_id=1, source_target_pairs={{0,1},{1,0},{2,3},{3,2},{4,5},{5,4},{6,7},{7,6},{8,9},{9,8},{10,11... | collective-permute-start | bytes 29192 | tf_op jit(solution)/shard_map/ppermute | solution.py:265
